TPU v7x, 512 devices: a whole 4x8x8 slice. The times are simulated.
512 devices in a mesh: chan: 8 (over z), sx: 8 (over x, core), sy: 8 (over y).
Axes of the slice: x: 4, y: 8, z: 8, core: 2. Of those that a mesh axis runs over, the one named last changes fastest.
Arguments:
- volume: bfloat16 [8, 64, 64, 256], P('sx', 'sy', None, 'chan'), may hold values from -6 to 6
- kernel: bfloat16 [27, 256, 256], P(None, 'chan'), may hold values from -0.078125 to 0.078125
- grad_out: bfloat16 [8, 64, 64, 256], P('sx', 'sy', None, 'chan'), may hold values from -6 to 6
Outputs:
- out: bfloat16 [8, 64, 64, 256], P('sx', 'sy', None, 'chan')
- grad_input: bfloat16 [8, 64, 64, 256], P('sx', 'sy', None, 'chan')
- grad_kernel: float32 [27, 256, 256], P(None, 'chan')
All inputs are finite; a program needn't handle non-finite values.
Results may differ from a plain program's by a relative error of at most 0.0015.
Values may be sent and summed in bfloat16 or wider, within the bound.
No kernel may reach another device: no remote copies, remote signals or barrier semaphores. Data moves between devices by JAX's collectives and lax.ppermute only.
A program may use at most 64 MiB of HBM per device.

v0:
```python
import math

import jax
import jax.numpy as jnp
from jax import lax
from jax.sharding import PartitionSpec as P


def padded_2(shard, sides, width):
    for axis, dim in sides:
        count, length = (lax.axis_size(axis), shard.shape[dim])
        up = [(i, (i + 1) % count) for i in range(count - 1)]
        down = [(j, i) for i, j in up]
        last = lax.slice_in_dim(shard, length - width, length, axis=dim)
        leading = lax.slice_in_dim(shard, 0, width, axis=dim)
        before = lax.ppermute(last, axis, up)
        after = lax.ppermute(leading, axis, down)
        shard = jnp.concatenate([before, shard, after], axis=dim)
    return shard


def body(volume, kernel, grad_out):
    size_x, size_y, size_z, own_in = volume.shape
    total_out = kernel.shape[2]
    cells = size_x * size_y * size_z
    rim = padded_2(volume, (("sx", 0), ("sy", 1)), 1)
    padded = jnp.pad(rim, ((0, 0), (0, 0), (1, 1), (0, 0)))
    offsets = [(index // 9, index // 3 % 3, index % 3) for index in range(27)]
    partial_out = jnp.zeros((cells, total_out), jnp.float32)
    for index in range(27):
        a, b, e = offsets[index]
        window = padded[a : a + size_x, b : b + size_y, e : e + size_z].reshape(cells, own_in)
        partial_out = partial_out + jnp.dot(
            window, kernel[index], preferred_element_type=jnp.float32
        )
    partial_out = partial_out.reshape(size_x, size_y, size_z, total_out)
    out = lax.psum_scatter(partial_out, "chan", scatter_dimension=3, tiled=True).astype(
        jnp.bfloat16
    )
    grad_full = lax.all_gather(grad_out, "chan", axis=3, tiled=True)
    grad_rimmed = padded_2(grad_full, (("sx", 0), ("sy", 1)), 1)
    grad_padded = jnp.pad(grad_rimmed, ((0, 0), (0, 0), (1, 1), (0, 0)))
    flat_grad = grad_full.reshape(cells, total_out)
    back = jnp.zeros((cells, own_in), jnp.float32)
    kernel_terms = []
    for index in range(27):
        a, b, e = offsets[index]
        window = grad_padded[
            2 - a : 2 - a + size_x, 2 - b : 2 - b + size_y, 2 - e : 2 - e + size_z
        ].reshape(cells, total_out)
        back = back + lax.dot_general(
            window, kernel[index], (((1,), (1,)), ((), ())), preferred_element_type=jnp.float32
        )
        in_window = padded[a : a + size_x, b : b + size_y, e : e + size_z].reshape(cells, own_in)
        kernel_terms.append(
            lax.dot_general(
                in_window, flat_grad, (((0,), (0,)), ((), ())), preferred_element_type=jnp.float32
            )
        )
    grad_input = back.reshape(size_x, size_y, size_z, own_in).astype(jnp.bfloat16)
    local_kernel = jnp.stack(kernel_terms)
    summed = lax.psum(local_kernel, ("sx", "sy"))
    all_cells = cells * lax.axis_size("sx") * lax.axis_size("sy")
    grad_kernel = summed / jnp.float32(math.sqrt(all_cells))
    return (out, grad_input, grad_kernel)


def solution(mesh):
    return jax.shard_map(
        body,
        mesh=mesh,
        in_specs=(P("sx", "sy", None, "chan"), P(None, "chan", None), P("sx", "sy", None, "chan")),
        out_specs=(P("sx", "sy", None, "chan"), P("sx", "sy", None, "chan"), P(None, "chan", None)),
        check_vma=False,
    )
```

profile of v0, /device:TPU:1, one launch (start us, length us, event | category | flops | bytes accessed | tf_op | source)
XLA Modules:
  0.0 341.4 jit_solution(3898932481704692713)
XLA Ops:
  8.1 4.5 %collective-permute-start = (bf16[1,8,64,32]{2,3,1,0:T(8,128)(2,1)}, bf16[1,8,64,32]{2,3,1,0:T(8,128)(2,1)S(1)}, u32[]{:S(2)}, u32[]{:S(2)}) collective-permute-start(bf16[1,8,64,32]{2,3,1,0:T(8,128)(2,1)} %param.3), channel_id=1, source_target_pairs={{0,8},{8,16},{16,24},{24,32},{32,40},{40,48},{48,56},{1,9},{9,17},... | collective-permute-start | bytes 98312 | tf_op jit(solution)/shard_map/ppermute | solution.py:16
  12.6 5.6 %collective-permute-start.1 = (bf16[1,8,64,32]{2,3,1,0:T(8,128)(2,1)}, bf16[1,8,64,32]{2,3,1,0:T(8,128)(2,1)S(1)}, u32[]{:S(2)}, u32[]{:S(2)}) collective-permute-start(bf16[1,8,64,32]{2,3,1,0:T(8,128)(2,1)} %param.3), channel_id=1, source_target_pairs={{8,0},{16,8},{24,16},{32,24},{40,32},{48,40},{56,48},{9,1},{17,9},... | collective-permute-start | bytes 98312 | tf_op jit(solution)/shard_map/ppermute | solution.py:17
  21.3 4.0 %collective-permute-start.2 = (bf16[3,1,64,32]{2,3,1,0:T(8,128)(2,1)S(1)}, bf16[3,1,64,32]{2,3,1,0:T(8,128)(2,1)S(1)}, u32[]{:S(2)}, u32[]{:S(2)}) collective-permute-start(bf16[3,1,64,32]{2,3,1,0:T(8,128)(2,1)S(1)} %get-tuple-element.68), channel_id=1, source_target_pairs={{0,1},{1,2},{2,3},{3,4},{4,5},{5,6},{6,7},{8,9},{9,10},{10,11},{11... | collective-permute-start | bytes 36872 | tf_op jit(solution)/shard_map/ppermute | solution.py:16
  25.3 24.6 %all_gather.3 = bf16[1,8,64,256]{2,1,0,3:T(8,128)(2,1)S(1)} all-gather(bf16[1,8,64,32]{2,1,0,3:T(8,128)(2,1)S(1)} %copy.98), channel_id=1, replica_groups=mesh['chan'=8,'sx'=8,'sy'=8] {'chan'}, dimensions={3}, use_global_device_ids=true | all-gather | bytes 294912 | tf_op jit(solution)/shard_map/all_gather | solution.py:40
  50.2 5.5 %collective-permute-start.5 = (bf16[1,8,64,256]{3,2,1,0:T(8,128)(2,1)S(1)}, bf16[1,8,64,256]{3,2,1,0:T(8,128)(2,1)S(1)}, u32[]{:S(2)}, u32[]{:S(2)}) collective-permute-start(bf16[1,8,64,256]{3,2,1,0:T(8,128)(2,1)S(1)} %copy.99), channel_id=1, source_target_pairs={{8,0},{16,8},{24,16},{32,24},{40,32},{48,40},{56,48},{9,1},{17,9},... | collective-permute-start | bytes 786440 | tf_op jit(solution)/shard_map/ppermute | solution.py:17
  55.7 4.7 %collective-permute-start.4 = (bf16[1,8,64,256]{3,2,1,0:T(8,128)(2,1)S(1)}, bf16[1,8,64,256]{3,2,1,0:T(8,128)(2,1)S(1)}, u32[]{:S(2)}, u32[]{:S(2)}) collective-permute-start(bf16[1,8,64,256]{3,2,1,0:T(8,128)(2,1)S(1)} %copy.99), channel_id=1, source_target_pairs={{0,8},{8,16},{16,24},{24,32},{32,40},{40,48},{48,56},{1,9},{9,17},... | collective-permute-start | bytes 786440 | tf_op jit(solution)/shard_map/ppermute | solution.py:16
  74.1 1.6 reshape.329
  75.7 1.5 copy.77
  77.2 1.6 reshape.330
  78.8 1.5 copy.78
  80.3 1.6 reshape.331
  81.8 1.5 copy.79
  83.3 1.6 reshape.332
  85.5 1.6 reshape.333
  87.7 1.6 reshape.334
  89.9 1.6 reshape.335
  91.5 1.5 copy.84
  93.0 1.6 reshape.337
  96.1 1.6 reshape.338
  98.3 1.6 reshape.339
  100.5 1.6 reshape.340
  102.0 1.5 copy.88
  103.5 1.6 reshape.341
  105.8 1.6 reshape.342
  107.3 1.5 copy.90
  108.8 1.6 reshape.343
  111.8 1.6 reshape.344
  114.1 1.6 reshape.347
  147.7 4.2 %collective-permute-start.6 = (bf16[3,1,64,256]{3,2,1,0:T(8,128)(2,1)S(1)}, bf16[3,1,64,256]{3,2,1,0:T(8,128)(2,1)S(1)}, u32[]{:S(2)}, u32[]{:S(2)}) collective-permute-start(bf16[3,1,64,256]{3,2,1,0:T(8,128)(2,1)S(1)} %get-tuple-element.39), channel_id=1, source_target_pairs={{0,1},{1,2},{2,3},{3,4},{4,5},{5,6},{6,7},{8,9},{9,10},{10,11},{11... | collective-permute-start | bytes 294920 | tf_op jit(solution)/shard_map/ppermute | solution.py:16
  161.2 168.9 %all-reduce.4.cloned.1.call-done = f32[27,32,256]{2,1,0:T(8,128)} async-done(((f32[27,32,256]{2,1,0:T(8,128)}), f32[27,32,256]{2,1,0:T(8,128)}) %all-reduce.4.cloned.1.call-update) | async-done | bytes 884752 | tf_op jit(solution)/shard_map/psum | solution.py:62
  330.2 2.2 broadcast_multiply_fusion
  332.4 1.5 convert_element_type.21
  (221 shorter events, 65.5 us)
Async XLA Ops:
  8.0 52.4 %copy-start.4 = (bf16[1,8,64,32]{2,3,1,0:T(8,128)(2,1)S(1)}, bf16[1,8,64,32]{2,3,1,0:T(8,128)(2,1)}, u32[]{:S(2)}) copy-start(bf16[1,8,64,32]{2,3,1,0:T(8,128)(2,1)} %param.3) | copy-start | bytes 98308
  8.0 322.2 %all-reduce.4.cloned.1.call-start = ((), (), s32[]{:S(2)}) async-start(), calls=%async_computation.2 | async-start | bytes 1769472 | tf_op jit(solution)/shard_map/psum | solution.py:62
  8.1 11.0 %collective-permute-start = (bf16[1,8,64,32]{2,3,1,0:T(8,128)(2,1)}, bf16[1,8,64,32]{2,3,1,0:T(8,128)(2,1)S(1)}, u32[]{:S(2)}, u32[]{:S(2)}) collective-permute-start(bf16[1,8,64,32]{2,3,1,0:T(8,128)(2,1)} %param.3), channel_id=1, source_target_pairs={{0,8},{8,16},{16,24},{24,32},{32,40},{40,48},{48,56},{1,9},{9,17},... | collective-permute-start | bytes 98312 | tf_op jit(solution)/shard_map/ppermute | solution.py:16
  12.6 7.4 %collective-permute-start.1 = (bf16[1,8,64,32]{2,3,1,0:T(8,128)(2,1)}, bf16[1,8,64,32]{2,3,1,0:T(8,128)(2,1)S(1)}, u32[]{:S(2)}, u32[]{:S(2)}) collective-permute-start(bf16[1,8,64,32]{2,3,1,0:T(8,128)(2,1)} %param.3), channel_id=1, source_target_pairs={{8,0},{16,8},{24,16},{32,24},{40,32},{48,40},{56,48},{9,1},{17,9},... | collective-permute-start | bytes 98312 | tf_op jit(solution)/shard_map/ppermute | solution.py:17
  19.0 42.2 %copy-start.8 = (bf16[1,8,64,32]{2,3,1,0:T(8,128)(2,1)}, bf16[1,8,64,32]{2,3,1,0:T(8,128)(2,1)S(1)}, u32[]{:S(2)}) copy-start(bf16[1,8,64,32]{2,3,1,0:T(8,128)(2,1)S(1)} %collective-permute-done) | copy-start | bytes 98308
  19.9 42.2 %copy-start.6 = (bf16[1,8,64,32]{2,3,1,0:T(8,128)(2,1)}, bf16[1,8,64,32]{2,3,1,0:T(8,128)(2,1)S(1)}, u32[]{:S(2)}) copy-start(bf16[1,8,64,32]{2,3,1,0:T(8,128)(2,1)S(1)} %collective-permute-done.1) | copy-start | bytes 98308
  20.0 42.1 %collective-permute-start.3 = (bf16[3,1,64,32]{2,3,1,0:T(8,128)(2,1)S(1)}, bf16[3,1,64,32]{2,3,1,0:T(8,128)(2,1)S(1)}, u32[]{:S(2)}, u32[]{:S(2)}) collective-permute-start(bf16[3,1,64,32]{2,3,1,0:T(8,128)(2,1)S(1)} %get-tuple-element.69), channel_id=1, source_target_pairs={{1,0},{2,1},{3,2},{4,3},{5,4},{6,5},{7,6},{9,8},{10,9},{11,10},{12... | collective-permute-start | bytes 36872 | tf_op jit(solution)/shard_map/ppermute | solution.py:17
  21.3 40.9 %collective-permute-start.2 = (bf16[3,1,64,32]{2,3,1,0:T(8,128)(2,1)S(1)}, bf16[3,1,64,32]{2,3,1,0:T(8,128)(2,1)S(1)}, u32[]{:S(2)}, u32[]{:S(2)}) collective-permute-start(bf16[3,1,64,32]{2,3,1,0:T(8,128)(2,1)S(1)} %get-tuple-element.68), channel_id=1, source_target_pairs={{0,1},{1,2},{2,3},{3,4},{4,5},{5,6},{6,7},{8,9},{9,10},{10,11},{11... | collective-permute-start | bytes 36872 | tf_op jit(solution)/shard_map/ppermute | solution.py:16
  50.2 96.1 %collective-permute-start.5 = (bf16[1,8,64,256]{3,2,1,0:T(8,128)(2,1)S(1)}, bf16[1,8,64,256]{3,2,1,0:T(8,128)(2,1)S(1)}, u32[]{:S(2)}, u32[]{:S(2)}) collective-permute-start(bf16[1,8,64,256]{3,2,1,0:T(8,128)(2,1)S(1)} %copy.99), channel_id=1, source_target_pairs={{8,0},{16,8},{24,16},{32,24},{40,32},{48,40},{56,48},{9,1},{17,9},... | collective-permute-start | bytes 786440 | tf_op jit(solution)/shard_map/ppermute | solution.py:17
  55.7 90.7 %collective-permute-start.4 = (bf16[1,8,64,256]{3,2,1,0:T(8,128)(2,1)S(1)}, bf16[1,8,64,256]{3,2,1,0:T(8,128)(2,1)S(1)}, u32[]{:S(2)}, u32[]{:S(2)}) collective-permute-start(bf16[1,8,64,256]{3,2,1,0:T(8,128)(2,1)S(1)} %copy.99), channel_id=1, source_target_pairs={{0,8},{8,16},{16,24},{24,32},{32,40},{40,48},{48,56},{1,9},{9,17},... | collective-permute-start | bytes 786440 | tf_op jit(solution)/shard_map/ppermute | solution.py:16
  63.5 2.3 copy-start
  68.1 18.9 %copy-start.14 = (bf16[1,8,64,32]{2,3,1,0:T(8,128)(2,1)S(1)}, bf16[1,8,64,32]{2,3,1,0:T(8,128)(2,1)}, u32[]{:S(2)}) copy-start(bf16[1,8,64,32]{2,3,1,0:T(8,128)(2,1)} %get-tuple-element.51) | copy-start | bytes 98308
  68.1 21.2 %copy-start.13 = (bf16[1,8,64,32]{2,3,1,0:T(8,128)(2,1)S(1)}, bf16[1,8,64,32]{2,3,1,0:T(8,128)(2,1)}, u32[]{:S(2)}) copy-start(bf16[1,8,64,32]{2,3,1,0:T(8,128)(2,1)} %get-tuple-element.50) | copy-start | bytes 98308
  74.1 25.7 %copy-start.12 = (bf16[1,8,64,32]{2,3,1,0:T(8,128)(2,1)S(1)}, bf16[1,8,64,32]{2,3,1,0:T(8,128)(2,1)}, u32[]{:S(2)}) copy-start(bf16[1,8,64,32]{2,3,1,0:T(8,128)(2,1)} %get-tuple-element.47) | copy-start | bytes 98308
  87.7 25.7 %copy-start.11 = (bf16[1,8,64,32]{2,3,1,0:T(8,128)(2,1)S(1)}, bf16[1,8,64,32]{2,3,1,0:T(8,128)(2,1)}, u32[]{:S(2)}) copy-start(bf16[1,8,64,32]{2,3,1,0:T(8,128)(2,1)} %get-tuple-element.42) | copy-start | bytes 98308
  89.9 25.7 %copy-start.3 = (bf16[1,8,64,32]{2,3,1,0:T(8,128)(2,1)S(1)}, bf16[1,8,64,32]{2,3,1,0:T(8,128)(2,1)}, u32[]{:S(2)}) copy-start(bf16[1,8,64,32]{2,3,1,0:T(8,128)(2,1)} %copy-done.2) | copy-start | bytes 98308
  102.0 16.1 %copy-start.9 = (bf16[1,8,64,32]{2,3,1,0:T(8,128)(2,1)S(1)}, bf16[1,8,64,32]{2,3,1,0:T(8,128)(2,1)}, u32[]{:S(2)}) copy-start(bf16[1,8,64,32]{2,3,1,0:T(8,128)(2,1)} %copy-done.8) | copy-start | bytes 98308
  115.6 5.0 %copy-start.1 = (bf16[1,8,64,32]{2,3,1,0:T(8,128)(2,1)S(1)}, bf16[1,8,64,32]{2,3,1,0:T(8,128)(2,1)}, u32[]{:S(2)}) copy-start(bf16[1,8,64,32]{2,3,1,0:T(8,128)(2,1)} %get-tuple-element.60) | copy-start | bytes 98308
  120.7 5.0 %copy-start.5 = (bf16[1,8,64,32]{2,3,1,0:T(8,128)(2,1)S(1)}, bf16[1,8,64,32]{2,3,1,0:T(8,128)(2,1)}, u32[]{:S(2)}) copy-start(bf16[1,8,64,32]{2,3,1,0:T(8,128)(2,1)} %param.3) | copy-start | bytes 98308
  128.2 5.0 %copy-start.7 = (bf16[1,8,64,32]{2,3,1,0:T(8,128)(2,1)S(1)}, bf16[1,8,64,32]{2,3,1,0:T(8,128)(2,1)}, u32[]{:S(2)}) copy-start(bf16[1,8,64,32]{2,3,1,0:T(8,128)(2,1)} %copy-done.6) | copy-start | bytes 98308
  134.0 3.5 %copy-start.17 = (bf16[512,32]{0,1:T(8,128)(2,1)S(1)}, bf16[512,32]{0,1:T(8,128)(2,1)}, u32[]{:S(2)}) copy-start(bf16[512,32]{0,1:T(8,128)(2,1)} %reshape.324) | copy-start | bytes 98308
  136.5 1.2 copy-start.21
  137.4 194.9 %reduce-scatter.2.cloned.1.call-start = ((), (), s32[]{:S(2)}) async-start(), calls=%async_computation.1 | async-start | bytes 1179648 | tf_op jit(solution)/shard_map/reduce_scatter | solution.py:37
  137.8 0.8 copy-start.16
  138.2 0.8 copy-start.18
  138.5 0.8 copy-start.19
  139.0 0.8 copy-start.20
  139.3 0.8 copy-start.22
  139.7 0.8 copy-start.23
  145.4 0.8 copy-start.10
  146.4 7.1 %collective-permute-start.7 = (bf16[3,1,64,256]{3,2,1,0:T(8,128)(2,1)S(1)}, bf16[3,1,64,256]{3,2,1,0:T(8,128)(2,1)S(1)}, u32[]{:S(2)}, u32[]{:S(2)}) collective-permute-start(bf16[3,1,64,256]{3,2,1,0:T(8,128)(2,1)S(1)} %get-tuple-element.40), channel_id=1, source_target_pairs={{1,0},{2,1},{3,2},{4,3},{5,4},{6,5},{7,6},{9,8},{10,9},{11,10},{12... | collective-permute-start | bytes 294920 | tf_op jit(solution)/shard_map/ppermute | solution.py:17
  147.7 5.8 %collective-permute-start.6 = (bf16[3,1,64,256]{3,2,1,0:T(8,128)(2,1)S(1)}, bf16[3,1,64,256]{3,2,1,0:T(8,128)(2,1)S(1)}, u32[]{:S(2)}, u32[]{:S(2)}) collective-permute-start(bf16[3,1,64,256]{3,2,1,0:T(8,128)(2,1)S(1)} %get-tuple-element.39), channel_id=1, source_target_pairs={{0,1},{1,2},{2,3},{3,4},{4,5},{5,6},{6,7},{8,9},{9,10},{10,11},{11... | collective-permute-start | bytes 294920 | tf_op jit(solution)/shard_map/ppermute | solution.py:16
  (16 other events, 11.7 us)
Sparse Core Ops, SparseCore 0:
  137.6 192.5 all-reduce.3
Sparse Core Ops, SparseCore 1:
  153.6 35.7 reduce-scatter.1
where the time goes:
time: 345 us; the launch traced here: 341 us
  waiting for transfers between devices  169 us (49%)
  local copies, waits for them, and re-layouts  60 us (17%)
  matrix products  34.2 us (10%)
  starting transfers between devices  31.1 us (9%)
  blocking collectives  24.6 us (7%)
  between operations  16.2 us (5%)
  other arithmetic  6.23 us (2%)
    psum x1, waiting for transfers between devices, body(): summed = lax.psum(local_kernel, ('sx', 'sy'))  169 us
    reshape x27, local copies, waits for them, and re-layouts, body(): padded[a:a + size_x, b:b + size_y, e:e + size_z].reshape(cells, own_in)  29.3 us
    all_gather x1, blocking collectives, body(): grad_full = lax.all_gather(grad_out, 'chan', axis=3, tiled=True)  24.6 us
    dot_general x27, matrix products, body(): lax.dot_general(in_window, flat_grad, (((0,), (0,)), ((), ())), preferred...  22.6 us
    slice x25, local copies, waits for them, and re-layouts, body(): padded[a:a + size_x, b:b + size_y, e:e + size_z].reshape(cells, own_in)  21 us
    ppermute x4, starting transfers between devices, padded_2(): before = lax.ppermute(last, axis, up)  17.4 us
    ppermute x4, starting transfers between devices, padded_2(): after = lax.ppermute(leading, axis, down)  13.6 us
    unnamed x81, local copies, waits for them, and re-layouts  6.98 us
  transfers between devices with their start and end apart: 10, of which 1 were waited for; matrix products, arithmetic and copies ran while one was open for 28% of the time, Pallas kernels for 0%

commit v1 on v0

v1 whole, which is shorter than its diff:
```python
import math

import jax
import jax.numpy as jnp
from jax import lax
from jax.experimental import pallas as pl
from jax.experimental.pallas import tpu as pltpu
from jax.sharding import Mesh
from jax.sharding import PartitionSpec as P

F32 = jnp.float32
BF16 = jnp.bfloat16
PLANE = ("x", "core")
PARAMS = pltpu.CompilerParams(vmem_limit_bytes=16 * 2**20)


def call(kernel, outs, flops, *args):
    moved = sum(a.size * a.dtype.itemsize for a in args)
    moved += sum(math.prod(s) * jnp.dtype(d).itemsize for s, d in outs)
    specs = [
        pl.BlockSpec(memory_space=pltpu.SMEM if a.dtype == jnp.int32 else pltpu.VMEM) for a in args
    ]
    return pl.pallas_call(
        kernel,
        out_shape=[jax.ShapeDtypeStruct(s, d) for s, d in outs],
        in_specs=specs,
        out_specs=[pl.BlockSpec(memory_space=pltpu.VMEM) for _ in outs],
        compiler_params=PARAMS,
        cost_estimate=pl.CostEstimate(flops=flops, bytes_accessed=moved, transcendentals=0),
    )(*args)


def edge_rows(v, g, first, last):
    c, rows = v.shape[1], v.shape[0]
    first[:c] = v[0]
    first[c:] = g[0]
    last[:c] = v[rows - 1]
    last[c:] = g[rows - 1]


def ring_rows(v, g, before, after, v_ring, g_copies):
    rows, c, z = v.shape
    for own, lo, out in ((v, 0, v_ring), (g, c, None)):
        parts = [own[r] for r in range(rows)]
        parts += [after[lo : lo + c], before[lo : lo + c]]
        ring = jnp.concatenate([part.astype(F32) for part in parts], axis=1).astype(BF16)
        if out is None:
            for copy in range(g_copies.shape[0]):
                g_copies[copy] = ring
        else:
            out[...] = ring


def in_line(shape, z, shift):
    at = lax.broadcasted_iota(jnp.int32, shape, 1) % z + shift
    return (at >= 0) & (at < z)


def forward_and_weights(z, core, below, own, above, g, k, keep, send, partial, columns):
    c = own.shape[0]
    lanes = own.shape[1]
    cells = lanes - 2 * z
    planes = jnp.concatenate([below[...], own[...], above[...]], axis=0).astype(F32)
    for e in range(3):
        moved = planes if e == 1 else pltpu.roll(planes, (1 - e) % lanes, 1)
        if e != 1:
            moved = jnp.where(in_line(moved.shape, z, e - 1), moved, 0.0)
        for b in range(3):
            window = moved if b == 1 else pltpu.roll(moved, (z * (1 - b)) % lanes, 1)
            window = window[:, :cells].astype(BF16)
            for a in range(3):
                at = (9 * a + 3 * b + e) * c
                columns[at : at + c, :] = window[a * c : (a + 1) * c]
    groups, total = g.shape[0], g.shape[0] * g.shape[1]
    g_own = g[...].reshape(total, lanes)[:, :cells]
    terms = lax.dot_general(
        columns[...], g_own, (((1,), (1,)), ((), ())), preferred_element_type=F32
    )
    half = total // 2
    low, high = terms[:, :half], terms[:, half:]
    first = core[0] == 0
    kept = jnp.where(first, low, high)
    sent = jnp.where(first, high, low)
    pieces, rows = keep.shape[0], keep.shape[1]
    for piece in range(pieces):
        keep[piece] = kept[piece * rows : (piece + 1) * rows]
        send[piece] = sent[piece * rows : (piece + 1) * rows]
    out = lax.dot_general(k[...], columns[...], (((0,), (0,)), ((), ())), preferred_element_type=F32)
    partial[...] = out.reshape(groups, total // groups, cells)


def input_gradient(z, below, own, above, k, out):
    rows, c = out.shape[0], out.shape[1]
    total = own.shape[0] * own.shape[1]
    lanes = own.shape[2]
    taps = k.shape[0] // 3
    terms = jnp.zeros((taps, lanes), F32)
    for a, plane in enumerate((above, own, below)):
        terms += jnp.dot(
            k[a * taps : (a + 1) * taps, :],
            plane[...].reshape(total, lanes),
            preferred_element_type=F32,
        )
    result = jnp.zeros((c, lanes), F32)
    for e in range(3):
        line = jnp.zeros((c, lanes), F32)
        for b in range(3):
            at = (3 * b + e) * c
            term = terms[at : at + c]
            line += term if b == 1 else pltpu.roll(term, (z * (b - 1)) % lanes, 1)
        if e != 1:
            line = pltpu.roll(line, (e - 1) % lanes, 1)
            line = jnp.where(in_line(line.shape, z, 1 - e), line, 0.0)
        result += line
    split_rows(result, out)


def split_rows(value, out):
    rows, z = out.shape[0], out.shape[2]
    lanes = value.shape[1]
    for r in range(rows):
        shifted = value if r == 0 else pltpu.roll(value, lanes - r * z, 1)
        out[r] = shifted[:, :z].astype(BF16)


def sum_outputs(partial, out):
    total = partial[0]
    for part in range(1, partial.shape[0]):
        total += partial[part]
    split_rows(total, out)


def add_halves(keep, other, out):
    out[...] = keep[...] + other[...]


def sum_pieces(scale, parts, out):
    total = parts[0]
    for part in range(1, parts.shape[0]):
        total += parts[part]
    total = total / scale
    for copy in range(out.shape[0]):
        out[copy] = total


def join_halves(core, mine, other, out):
    pieces, rows, half = mine.shape
    first = core[0] == 0
    for piece in range(pieces):
        a, b = mine[piece], other[piece]
        out[piece * rows : (piece + 1) * rows, :half] = jnp.where(first, a, b)
        out[piece * rows : (piece + 1) * rows, half:] = jnp.where(first, b, a)


def neighbours(value_up, value_down, axis):
    n = lax.axis_size(axis)
    up = [(i, i + 1) for i in range(n - 1)]
    down = [(i + 1, i) for i in range(n - 1)]
    return lax.ppermute(value_up, axis, up), lax.ppermute(value_down, axis, down)


def exchange(value, axis):
    return lax.all_to_all(value, axis, 0, 0, tiled=True)


def body(volume, kernel, grad_out):
    _, rows, z, c = volume.shape
    taps, _, total = kernel.shape
    cells, lanes = rows * z, (rows + 2) * z
    groups = lax.axis_size("chan")
    pieces = lax.axis_size("x") * lax.axis_size("sy")
    devices = pieces * lax.axis_size("core")
    v = volume[0].transpose(0, 2, 1)
    g = grad_out[0].transpose(0, 2, 1)
    k = kernel.reshape(taps * c, total)
    core = lax.axis_index("core").reshape(1)
    work = 2 * taps * c * total * cells

    first, last = call(edge_rows, [((2 * c, z), BF16)] * 2, 0, v, g)
    before, after = neighbours(last, first, "sy")
    v_ring, g_copies = call(
        ring_rows,
        [((c, lanes), BF16), ((groups, c, lanes), BF16)],
        0,
        v,
        g,
        before,
        after,
    )
    g_ring = exchange(g_copies, "chan")
    v_below, v_above = neighbours(v_ring, v_ring, PLANE)

    piece = (pieces, taps * c // pieces, total // 2)

    def weights(*refs):
        forward_and_weights(z, *refs)

    operands = (core, v_below, v_ring, v_above, g_ring, k)
    moved = sum(a.size * a.dtype.itemsize for a in operands) + 3 * math.prod(piece) * 4
    keep, send, partial = pl.pallas_call(
        weights,
        out_shape=[
            jax.ShapeDtypeStruct(piece, F32),
            jax.ShapeDtypeStruct(piece, F32),
            jax.ShapeDtypeStruct((groups, total // groups, cells), F32),
        ],
        in_specs=[pl.BlockSpec(memory_space=pltpu.SMEM)]
        + [pl.BlockSpec(memory_space=pltpu.VMEM)] * 5,
        out_specs=[pl.BlockSpec(memory_space=pltpu.VMEM)] * 3,
        scratch_shapes=[pltpu.VMEM((taps * c, cells), BF16)],
        compiler_params=PARAMS,
        cost_estimate=pl.CostEstimate(flops=2 * work, bytes_accessed=moved, transcendentals=0),
    )(*operands)

    swap = [(0, 1), (1, 0)]
    (halves,) = call(add_halves, [(piece, F32)], 0, keep, lax.ppermute(send, "core", swap))
    parts = exchange(halves, ("x", "sy"))
    scale = math.sqrt(cells * devices)

    def reduce_pieces(*refs):
        sum_pieces(scale, *refs)

    (copies,) = call(reduce_pieces, [(piece, F32)], 0, parts)
    mine = exchange(copies, ("x", "sy"))
    other = lax.ppermute(mine, "core", swap)
    (grad_kernel,) = call(join_halves, [((taps * c, total), F32)], 0, core, mine, other)

    (out,) = call(sum_outputs, [((rows, c, z), BF16)], 0, exchange(partial, "chan"))

    g_below, g_above = neighbours(g_ring, g_ring, PLANE)

    def inputs(*refs):
        input_gradient(z, *refs)

    (grad_input,) = call(inputs, [((rows, c, z), BF16)], work, g_below, g_ring, g_above, k)
    return (
        out.transpose(0, 2, 1)[None],
        grad_input.transpose(0, 2, 1)[None],
        grad_kernel.reshape(taps, c, total),
    )


def solution(mesh):
    cores = 2
    shape = (mesh.shape["chan"], mesh.shape["sx"] // cores, cores, mesh.shape["sy"])
    split = Mesh(mesh.devices.reshape(shape), ("chan", "x", "core", "sy"))
    cells = P(PLANE, "sy", None, "chan")
    weights = P(None, "chan", None)
    return jax.shard_map(
        body,
        mesh=split,
        in_specs=(cells, weights, cells),
        out_specs=(cells, cells, weights),
        check_vma=False,
    )
```

time: 345 us -> 112 us (0.32)
  waiting for transfers between devices: 169 us -> 11.3 us
  local copies, waits for them, and re-layouts: 60 us -> 1.68 us
  matrix products: 34.2 us -> 0 us
  blocking collectives: 24.6 us -> 45.8 us
  between operations: 16.2 us -> 0.75 us
  starting transfers between devices: 31.1 us -> 43.9 us
  other arithmetic: 6.23 us -> 0 us
  Pallas kernels: 0 us -> 5.92 us
    psum x1 -> x0, waiting for transfers between devices: 169 us -> none  [body(): summed = lax.psum(local_kernel, ('sx', 'sy'))]
    all_to_all x0 -> x2, blocking collectives: none -> 45.8 us  [exchange(): return lax.all_to_all(value, axis, 0, 0, tiled=True)]
    dot_general x81 -> x0, matrix products: 34.2 us -> none  [the longest x27 22.6 us: body(): lax.dot_general(in_window, flat_grad, (((0,), (0,)), ((), ())), preferred...]
    reshape x28 -> x0, local copies, waits for them, and re-layouts: 30.6 us -> none  [the longest x27 29.3 us: body(): padded[a:a + size_x, b:b + size_y, e:e + size_z].reshape(cells, own_in)]
    all_gather x1 -> x0, blocking collectives: 24.6 us -> none  [body(): grad_full = lax.all_gather(grad_out, 'chan', axis=3, tiled=True)]
    slice x27 -> x0, local copies, waits for them, and re-layouts: 21.9 us -> none  [the longest x25 21 us: body(): padded[a:a + size_x, b:b + size_y, e:e + size_z].reshape(cells, own_in)]
    all_to_all x0 -> x2, starting transfers between devices: none -> 13.5 us  [exchange(): return lax.all_to_all(value, axis, 0, 0, tiled=True)]
    ppermute x8, waiting for transfers between devices: 0.02 us -> 9.76 us  [the longest x3 6.02 us: neighbours(): lax.ppermute(value_down, axis, down)]
  transfers between devices with their start and end apart: 10 -> 10, of which waited for: 1 -> 6; matrix products, arithmetic and copies ran while one was open for 28% -> 0% of each run, Pallas kernels for 0% -> 2%
where the time goes in v1:
time: 112 us; the launch traced here: 109 us
  blocking collectives  45.8 us (41%)
  starting transfers between devices  43.9 us (39%)
  waiting for transfers between devices  11.3 us (10%)
  Pallas kernels  5.92 us (5%)
  local copies, waits for them, and re-layouts  1.68 us (2%)
    all_to_all x2, blocking collectives, exchange(): return lax.all_to_all(value, axis, 0, 0, tiled=True)  45.8 us
    all_to_all x2, starting transfers between devices, exchange(): return lax.all_to_all(value, axis, 0, 0, tiled=True)  13.5 us
    ppermute x3, starting transfers between devices, neighbours(): lax.ppermute(value_up, axis, up)  10.8 us
    ppermute x3, starting transfers between devices, neighbours(): lax.ppermute(value_down, axis, down)  7.49 us
    ppermute x1, starting transfers between devices, body(): lax.ppermute(send, 'core', swap)  6.17 us
    ppermute x3, waiting for transfers between devices, neighbours(): lax.ppermute(value_down, axis, down)  6.02 us
    ppermute x1, starting transfers between devices, body(): other = lax.ppermute(mine, 'core', swap)  5.94 us
    pallas_call x7, Pallas kernels, call(): pl.pallas_call(kernel, out_shape=[jax.ShapeDtypeStruct(s, d) for s, d in...  4.12 us
  transfers between devices with their start and end apart: 10, of which 6 were waited for; matrix products, arithmetic and copies ran while one was open for 0% of the time, Pallas kernels for 2%

profile of v1, /device:TPU:1, one launch (start us, length us, event | category | flops | bytes accessed | tf_op | source)
XLA Modules:
  0.0 109.4 jit_solution(7086580742269889617)
XLA Ops:
  0.6 0.8 copy-done.1
  1.5 0.8 copy-done.2
  2.3 4.2 %collective-permute-start = (bf16[64,64]{1,0:T(8,128)(2,1)S(1)}, bf16[64,64]{1,0:T(8,128)(2,1)S(1)}, u32[]{:S(2)}, u32[]{:S(2)}) collective-permute-start(bf16[64,64]{1,0:T(8,128)(2,1)S(1)} %get-tuple-element.10), channel_id=1, source_target_pairs={{0,1},{1,2},{2,3},{3,4},{4,5},{5,6},{6,7},{8,9},{9,10},{10,11},{11... | collective-permute-start | bytes 24584 | tf_op jit(solution)/shard_map/ppermute | solution.py:159
  6.5 1.3 %collective-permute-start.1 = (bf16[64,64]{1,0:T(8,128)(2,1)S(1)}, bf16[64,64]{1,0:T(8,128)(2,1)S(1)}, u32[]{:S(2)}, u32[]{:S(2)}) collective-permute-start(bf16[64,64]{1,0:T(8,128)(2,1)S(1)} %get-tuple-element.11), channel_id=1, source_target_pairs={{1,0},{2,1},{3,2},{4,3},{5,4},{6,5},{7,6},{9,8},{10,9},{11,10},{12... | collective-permute-start | bytes 24584 | tf_op jit(solution)/shard_map/ppermute | solution.py:159
  7.8 0.0 collective-permute-done.before
  7.8 3.2 %collective-permute-done.1.after = bf16[64,64]{1,0:T(8,128)(2,1)S(1)} collective-permute-done((bf16[64,64]{1,0:T(8,128)(2,1)S(1)}, bf16[64,64]{1,0:T(8,128)(2,1)S(1)}, u32[]{:S(2)}, u32[]{:S(2)}) %collective-permute-start.1) | collective-permute-done | bytes 8224 | tf_op jit(solution)/shard_map/ppermute | solution.py:159
  11.0 0.8 shard_map.59
  11.8 10.0 %all-to-all-start = ((bf16[8,32,640]{2,1,0:T(8,128)(2,1)}), bf16[8,32,640]{2,1,0:T(8,128)(2,1)S(1)}, u32[]{:S(2)}, u32[]{:S(2)}) async-start(bf16[8,32,640]{2,1,0:T(8,128)(2,1)} %get-tuple-element.13), calls=%async_computation | async-start | bytes 655360 | tf_op jit(solution)/shard_map/all_to_all | solution.py:163
  21.8 4.3 %collective-permute-start.3 = (bf16[32,640]{1,0:T(8,128)(2,1)S(1)}, bf16[32,640]{1,0:T(8,128)(2,1)S(1)}, u32[]{:S(2)}, u32[]{:S(2)}) collective-permute-start(bf16[32,640]{1,0:T(8,128)(2,1)S(1)} %get-tuple-element.12.refs_2_), channel_id=1, source_target_pairs={{8,0},{16,8},{24,16},{32,24},{40,32},{48,40},{56,48},{9,1},{17,9},... | collective-permute-start | bytes 122888 | tf_op jit(solution)/shard_map/ppermute | solution.py:159
  26.1 3.0 %collective-permute-start.2 = (bf16[32,640]{1,0:T(8,128)(2,1)S(1)}, bf16[32,640]{1,0:T(8,128)(2,1)S(1)}, u32[]{:S(2)}, u32[]{:S(2)}) collective-permute-start(bf16[32,640]{1,0:T(8,128)(2,1)S(1)} %get-tuple-element.12.refs_2_), channel_id=1, source_target_pairs={{0,8},{8,16},{16,24},{24,32},{32,40},{40,48},{48,56},{1,9},{9,17},... | collective-permute-start | bytes 122888 | tf_op jit(solution)/shard_map/ppermute | solution.py:159
  29.2 0.0 collective-permute-done.3.refs_3_
  29.2 1.0 collective-permute-done.2.refs_1_
  30.2 1.6 %all-to-all-done.refs_4_.refs_1_ = bf16[8,32,640]{2,1,0:T(8,128)(2,1)S(1)} async-done(((bf16[8,32,640]{2,1,0:T(8,128)(2,1)}), bf16[8,32,640]{2,1,0:T(8,128)(2,1)S(1)}, u32[]{:S(2)}, u32[]{:S(2)}) %all-to-all-start) | async-done | bytes 327712 | tf_op jit(solution)/shard_map/all_to_all | solution.py:163
  31.8 0.0 copy-done
  31.8 1.8 %shard_map.60 = (f32[32,27,128]{2,1,0:T(8,128)S(1)}, f32[32,27,128]{2,1,0:T(8,128)S(1)}, f32[8,32,512]{2,1,0:T(8,128)}) custom-call(s32[1]{0:T(128)} %bitcast.refs_0_.core, bf16[32,640]{1,0:T(8,128)(2,1)S(1)} %collective-permute-done.2.refs_1_, bf16[32,640]{1,0:T(8,128)(2,1)S(1)} %get-tuple-element.12.refs_2_, ...), custom_call_target="tpu_custom_call" | custom-call | flops 452984832 | bytes 2220036 | tf_op jit(solution)/shard_map/pallas_call | solution.py:200
  33.6 6.2 %collective-permute-start.6 = (f32[32,27,128]{2,1,0:T(8,128)S(1)}, f32[32,27,128]{2,1,0:T(8,128)S(1)}, u32[]{:S(2)}, u32[]{:S(2)}) collective-permute-start(f32[32,27,128]{2,1,0:T(8,128)S(1)} %get-tuple-element.16), channel_id=1, source_target_pairs={{0,8},{8,0},{1,9},{9,1},{2,10},{10,2},{3,11},{11,3},{4,12},{12,4},... | collective-permute-start | bytes 1327112 | tf_op jit(solution)/shard_map/ppermute | solution.py:216
  39.8 1.5 %collective-permute-done.6.other = f32[32,27,128]{2,1,0:T(8,128)S(1)} collective-permute-done((f32[32,27,128]{2,1,0:T(8,128)S(1)}, f32[32,27,128]{2,1,0:T(8,128)S(1)}, u32[]{:S(2)}, u32[]{:S(2)}) %collective-permute-start.6) | collective-permute-done | bytes 442400 | tf_op jit(solution)/shard_map/ppermute | solution.py:216
  41.3 0.1 shard_map.63
  41.4 23.8 %all_to_all.20.refs_0_ = f32[32,27,128]{2,1,0:T(8,128)S(1)} all-to-all(f32[32,27,128]{2,1,0:T(8,128)S(1)} %shard_map.63), channel_id=1, replica_groups=mesh['chan'=8,'x'=4,'core'=2,'sy'=8] {'x','sy'}, dimensions={0} | all-to-all | bytes 884736 | tf_op jit(solution)/shard_map/all_to_all | solution.py:163
  65.2 0.1 shard_map.64
  65.3 22.0 %all_to_all.21.mine = f32[32,27,128]{2,1,0:T(8,128)S(1)} all-to-all(f32[32,27,128]{2,1,0:T(8,128)S(1)} %shard_map.64), channel_id=1, replica_groups=mesh['chan'=8,'x'=4,'core'=2,'sy'=8] {'x','sy'}, dimensions={0} | all-to-all | bytes 884736 | tf_op jit(solution)/shard_map/all_to_all | solution.py:163
  87.3 3.5 %all-to-all-start.1 = ((f32[8,32,512]{2,1,0:T(8,128)}), f32[8,32,512]{2,1,0:T(8,128)S(1)}, u32[]{:S(2)}, u32[]{:S(2)}) async-start(f32[8,32,512]{2,1,0:T(8,128)} %get-tuple-element.14), calls=%async_computation.1 | async-start | bytes 1048576 | tf_op jit(solution)/shard_map/all_to_all | solution.py:163
  90.8 5.9 %collective-permute-start.7 = (f32[32,27,128]{2,1,0:T(8,128)S(1)}, f32[32,27,128]{2,1,0:T(8,128)S(1)}, u32[]{:S(2)}, u32[]{:S(2)}) collective-permute-start(f32[32,27,128]{2,1,0:T(8,128)S(1)} %all_to_all.21.mine), channel_id=1, source_target_pairs={{0,8},{8,0},{1,9},{9,1},{2,10},{10,2},{3,11},{11,3},{4,12},{12,4},... | collective-permute-start | bytes 1327112 | tf_op jit(solution)/shard_map/ppermute | solution.py:225
  96.7 1.9 %collective-permute-start.5 = (bf16[8,32,640]{2,1,0:T(8,128)(2,1)S(1)}, bf16[8,32,640]{2,1,0:T(8,128)(2,1)S(1)}, u32[]{:S(2)}, u32[]{:S(2)}) collective-permute-start(bf16[8,32,640]{2,1,0:T(8,128)(2,1)S(1)} %all-to-all-done.refs_4_.refs_1_), channel_id=1, source_target_pairs={{8,0},{16,8},{24,16},{32,24},{40,32},{48,40},{56,48},{9,1},{17,9},... | collective-permute-start | bytes 983048 | tf_op jit(solution)/shard_map/ppermute | solution.py:159
  98.6 3.6 %collective-permute-start.4 = (bf16[8,32,640]{2,1,0:T(8,128)(2,1)S(1)}, bf16[8,32,640]{2,1,0:T(8,128)(2,1)S(1)}, u32[]{:S(2)}, u32[]{:S(2)}) collective-permute-start(bf16[8,32,640]{2,1,0:T(8,128)(2,1)S(1)} %all-to-all-done.refs_4_.refs_1_), channel_id=1, source_target_pairs={{0,8},{8,16},{16,24},{24,32},{32,40},{40,48},{48,56},{1,9},{9,17},... | collective-permute-start | bytes 983048 | tf_op jit(solution)/shard_map/ppermute | solution.py:159
  102.3 2.8 %collective-permute-done.5.refs_2_ = bf16[8,32,640]{2,1,0:T(8,128)(2,1)S(1)} collective-permute-done((bf16[8,32,640]{2,1,0:T(8,128)(2,1)S(1)}, bf16[8,32,640]{2,1,0:T(8,128)(2,1)S(1)}, u32[]{:S(2)}, u32[]{:S(2)}) %collective-permute-start.5) | collective-permute-done | bytes 327712 | tf_op jit(solution)/shard_map/ppermute | solution.py:159
  105.1 1.2 %collective-permute-done.4.refs_0_ = bf16[8,32,640]{2,1,0:T(8,128)(2,1)S(1)} collective-permute-done((bf16[8,32,640]{2,1,0:T(8,128)(2,1)S(1)}, bf16[8,32,640]{2,1,0:T(8,128)(2,1)S(1)}, u32[]{:S(2)}, u32[]{:S(2)}) %collective-permute-start.4) | collective-permute-done | bytes 327712 | tf_op jit(solution)/shard_map/ppermute | solution.py:159
  106.3 1.4 %shard_map.62 = bf16[8,32,64]{2,1,0:T(8,128)(2,1)} custom-call(bf16[8,32,640]{2,1,0:T(8,128)(2,1)S(1)} %collective-permute-done.4.refs_0_, bf16[8,32,640]{2,1,0:T(8,128)(2,1)S(1)} %all-to-all-done.refs_4_.refs_1_, bf16[8,32,640]{2,1,0:T(8,128)(2,1)S(1)} %collective-permute-done.5.refs_2_, bf16[864,256]{1,0:T(8,128)(2,1)S(1)} %bitcast.16), custom_call_target="tpu_custom_call" | custom-call | flops 226492416 | bytes 1458176 | tf_op jit(solution)/shard_map/pallas_call | solution.py:23
  107.7 0.0 all-to-all-done.1.partial
  107.7 0.7 shard_map.61
  108.4 0.0 collective-permute-done.7.other
  108.4 1.0 shard_map.65
  (4 shorter events, 0.0 us)
Async XLA Ops:
  0.6 0.8 copy-start.1
  1.5 0.8 copy-start.2
  2.3 29.5 %copy-start = (bf16[27,32,256]{2,1,0:T(8,128)(2,1)S(1)}, bf16[27,32,256]{2,1,0:T(8,128)(2,1)}, u32[]{:S(2)}) copy-start(bf16[27,32,256]{2,1,0:T(8,128)(2,1)} %param.4) | copy-start | bytes 1327108
  2.3 5.5 %collective-permute-start = (bf16[64,64]{1,0:T(8,128)(2,1)S(1)}, bf16[64,64]{1,0:T(8,128)(2,1)S(1)}, u32[]{:S(2)}, u32[]{:S(2)}) collective-permute-start(bf16[64,64]{1,0:T(8,128)(2,1)S(1)} %get-tuple-element.10), channel_id=1, source_target_pairs={{0,1},{1,2},{2,3},{3,4},{4,5},{5,6},{6,7},{8,9},{9,10},{10,11},{11... | collective-permute-start | bytes 24584 | tf_op jit(solution)/shard_map/ppermute | solution.py:159
  6.5 4.5 %collective-permute-start.1 = (bf16[64,64]{1,0:T(8,128)(2,1)S(1)}, bf16[64,64]{1,0:T(8,128)(2,1)S(1)}, u32[]{:S(2)}, u32[]{:S(2)}) collective-permute-start(bf16[64,64]{1,0:T(8,128)(2,1)S(1)} %get-tuple-element.11), channel_id=1, source_target_pairs={{1,0},{2,1},{3,2},{4,3},{5,4},{6,5},{7,6},{9,8},{10,9},{11,10},{12... | collective-permute-start | bytes 24584 | tf_op jit(solution)/shard_map/ppermute | solution.py:159
  11.8 20.0 %all-to-all-start = ((bf16[8,32,640]{2,1,0:T(8,128)(2,1)}), bf16[8,32,640]{2,1,0:T(8,128)(2,1)S(1)}, u32[]{:S(2)}, u32[]{:S(2)}) async-start(bf16[8,32,640]{2,1,0:T(8,128)(2,1)} %get-tuple-element.13), calls=%async_computation | async-start | bytes 655360 | tf_op jit(solution)/shard_map/all_to_all | solution.py:163
  21.8 7.4 %collective-permute-start.3 = (bf16[32,640]{1,0:T(8,128)(2,1)S(1)}, bf16[32,640]{1,0:T(8,128)(2,1)S(1)}, u32[]{:S(2)}, u32[]{:S(2)}) collective-permute-start(bf16[32,640]{1,0:T(8,128)(2,1)S(1)} %get-tuple-element.12.refs_2_), channel_id=1, source_target_pairs={{8,0},{16,8},{24,16},{32,24},{40,32},{48,40},{56,48},{9,1},{17,9},... | collective-permute-start | bytes 122888 | tf_op jit(solution)/shard_map/ppermute | solution.py:159
  26.1 4.1 %collective-permute-start.2 = (bf16[32,640]{1,0:T(8,128)(2,1)S(1)}, bf16[32,640]{1,0:T(8,128)(2,1)S(1)}, u32[]{:S(2)}, u32[]{:S(2)}) collective-permute-start(bf16[32,640]{1,0:T(8,128)(2,1)S(1)} %get-tuple-element.12.refs_2_), channel_id=1, source_target_pairs={{0,8},{8,16},{16,24},{24,32},{32,40},{40,48},{48,56},{1,9},{9,17},... | collective-permute-start | bytes 122888 | tf_op jit(solution)/shard_map/ppermute | solution.py:159
  33.6 7.7 %collective-permute-start.6 = (f32[32,27,128]{2,1,0:T(8,128)S(1)}, f32[32,27,128]{2,1,0:T(8,128)S(1)}, u32[]{:S(2)}, u32[]{:S(2)}) collective-permute-start(f32[32,27,128]{2,1,0:T(8,128)S(1)} %get-tuple-element.16), channel_id=1, source_target_pairs={{0,8},{8,0},{1,9},{9,1},{2,10},{10,2},{3,11},{11,3},{4,12},{12,4},... | collective-permute-start | bytes 1327112 | tf_op jit(solution)/shard_map/ppermute | solution.py:216
  87.3 20.4 %all-to-all-start.1 = ((f32[8,32,512]{2,1,0:T(8,128)}), f32[8,32,512]{2,1,0:T(8,128)S(1)}, u32[]{:S(2)}, u32[]{:S(2)}) async-start(f32[8,32,512]{2,1,0:T(8,128)} %get-tuple-element.14), calls=%async_computation.1 | async-start | bytes 1048576 | tf_op jit(solution)/shard_map/all_to_all | solution.py:163
  90.8 17.6 %collective-permute-start.7 = (f32[32,27,128]{2,1,0:T(8,128)S(1)}, f32[32,27,128]{2,1,0:T(8,128)S(1)}, u32[]{:S(2)}, u32[]{:S(2)}) collective-permute-start(f32[32,27,128]{2,1,0:T(8,128)S(1)} %all_to_all.21.mine), channel_id=1, source_target_pairs={{0,8},{8,0},{1,9},{9,1},{2,10},{10,2},{3,11},{11,3},{4,12},{12,4},... | collective-permute-start | bytes 1327112 | tf_op jit(solution)/shard_map/ppermute | solution.py:225
  96.7 8.4 %collective-permute-start.5 = (bf16[8,32,640]{2,1,0:T(8,128)(2,1)S(1)}, bf16[8,32,640]{2,1,0:T(8,128)(2,1)S(1)}, u32[]{:S(2)}, u32[]{:S(2)}) collective-permute-start(bf16[8,32,640]{2,1,0:T(8,128)(2,1)S(1)} %all-to-all-done.refs_4_.refs_1_), channel_id=1, source_target_pairs={{8,0},{16,8},{24,16},{32,24},{40,32},{48,40},{56,48},{9,1},{17,9},... | collective-permute-start | bytes 983048 | tf_op jit(solution)/shard_map/ppermute | solution.py:159
  98.6 7.6 %collective-permute-start.4 = (bf16[8,32,640]{2,1,0:T(8,128)(2,1)S(1)}, bf16[8,32,640]{2,1,0:T(8,128)(2,1)S(1)}, u32[]{:S(2)}, u32[]{:S(2)}) collective-permute-start(bf16[8,32,640]{2,1,0:T(8,128)(2,1)S(1)} %all-to-all-done.refs_4_.refs_1_), channel_id=1, source_target_pairs={{0,8},{8,16},{16,24},{24,32},{32,40},{40,48},{48,56},{1,9},{9,17},... | collective-permute-start | bytes 983048 | tf_op jit(solution)/shard_map/ppermute | solution.py:159

commit v2 on v1

--- a/solution.py
+++ b/solution.py
@@ -30,12 +30,17 @@
     )(*args)
 
 
-def edge_rows(v, g, first, last):
-    c, rows = v.shape[1], v.shape[0]
-    first[:c] = v[0]
-    first[c:] = g[0]
-    last[:c] = v[rows - 1]
-    last[c:] = g[rows - 1]
+def edge_rows(v, g, first, last, sems):
+    rows, c = v.shape[0], v.shape[1]
+    copies = []
+    for row, out in ((0, first), (rows - 1, last)):
+        for i, source in enumerate((v, g)):
+            to = out.at[pl.ds(i * c, c)]
+            copies.append(pltpu.make_async_copy(source.at[row], to, sems.at[len(copies)]))
+    for copy in copies:
+        copy.start()
+    for copy in copies:
+        copy.wait()
 
 
 def ring_rows(v, g, before, after, v_ring, g_copies):
@@ -56,7 +61,7 @@
     return (at >= 0) & (at < z)
 
 
-def forward_and_weights(z, core, below, own, above, g, k, keep, send, partial, columns):
+def forward_and_weights(z, at_device, below, own, above, g, k, keep, send, o_keep, o_send, columns):
     c = own.shape[0]
     lanes = own.shape[1]
     cells = lanes - 2 * z
@@ -78,7 +83,7 @@
     )
     half = total // 2
     low, high = terms[:, :half], terms[:, half:]
-    first = core[0] == 0
+    first = at_device[0] == 0
     kept = jnp.where(first, low, high)
     sent = jnp.where(first, high, low)
     pieces, rows = keep.shape[0], keep.shape[1]
@@ -86,7 +91,19 @@
         keep[piece] = kept[piece * rows : (piece + 1) * rows]
         send[piece] = sent[piece * rows : (piece + 1) * rows]
     out = lax.dot_general(k[...], columns[...], (((0,), (0,)), ((), ())), preferred_element_type=F32)
-    partial[...] = out.reshape(groups, total // groups, cells)
+    out = out.reshape(groups // 2, 2, total // groups, cells)
+    even = at_device[1] % 2 == 0
+    o_keep[...] = jnp.where(even, out[:, 0], out[:, 1])
+    o_send[...] = jnp.where(even, out[:, 1], out[:, 0])
+
+
+def halve_outputs(bit, at_device, mine, other, o_keep, o_send):
+    even = (at_device[1] // bit) % 2 == 0
+    for i in range(o_keep.shape[0]):
+        a = mine[2 * i] + other[2 * i]
+        b = mine[2 * i + 1] + other[2 * i + 1]
+        o_keep[i] = jnp.where(even, a, b)
+        o_send[i] = jnp.where(even, b, a)
 
 
 def input_gradient(z, below, own, above, k, out):
@@ -123,11 +140,8 @@
         out[r] = shifted[:, :z].astype(BF16)
 
 
-def sum_outputs(partial, out):
-    total = partial[0]
-    for part in range(1, partial.shape[0]):
-        total += partial[part]
-    split_rows(total, out)
+def sum_outputs(mine, other, out):
+    split_rows(mine[0] + other[0], out)
 
 
 def add_halves(keep, other, out):
@@ -143,9 +157,9 @@
         out[copy] = total
 
 
-def join_halves(core, mine, other, out):
+def join_halves(at_device, mine, other, out):
     pieces, rows, half = mine.shape
-    first = core[0] == 0
+    first = at_device[0] == 0
     for piece in range(pieces):
         a, b = mine[piece], other[piece]
         out[piece * rows : (piece + 1) * rows, :half] = jnp.where(first, a, b)
@@ -157,6 +171,10 @@
     up = [(i, i + 1) for i in range(n - 1)]
     down = [(i + 1, i) for i in range(n - 1)]
     return lax.ppermute(value_up, axis, up), lax.ppermute(value_down, axis, down)
+
+
+def swapped(value, bit):
+    return lax.ppermute(value, "chan", [(i, i ^ bit) for i in range(lax.axis_size("chan"))])
 
 
 def exchange(value, axis):
@@ -173,10 +191,19 @@
     v = volume[0].transpose(0, 2, 1)
     g = grad_out[0].transpose(0, 2, 1)
     k = kernel.reshape(taps * c, total)
-    core = lax.axis_index("core").reshape(1)
+    at_device = jnp.stack([lax.axis_index("core"), lax.axis_index("chan")]).astype(jnp.int32)
     work = 2 * taps * c * total * cells
 
-    first, last = call(edge_rows, [((2 * c, z), BF16)] * 2, 0, v, g)
+    edge = jax.ShapeDtypeStruct((2 * c, z), BF16)
+    first, last = pl.pallas_call(
+        edge_rows,
+        out_shape=[edge, edge],
+        in_specs=[pl.BlockSpec(memory_space=pltpu.HBM)] * 2,
+        out_specs=[pl.BlockSpec(memory_space=pltpu.VMEM)] * 2,
+        scratch_shapes=[pltpu.SemaphoreType.DMA((4,))],
+        compiler_params=PARAMS,
+        cost_estimate=pl.CostEstimate(flops=0, bytes_accessed=4 * c * z * 2, transcendentals=0),
+    )(v, g)
     before, after = neighbours(last, first, "sy")
     v_ring, g_copies = call(
         ring_rows,
@@ -195,18 +222,16 @@
     def weights(*refs):
         forward_and_weights(z, *refs)
 
-    operands = (core, v_below, v_ring, v_above, g_ring, k)
+    operands = (at_device, v_below, v_ring, v_above, g_ring, k)
     moved = sum(a.size * a.dtype.itemsize for a in operands) + 3 * math.prod(piece) * 4
-    keep, send, partial = pl.pallas_call(
+    block = (total // groups, cells)
+    keep, send, o_keep, o_send = pl.pallas_call(
         weights,
-        out_shape=[
-            jax.ShapeDtypeStruct(piece, F32),
-            jax.ShapeDtypeStruct(piece, F32),
-            jax.ShapeDtypeStruct((groups, total // groups, cells), F32),
-        ],
+        out_shape=[jax.ShapeDtypeStruct(piece, F32)] * 2
+        + [jax.ShapeDtypeStruct((groups // 2, *block), F32)] * 2,
         in_specs=[pl.BlockSpec(memory_space=pltpu.SMEM)]
         + [pl.BlockSpec(memory_space=pltpu.VMEM)] * 5,
-        out_specs=[pl.BlockSpec(memory_space=pltpu.VMEM)] * 3,
+        out_specs=[pl.BlockSpec(memory_space=pltpu.VMEM)] * 4,
         scratch_shapes=[pltpu.VMEM((taps * c, cells), BF16)],
         compiler_params=PARAMS,
         cost_estimate=pl.CostEstimate(flops=2 * work, bytes_accessed=moved, transcendentals=0),
@@ -214,25 +239,39 @@
 
     swap = [(0, 1), (1, 0)]
     (halves,) = call(add_halves, [(piece, F32)], 0, keep, lax.ppermute(send, "core", swap))
+    halves, o_send, g_ring = lax.optimization_barrier((halves, o_send, g_ring))
     parts = exchange(halves, ("x", "sy"))
+    g_below, g_above = neighbours(g_ring, g_ring, PLANE)
+    bit = 1
+    o_other = swapped(o_send, bit)
+    parts, o_other, g_below, g_above = lax.optimization_barrier((parts, o_other, g_below, g_above))
     scale = math.sqrt(cells * devices)
 
     def reduce_pieces(*refs):
         sum_pieces(scale, *refs)
 
     (copies,) = call(reduce_pieces, [(piece, F32)], 0, parts)
+    copies, o_other = lax.optimization_barrier((copies, o_other))
     mine = exchange(copies, ("x", "sy"))
-    other = lax.ppermute(mine, "core", swap)
-    (grad_kernel,) = call(join_halves, [((taps * c, total), F32)], 0, core, mine, other)
-
-    (out,) = call(sum_outputs, [((rows, c, z), BF16)], 0, exchange(partial, "chan"))
-
-    g_below, g_above = neighbours(g_ring, g_ring, PLANE)
+
+    while o_keep.shape[0] > 1:
+        bit *= 2
+
+        def halve(*refs, bit=bit):
+            halve_outputs(bit, *refs)
+
+        left = [((o_keep.shape[0] // 2, *block), F32)] * 2
+        o_keep, o_send = call(halve, left, 0, at_device, o_keep, o_other)
+        o_other = swapped(o_send, bit)
+    (out,) = call(sum_outputs, [((rows, c, z), BF16)], 0, o_keep, o_other)
 
     def inputs(*refs):
         input_gradient(z, *refs)
 
     (grad_input,) = call(inputs, [((rows, c, z), BF16)], work, g_below, g_ring, g_above, k)
+    mine, out, grad_input = lax.optimization_barrier((mine, out, grad_input))
+    other = lax.ppermute(mine, "core", swap)
+    (grad_kernel,) = call(join_halves, [((taps * c, total), F32)], 0, at_device, mine, other)
     return (
         out.transpose(0, 2, 1)[None],
         grad_input.transpose(0, 2, 1)[None],

time: 112 us -> 107 us (0.955); the launches traced: 109 us -> 106 us
  blocking collectives: 45.8 us -> 0 us
  starting transfers between devices: 43.9 us -> 64.5 us
  waiting for transfers between devices: 11.3 us -> 30.1 us
  Pallas kernels: 5.92 us -> 8.98 us
    all_to_all x2 -> x0, blocking collectives: 45.8 us -> none  [exchange(): return lax.all_to_all(value, axis, 0, 0, tiled=True)]
    ppermute x0 -> x3, waiting for transfers between devices: none -> 21.3 us  [swapped(): lax.ppermute(value, 'chan', [(i, i ^ bit) for i in range(lax.axis_size('c...]
    all_to_all x2 -> x3, starting transfers between devices: 13.5 us -> 29.1 us  [exchange(): return lax.all_to_all(value, axis, 0, 0, tiled=True)]
    ppermute x0 -> x3, starting transfers between devices: none -> 7.05 us  [swapped(): lax.ppermute(value, 'chan', [(i, i ^ bit) for i in range(lax.axis_size('c...]
    pallas_call x7 -> x8, Pallas kernels: 4.12 us -> 7.39 us  [call(): pl.pallas_call(kernel, out_shape=[jax.ShapeDtypeStruct(s, d) for s, d in...]
    ppermute x3, waiting for transfers between devices: 6.02 us -> 3.18 us  [neighbours(): lax.ppermute(value_down, axis, down)]
    ppermute x1, starting transfers between devices: 5.94 us -> 3.54 us  [body(): other = lax.ppermute(mine, 'core', swap)]
    ppermute x1, waiting for transfers between devices: 0.01 us -> 1.51 us  [body(): other = lax.ppermute(mine, 'core', swap)]
  transfers between devices with their start and end apart: 10 -> 14, of which waited for: 6 -> 8; matrix products, arithmetic and copies ran while one was open for 0% -> 0% of each run, Pallas kernels for 2% -> 3%
where the time goes in v2:
time: 107 us; the launch traced here: 106 us
  starting transfers between devices  64.5 us (60%)
  waiting for transfers between devices  30.1 us (28%)
  Pallas kernels  8.98 us (8%)
  local copies, waits for them, and re-layouts  1.68 us (2%)
    all_to_all x3, starting transfers between devices, exchange(): return lax.all_to_all(value, axis, 0, 0, tiled=True)  29.1 us
    ppermute x3, waiting for transfers between devices, swapped(): lax.ppermute(value, 'chan', [(i, i ^ bit) for i in range(lax.axis_size('c...  21.3 us
    ppermute x3, starting transfers between devices, neighbours(): lax.ppermute(value_up, axis, up)  10.5 us
    ppermute x3, starting transfers between devices, neighbours(): lax.ppermute(value_down, axis, down)  8.14 us
    pallas_call x8, Pallas kernels, call(): pl.pallas_call(kernel, out_shape=[jax.ShapeDtypeStruct(s, d) for s, d in...  7.39 us
    ppermute x3, starting transfers between devices, swapped(): lax.ppermute(value, 'chan', [(i, i ^ bit) for i in range(lax.axis_size('c...  7.05 us
    ppermute x1, starting transfers between devices, body(): lax.ppermute(send, 'core', swap)  6.18 us
    ppermute x1, starting transfers between devices, body(): other = lax.ppermute(mine, 'core', swap)  3.54 us
  transfers between devices with their start and end apart: 14, of which 8 were waited for; matrix products, arithmetic and copies ran while one was open for 0% of the time, Pallas kernels for 3%

profile of v2, /device:TPU:1, one launch (start us, length us, event | category | flops | bytes accessed | tf_op | source)
XLA Modules:
  0.0 106.1 jit_solution(14347814119421836418)
XLA Ops:
  0.6 0.8 copy-done.1
  1.5 0.8 copy-done.2
  2.4 4.2 %collective-permute-start = (bf16[64,64]{1,0:T(8,128)(2,1)S(1)}, bf16[64,64]{1,0:T(8,128)(2,1)S(1)}, u32[]{:S(2)}, u32[]{:S(2)}) collective-permute-start(bf16[64,64]{1,0:T(8,128)(2,1)S(1)} %get-tuple-element.27), channel_id=1, source_target_pairs={{0,1},{1,2},{2,3},{3,4},{4,5},{5,6},{6,7},{8,9},{9,10},{10,11},{11... | collective-permute-start | bytes 24584 | tf_op jit(solution)/shard_map/ppermute | solution.py:173
  6.6 1.3 %collective-permute-start.1 = (bf16[64,64]{1,0:T(8,128)(2,1)S(1)}, bf16[64,64]{1,0:T(8,128)(2,1)S(1)}, u32[]{:S(2)}, u32[]{:S(2)}) collective-permute-start(bf16[64,64]{1,0:T(8,128)(2,1)S(1)} %get-tuple-element.28), channel_id=1, source_target_pairs={{1,0},{2,1},{3,2},{4,3},{5,4},{6,5},{7,6},{9,8},{10,9},{11,10},{12... | collective-permute-start | bytes 24584 | tf_op jit(solution)/shard_map/ppermute | solution.py:173
  7.9 3.2 %collective-permute-done.1.after = bf16[64,64]{1,0:T(8,128)(2,1)S(1)} collective-permute-done((bf16[64,64]{1,0:T(8,128)(2,1)S(1)}, bf16[64,64]{1,0:T(8,128)(2,1)S(1)}, u32[]{:S(2)}, u32[]{:S(2)}) %collective-permute-start.1) | collective-permute-done | bytes 8224 | tf_op jit(solution)/shard_map/ppermute | solution.py:173
  11.0 0.8 shard_map.59
  11.9 10.0 %all-to-all-start = ((bf16[8,32,640]{2,1,0:T(8,128)(2,1)}), bf16[8,32,640]{2,1,0:T(8,128)(2,1)S(1)}, u32[]{:S(2)}, u32[]{:S(2)}) async-start(bf16[8,32,640]{2,1,0:T(8,128)(2,1)} %get-tuple-element.30), calls=%async_computation | async-start | bytes 655360 | tf_op jit(solution)/shard_map/all_to_all | solution.py:181
  21.9 4.3 %collective-permute-start.3 = (bf16[32,640]{1,0:T(8,128)(2,1)S(1)}, bf16[32,640]{1,0:T(8,128)(2,1)S(1)}, u32[]{:S(2)}, u32[]{:S(2)}) collective-permute-start(bf16[32,640]{1,0:T(8,128)(2,1)S(1)} %get-tuple-element.29.refs_2_), channel_id=1, source_target_pairs={{8,0},{16,8},{24,16},{32,24},{40,32},{48,40},{56,48},{9,1},{17,9},... | collective-permute-start | bytes 122888 | tf_op jit(solution)/shard_map/ppermute | solution.py:173
  26.2 3.0 %collective-permute-start.2 = (bf16[32,640]{1,0:T(8,128)(2,1)S(1)}, bf16[32,640]{1,0:T(8,128)(2,1)S(1)}, u32[]{:S(2)}, u32[]{:S(2)}) collective-permute-start(bf16[32,640]{1,0:T(8,128)(2,1)S(1)} %get-tuple-element.29.refs_2_), channel_id=1, source_target_pairs={{0,8},{8,16},{16,24},{24,32},{32,40},{40,48},{48,56},{1,9},{9,17},... | collective-permute-start | bytes 122888 | tf_op jit(solution)/shard_map/ppermute | solution.py:173
  29.3 1.0 collective-permute-done.2.refs_1_
  30.3 1.6 %all-to-all-done.refs_4_.refs_1_ = bf16[8,32,640]{2,1,0:T(8,128)(2,1)S(1)} async-done(((bf16[8,32,640]{2,1,0:T(8,128)(2,1)}), bf16[8,32,640]{2,1,0:T(8,128)(2,1)S(1)}, u32[]{:S(2)}, u32[]{:S(2)}) %all-to-all-start) | async-done | bytes 327712 | tf_op jit(solution)/shard_map/all_to_all | solution.py:181
  31.9 1.5 %shard_map.60 = (f32[32,27,128]{2,1,0:T(8,128)S(1)}, f32[32,27,128]{2,1,0:T(8,128)S(1)}, f32[4,32,512]{2,1,0:T(8,128)S(1)}, f32[4,32,512]{2,1,0:T(8,128)S(1)}) custom-call(s32[2]{0:T(128)S(1)} %pad_add_fusion.refs_0_.at_device, bf16[32,640]{1,0:T(8,128)(2,1)S(1)} %collective-permute-done.2.refs_1_, bf16[32,640]{1,0:T(8,128)(2,1)S(1)} %get-tuple-element.29.refs_2_, ...), custom_call_target="tpu_custom_call" | custom-call | flops 452984832 | bytes 2220040 | tf_op jit(solution)/shard_map/pallas_call | solution.py:228
  33.4 6.2 %collective-permute-start.4 = (f32[32,27,128]{2,1,0:T(8,128)S(1)}, f32[32,27,128]{2,1,0:T(8,128)S(1)}, u32[]{:S(2)}, u32[]{:S(2)}) collective-permute-start(f32[32,27,128]{2,1,0:T(8,128)S(1)} %get-tuple-element.32), channel_id=1, source_target_pairs={{0,8},{8,0},{1,9},{9,1},{2,10},{10,2},{3,11},{11,3},{4,12},{12,4},... | collective-permute-start | bytes 1327112 | tf_op jit(solution)/shard_map/ppermute | solution.py:241
  39.6 1.5 %collective-permute-done.4.other = f32[32,27,128]{2,1,0:T(8,128)S(1)} collective-permute-done((f32[32,27,128]{2,1,0:T(8,128)S(1)}, f32[32,27,128]{2,1,0:T(8,128)S(1)}, u32[]{:S(2)}, u32[]{:S(2)}) %collective-permute-start.4) | collective-permute-done | bytes 442400 | tf_op jit(solution)/shard_map/ppermute | solution.py:241
  41.1 0.9 shard_map.61
  42.0 9.9 %all-to-all-start.1 = ((f32[32,27,128]{2,1,0:T(8,128)}), f32[32,27,128]{2,1,0:T(8,128)S(1)}, u32[]{:S(2)}, u32[]{:S(2)}) async-start(f32[32,27,128]{2,1,0:T(8,128)} %shard_map.61), calls=%async_computation.1 | async-start | bytes 1048576 | tf_op jit(solution)/shard_map/all_to_all | solution.py:181
  51.9 2.6 %collective-permute-start.7 = (bf16[8,32,640]{2,1,0:T(8,128)(2,1)S(1)}, bf16[8,32,640]{2,1,0:T(8,128)(2,1)S(1)}, u32[]{:S(2)}, u32[]{:S(2)}) collective-permute-start(bf16[8,32,640]{2,1,0:T(8,128)(2,1)S(1)} %all-to-all-done.refs_4_.refs_1_), channel_id=1, source_target_pairs={{8,0},{16,8},{24,16},{32,24},{40,32},{48,40},{56,48},{9,1},{17,9},... | collective-permute-start | bytes 983048 | tf_op jit(solution)/shard_map/ppermute | solution.py:173
  54.4 3.3 %collective-permute-start.6 = (bf16[8,32,640]{2,1,0:T(8,128)(2,1)S(1)}, bf16[8,32,640]{2,1,0:T(8,128)(2,1)S(1)}, u32[]{:S(2)}, u32[]{:S(2)}) collective-permute-start(bf16[8,32,640]{2,1,0:T(8,128)(2,1)S(1)} %all-to-all-done.refs_4_.refs_1_), channel_id=1, source_target_pairs={{0,8},{8,16},{16,24},{24,32},{32,40},{40,48},{48,56},{1,9},{9,17},... | collective-permute-start | bytes 983048 | tf_op jit(solution)/shard_map/ppermute | solution.py:173
  57.8 2.2 %collective-permute-start.5 = (f32[4,32,512]{2,1,0:T(8,128)S(1)}, f32[4,32,512]{2,1,0:T(8,128)S(1)}, u32[]{:S(2)}, u32[]{:S(2)}) collective-permute-start(f32[4,32,512]{2,1,0:T(8,128)S(1)} %get-tuple-element.35), channel_id=1, source_target_pairs={{0,64},{64,0},{128,192},{192,128},{256,320},{320,256},{384,448},{4... | collective-permute-start | bytes 786440 | tf_op jit(solution)/shard_map/ppermute | solution.py:177
  60.0 7.6 %collective-permute-done.5.refs_2_ = f32[4,32,512]{2,1,0:T(8,128)S(1)} collective-permute-done((f32[4,32,512]{2,1,0:T(8,128)S(1)}, f32[4,32,512]{2,1,0:T(8,128)S(1)}, u32[]{:S(2)}, u32[]{:S(2)}) %collective-permute-start.5) | collective-permute-done | bytes 262176 | tf_op jit(solution)/shard_map/ppermute | solution.py:177
  67.6 0.9 shard_map.62
  68.5 9.2 %all-to-all-start.2 = ((f32[32,27,128]{2,1,0:T(8,128)}), f32[32,27,128]{2,1,0:T(8,128)S(1)}, u32[]{:S(2)}, u32[]{:S(2)}) async-start(f32[32,27,128]{2,1,0:T(8,128)} %shard_map.62), calls=%async_computation.2 | async-start | bytes 1048576 | tf_op jit(solution)/shard_map/all_to_all | solution.py:181
  77.7 0.6 shard_map.63
  78.3 1.9 %collective-permute-start.8 = (f32[2,32,512]{2,1,0:T(8,128)S(1)}, f32[2,32,512]{2,1,0:T(8,128)S(1)}, u32[]{:S(2)}, u32[]{:S(2)}) collective-permute-start(f32[2,32,512]{2,1,0:T(8,128)S(1)} %get-tuple-element.43), channel_id=1, source_target_pairs={{0,128},{64,192},{128,0},{192,64},{256,384},{320,448},{384,256},{4... | collective-permute-start | bytes 393224 | tf_op jit(solution)/shard_map/ppermute | solution.py:177
  80.2 9.1 %collective-permute-done.8.refs_2_ = f32[2,32,512]{2,1,0:T(8,128)S(1)} collective-permute-done((f32[2,32,512]{2,1,0:T(8,128)S(1)}, f32[2,32,512]{2,1,0:T(8,128)S(1)}, u32[]{:S(2)}, u32[]{:S(2)}) %collective-permute-start.8) | collective-permute-done | bytes 131104 | tf_op jit(solution)/shard_map/ppermute | solution.py:177
  89.9 2.9 %collective-permute-start.9 = (f32[1,32,512]{2,1,0:T(8,128)S(1)}, f32[1,32,512]{2,1,0:T(8,128)S(1)}, u32[]{:S(2)}, u32[]{:S(2)}) collective-permute-start(f32[1,32,512]{2,1,0:T(8,128)S(1)} %get-tuple-element.45), channel_id=1, source_target_pairs={{0,256},{64,320},{128,384},{192,448},{256,0},{320,64},{384,128},{4... | collective-permute-start | bytes 196616 | tf_op jit(solution)/shard_map/ppermute | solution.py:177
  92.8 1.4 %shard_map.66 = bf16[8,32,64]{2,1,0:T(8,128)(2,1)} custom-call(bf16[8,32,640]{2,1,0:T(8,128)(2,1)S(1)} %collective-permute-done.6.refs_0_, bf16[8,32,640]{2,1,0:T(8,128)(2,1)S(1)} %all-to-all-done.refs_4_.refs_1_, bf16[8,32,640]{2,1,0:T(8,128)(2,1)S(1)} %collective-permute-done.7.refs_2_, bf16[864,256]{1,0:T(8,128)(2,1)S(1)} %bitcast.17), custom_call_target="tpu_custom_call" | custom-call | flops 226492416 | bytes 1458176 | tf_op jit(solution)/shard_map/pallas_call | solution.py:23
  94.2 4.6 %collective-permute-done.9.other = f32[1,32,512]{2,1,0:T(8,128)S(1)} collective-permute-done((f32[1,32,512]{2,1,0:T(8,128)S(1)}, f32[1,32,512]{2,1,0:T(8,128)S(1)}, u32[]{:S(2)}, u32[]{:S(2)}) %collective-permute-start.9) | collective-permute-done | bytes 65568 | tf_op jit(solution)/shard_map/ppermute | solution.py:177
  98.8 0.7 shard_map.65
  99.5 3.5 %collective-permute-start.10 = (f32[32,27,128]{2,1,0:T(8,128)S(1)}, f32[32,27,128]{2,1,0:T(8,128)S(1)}, u32[]{:S(2)}, u32[]{:S(2)}) collective-permute-start(f32[32,27,128]{2,1,0:T(8,128)S(1)} %all-to-all-done.2.mine), channel_id=1, source_target_pairs={{0,8},{8,0},{1,9},{9,1},{2,10},{10,2},{3,11},{11,3},{4,12},{12,4},... | collective-permute-start | bytes 1327112 | tf_op jit(solution)/shard_map/ppermute | solution.py:273
  103.1 1.5 %collective-permute-done.10.other = f32[32,27,128]{2,1,0:T(8,128)S(1)} collective-permute-done((f32[32,27,128]{2,1,0:T(8,128)S(1)}, f32[32,27,128]{2,1,0:T(8,128)S(1)}, u32[]{:S(2)}, u32[]{:S(2)}) %collective-permute-start.10) | collective-permute-done | bytes 442400 | tf_op jit(solution)/shard_map/ppermute | solution.py:273
  104.6 1.6 %shard_map.67 = f32[864,256]{1,0:T(8,128)} custom-call(s32[2]{0:T(128)S(1)} %pad_add_fusion.refs_0_.at_device, f32[32,27,128]{2,1,0:T(8,128)S(1)} %all-to-all-done.2.mine, f32[32,27,128]{2,1,0:T(8,128)S(1)} %collective-permute-done.10.other), custom_call_target="tpu_custom_call" | custom-call | bytes 1769480 | tf_op jit(solution)/shard_map/pallas_call | solution.py:23
  (13 shorter events, 0.7 us)
Async XLA Ops:
  0.6 0.8 copy-start.1
  1.5 0.8 copy-start.2
  2.4 29.5 %copy-start = (bf16[27,32,256]{2,1,0:T(8,128)(2,1)S(1)}, bf16[27,32,256]{2,1,0:T(8,128)(2,1)}, u32[]{:S(2)}) copy-start(bf16[27,32,256]{2,1,0:T(8,128)(2,1)} %param.4) | copy-start | bytes 1327108
  2.4 5.5 %collective-permute-start = (bf16[64,64]{1,0:T(8,128)(2,1)S(1)}, bf16[64,64]{1,0:T(8,128)(2,1)S(1)}, u32[]{:S(2)}, u32[]{:S(2)}) collective-permute-start(bf16[64,64]{1,0:T(8,128)(2,1)S(1)} %get-tuple-element.27), channel_id=1, source_target_pairs={{0,1},{1,2},{2,3},{3,4},{4,5},{5,6},{6,7},{8,9},{9,10},{10,11},{11... | collective-permute-start | bytes 24584 | tf_op jit(solution)/shard_map/ppermute | solution.py:173
  6.6 4.5 %collective-permute-start.1 = (bf16[64,64]{1,0:T(8,128)(2,1)S(1)}, bf16[64,64]{1,0:T(8,128)(2,1)S(1)}, u32[]{:S(2)}, u32[]{:S(2)}) collective-permute-start(bf16[64,64]{1,0:T(8,128)(2,1)S(1)} %get-tuple-element.28), channel_id=1, source_target_pairs={{1,0},{2,1},{3,2},{4,3},{5,4},{6,5},{7,6},{9,8},{10,9},{11,10},{12... | collective-permute-start | bytes 24584 | tf_op jit(solution)/shard_map/ppermute | solution.py:173
  11.9 20.0 %all-to-all-start = ((bf16[8,32,640]{2,1,0:T(8,128)(2,1)}), bf16[8,32,640]{2,1,0:T(8,128)(2,1)S(1)}, u32[]{:S(2)}, u32[]{:S(2)}) async-start(bf16[8,32,640]{2,1,0:T(8,128)(2,1)} %get-tuple-element.30), calls=%async_computation | async-start | bytes 655360 | tf_op jit(solution)/shard_map/all_to_all | solution.py:181
  21.9 7.4 %collective-permute-start.3 = (bf16[32,640]{1,0:T(8,128)(2,1)S(1)}, bf16[32,640]{1,0:T(8,128)(2,1)S(1)}, u32[]{:S(2)}, u32[]{:S(2)}) collective-permute-start(bf16[32,640]{1,0:T(8,128)(2,1)S(1)} %get-tuple-element.29.refs_2_), channel_id=1, source_target_pairs={{8,0},{16,8},{24,16},{32,24},{40,32},{48,40},{56,48},{9,1},{17,9},... | collective-permute-start | bytes 122888 | tf_op jit(solution)/shard_map/ppermute | solution.py:173
  26.2 4.1 %collective-permute-start.2 = (bf16[32,640]{1,0:T(8,128)(2,1)S(1)}, bf16[32,640]{1,0:T(8,128)(2,1)S(1)}, u32[]{:S(2)}, u32[]{:S(2)}) collective-permute-start(bf16[32,640]{1,0:T(8,128)(2,1)S(1)} %get-tuple-element.29.refs_2_), channel_id=1, source_target_pairs={{0,8},{8,16},{16,24},{24,32},{32,40},{40,48},{48,56},{1,9},{9,17},... | collective-permute-start | bytes 122888 | tf_op jit(solution)/shard_map/ppermute | solution.py:173
  33.4 7.7 %collective-permute-start.4 = (f32[32,27,128]{2,1,0:T(8,128)S(1)}, f32[32,27,128]{2,1,0:T(8,128)S(1)}, u32[]{:S(2)}, u32[]{:S(2)}) collective-permute-start(f32[32,27,128]{2,1,0:T(8,128)S(1)} %get-tuple-element.32), channel_id=1, source_target_pairs={{0,8},{8,0},{1,9},{9,1},{2,10},{10,2},{3,11},{11,3},{4,12},{12,4},... | collective-permute-start | bytes 1327112 | tf_op jit(solution)/shard_map/ppermute | solution.py:241
  42.0 25.6 %all-to-all-start.1 = ((f32[32,27,128]{2,1,0:T(8,128)}), f32[32,27,128]{2,1,0:T(8,128)S(1)}, u32[]{:S(2)}, u32[]{:S(2)}) async-start(f32[32,27,128]{2,1,0:T(8,128)} %shard_map.61), calls=%async_computation.1 | async-start | bytes 1048576 | tf_op jit(solution)/shard_map/all_to_all | solution.py:181
  51.9 15.7 %collective-permute-start.7 = (bf16[8,32,640]{2,1,0:T(8,128)(2,1)S(1)}, bf16[8,32,640]{2,1,0:T(8,128)(2,1)S(1)}, u32[]{:S(2)}, u32[]{:S(2)}) collective-permute-start(bf16[8,32,640]{2,1,0:T(8,128)(2,1)S(1)} %all-to-all-done.refs_4_.refs_1_), channel_id=1, source_target_pairs={{8,0},{16,8},{24,16},{32,24},{40,32},{48,40},{56,48},{9,1},{17,9},... | collective-permute-start | bytes 983048 | tf_op jit(solution)/shard_map/ppermute | solution.py:173
  54.4 13.1 %collective-permute-start.6 = (bf16[8,32,640]{2,1,0:T(8,128)(2,1)S(1)}, bf16[8,32,640]{2,1,0:T(8,128)(2,1)S(1)}, u32[]{:S(2)}, u32[]{:S(2)}) collective-permute-start(bf16[8,32,640]{2,1,0:T(8,128)(2,1)S(1)} %all-to-all-done.refs_4_.refs_1_), channel_id=1, source_target_pairs={{0,8},{8,16},{16,24},{24,32},{32,40},{40,48},{48,56},{1,9},{9,17},... | collective-permute-start | bytes 983048 | tf_op jit(solution)/shard_map/ppermute | solution.py:173
  57.8 9.8 %collective-permute-start.5 = (f32[4,32,512]{2,1,0:T(8,128)S(1)}, f32[4,32,512]{2,1,0:T(8,128)S(1)}, u32[]{:S(2)}, u32[]{:S(2)}) collective-permute-start(f32[4,32,512]{2,1,0:T(8,128)S(1)} %get-tuple-element.35), channel_id=1, source_target_pairs={{0,64},{64,0},{128,192},{192,128},{256,320},{320,256},{384,448},{4... | collective-permute-start | bytes 786440 | tf_op jit(solution)/shard_map/ppermute | solution.py:177
  68.5 31.0 %all-to-all-start.2 = ((f32[32,27,128]{2,1,0:T(8,128)}), f32[32,27,128]{2,1,0:T(8,128)S(1)}, u32[]{:S(2)}, u32[]{:S(2)}) async-start(f32[32,27,128]{2,1,0:T(8,128)} %shard_map.62), calls=%async_computation.2 | async-start | bytes 1048576 | tf_op jit(solution)/shard_map/all_to_all | solution.py:181
  78.3 11.0 %collective-permute-start.8 = (f32[2,32,512]{2,1,0:T(8,128)S(1)}, f32[2,32,512]{2,1,0:T(8,128)S(1)}, u32[]{:S(2)}, u32[]{:S(2)}) collective-permute-start(f32[2,32,512]{2,1,0:T(8,128)S(1)} %get-tuple-element.43), channel_id=1, source_target_pairs={{0,128},{64,192},{128,0},{192,64},{256,384},{320,448},{384,256},{4... | collective-permute-start | bytes 393224 | tf_op jit(solution)/shard_map/ppermute | solution.py:177
  89.9 8.9 %collective-permute-start.9 = (f32[1,32,512]{2,1,0:T(8,128)S(1)}, f32[1,32,512]{2,1,0:T(8,128)S(1)}, u32[]{:S(2)}, u32[]{:S(2)}) collective-permute-start(f32[1,32,512]{2,1,0:T(8,128)S(1)} %get-tuple-element.45), channel_id=1, source_target_pairs={{0,256},{64,320},{128,384},{192,448},{256,0},{320,64},{384,128},{4... | collective-permute-start | bytes 196616 | tf_op jit(solution)/shard_map/ppermute | solution.py:177
  99.5 5.1 %collective-permute-start.10 = (f32[32,27,128]{2,1,0:T(8,128)S(1)}, f32[32,27,128]{2,1,0:T(8,128)S(1)}, u32[]{:S(2)}, u32[]{:S(2)}) collective-permute-start(f32[32,27,128]{2,1,0:T(8,128)S(1)} %all-to-all-done.2.mine), channel_id=1, source_target_pairs={{0,8},{8,0},{1,9},{9,1},{2,10},{10,2},{3,11},{11,3},{4,12},{12,4},... | collective-permute-start | bytes 1327112 | tf_op jit(solution)/shard_map/ppermute | solution.py:273

commit v3 on v1

v3 whole, which is shorter than its diff:
```python
import math

import jax
import jax.numpy as jnp
from jax import lax
from jax.experimental import pallas as pl
from jax.experimental.pallas import tpu as pltpu
from jax.sharding import Mesh
from jax.sharding import PartitionSpec as P

F32 = jnp.float32
BF16 = jnp.bfloat16
PLANE = ("x", "core")
PARAMS = pltpu.CompilerParams(vmem_limit_bytes=16 * 2**20)


def call(kernel, outs, flops, *args):
    moved = sum(a.size * a.dtype.itemsize for a in args)
    moved += sum(math.prod(s) * jnp.dtype(d).itemsize for s, d in outs)
    specs = [
        pl.BlockSpec(memory_space=pltpu.SMEM if a.dtype == jnp.int32 else pltpu.VMEM) for a in args
    ]
    return pl.pallas_call(
        kernel,
        out_shape=[jax.ShapeDtypeStruct(s, d) for s, d in outs],
        in_specs=specs,
        out_specs=[pl.BlockSpec(memory_space=pltpu.VMEM) for _ in outs],
        compiler_params=PARAMS,
        cost_estimate=pl.CostEstimate(flops=flops, bytes_accessed=moved, transcendentals=0),
    )(*args)


def first_sends(v, g, k, first, last, sends, v_own, g_own, k_own, sems):
    rows, c, z = g_own.shape
    cells, weights = rows * z, k.shape[0]
    moves = [
        pltpu.make_async_copy(v, v_own, sems.at[0]),
        pltpu.make_async_copy(g, g_own, sems.at[1]),
        pltpu.make_async_copy(k, k_own.at[pl.ds(0, weights)], sems.at[2]),
    ]
    for move in moves:
        move.start()
    k_own[weights:] = jnp.zeros((k_own.shape[0] - weights, k_own.shape[1]), BF16)
    moves[0].wait()
    first[...] = v_own[0]
    last[...] = v_own[rows - 1]
    v_flat = in_row([v_own[r] for r in range(rows)])
    moves[1].wait()
    g_flat = in_row([g_own[r] for r in range(rows)])
    moves[2].wait()
    turned = k_own[...].astype(F32).T.astype(BF16)
    for to in range(sends.shape[0]):
        sends[to, :, :cells] = g_flat
        sends[to, :, cells : 2 * cells] = v_flat
        sends[to, :, 2 * cells :] = turned[to * c : (to + 1) * c]


def in_row(parts):
    return jnp.concatenate([part.astype(F32) for part in parts], axis=1).astype(BF16)


def volume_ring(v, before, after, ring):
    ring[...] = in_row([v[r] for r in range(v.shape[0])] + [after[...], before[...]])


def both_rings(received, before, after, ring):
    groups, c, _ = received.shape
    half, z = groups * c, before.shape[1]
    cells = ring.shape[1] - 2 * z
    ring[:half, :cells] = received[:, :, :cells].reshape(half, cells)
    ring[half:, :cells] = received[:, :, cells : 2 * cells].reshape(half, cells)
    ring[:, cells:] = in_row([after[...], before[...]])


def weights_by_output(received, k_out):
    groups, c, width = received.shape
    taps = k_out.shape[0] // c
    start = width - pl.cdiv(taps * c, 128) * 128
    for tap in range(taps):
        at = start + tap * c
        k_out[tap * c : (tap + 1) * c] = in_row([received[i][:, at : at + c] for i in range(groups)])


def in_line(shape, z, shift):
    at = lax.broadcasted_iota(jnp.int32, shape, 1) % z + shift
    return (at >= 0) & (at < z)


def windows(z, below, own, above, columns):
    c = own.shape[0]
    lanes = own.shape[1]
    cells = lanes - 2 * z
    planes = jnp.concatenate([below[...], own[...], above[...]], axis=0).astype(F32)
    for e in range(3):
        moved = planes if e == 1 else pltpu.roll(planes, (1 - e) % lanes, 1)
        if e != 1:
            moved = jnp.where(in_line(moved.shape, z, e - 1), moved, 0.0)
        for b in range(3):
            window = moved if b == 1 else pltpu.roll(moved, (z * (1 - b)) % lanes, 1)
            window = window[:, :cells].astype(BF16)
            for a in range(3):
                at = (9 * a + 3 * b + e) * c
                columns[at : at + c, :] = window[a * c : (a + 1) * c]


def weight_terms(core, columns, received, keep, send, first, last):
    groups, c, _ = received.shape
    cells, total, z = columns.shape[1], groups * c, first.shape[1]
    g_own = received[:, :, :cells].reshape(total, cells)
    terms = lax.dot_general(
        columns[...], g_own, (((1,), (1,)), ((), ())), preferred_element_type=F32
    )
    half = total // 2
    low, high = terms[:, :half], terms[:, half:]
    is_low = core[0] == 0
    kept = jnp.where(is_low, low, high)
    sent = jnp.where(is_low, high, low)
    pieces, rows = keep.shape[0], keep.shape[1]
    for piece in range(pieces):
        keep[piece] = kept[piece * rows : (piece + 1) * rows]
        send[piece] = sent[piece * rows : (piece + 1) * rows]
    for i in range(2):
        at = slice(i * total, (i + 1) * total)
        first[at] = received[:, :, i * cells : i * cells + z].reshape(total, z)
        end = received[:, :, (i + 1) * cells - 2 * z : (i + 1) * cells].reshape(total, 2 * z)
        last[at] = pltpu.roll(end.astype(F32), z, 1)[:, :z].astype(BF16)


def convolve(z, sign, planes, k, out):
    lanes = planes[0].shape[1]
    taps = k.shape[0] // 3
    c = taps // 9
    terms = jnp.zeros((taps, lanes), F32)
    for a, plane in enumerate(planes[::sign]):
        terms += jnp.dot(k[a * taps : (a + 1) * taps, :], plane, preferred_element_type=F32)
    result = jnp.zeros((c, lanes), F32)
    for e in range(3):
        line = jnp.zeros((c, lanes), F32)
        for b in range(3):
            at = (3 * b + e) * c
            term = terms[at : at + c]
            line += term if b == 1 else pltpu.roll(term, (sign * z * (1 - b)) % lanes, 1)
        if e != 1:
            line = pltpu.roll(line, (sign * (1 - e)) % lanes, 1)
            line = jnp.where(in_line(line.shape, z, sign * (e - 1)), line, 0.0)
        result += line
    split_rows(result, out)


def both_convolutions(z, below, own, above, k, k_out, out, grad_input):
    half = own.shape[0] // 2
    convolve(z, 1, [ref[half:] for ref in (below, own, above)], k_out, out)
    convolve(z, -1, [ref[:half] for ref in (below, own, above)], k, grad_input)


def split_rows(value, out):
    rows, z = out.shape[0], out.shape[2]
    lanes = value.shape[1]
    for r in range(rows):
        shifted = value if r == 0 else pltpu.roll(value, lanes - r * z, 1)
        out[r] = shifted[:, :z].astype(BF16)


def add_halves(keep, other, out):
    out[...] = keep[...] + other[...]


def sum_pieces(scale, parts, out):
    total = parts[0]
    for part in range(1, parts.shape[0]):
        total += parts[part]
    total = total / scale
    for copy in range(out.shape[0]):
        out[copy] = total


def join_halves(core, mine, other, out):
    pieces, rows, half = mine.shape
    first = core[0] == 0
    for piece in range(pieces):
        a, b = mine[piece], other[piece]
        out[piece * rows : (piece + 1) * rows, :half] = jnp.where(first, a, b)
        out[piece * rows : (piece + 1) * rows, half:] = jnp.where(first, b, a)


def neighbours(value_up, value_down, axis):
    n = lax.axis_size(axis)
    up = [(i, i + 1) for i in range(n - 1)]
    down = [(i + 1, i) for i in range(n - 1)]
    return lax.ppermute(value_up, axis, up), lax.ppermute(value_down, axis, down)


def exchange(value, axis):
    return lax.all_to_all(value, axis, 0, 0, tiled=True)


def body(volume, kernel, grad_out):
    _, rows, z, c = volume.shape
    taps, _, total = kernel.shape
    cells, lanes = rows * z, (rows + 2) * z
    groups = lax.axis_size("chan")
    pieces = lax.axis_size("x") * lax.axis_size("sy")
    devices = pieces * lax.axis_size("core")
    v = volume[0].transpose(0, 2, 1)
    g = grad_out[0].transpose(0, 2, 1)
    k = kernel.reshape(taps * c, total)
    core = lax.axis_index("core").reshape(1).astype(jnp.int32)
    work = 2 * taps * c * total * cells
    weights = pl.cdiv(taps * c, 128) * 128
    width = 2 * cells + weights

    edge = jax.ShapeDtypeStruct((c, z), BF16)
    first, last, sends = pl.pallas_call(
        first_sends,
        out_shape=[edge, edge, jax.ShapeDtypeStruct((groups, c, width), BF16)],
        in_specs=[pl.BlockSpec(memory_space=pltpu.HBM)] * 3,
        out_specs=[pl.BlockSpec(memory_space=pltpu.VMEM)] * 3,
        scratch_shapes=[
            pltpu.VMEM((rows, c, z), BF16),
            pltpu.VMEM((rows, c, z), BF16),
            pltpu.VMEM((weights, total), BF16),
            pltpu.SemaphoreType.DMA((3,)),
        ],
        compiler_params=pltpu.CompilerParams(vmem_limit_bytes=60 * 2**20),
        cost_estimate=pl.CostEstimate(
            flops=0, bytes_accessed=groups * c * width * 4, transcendentals=0
        ),
    )(v, g, k)
    before, after = neighbours(last, first, "sy")
    received = exchange(sends, "chan")
    (v_ring,) = call(volume_ring, [((c, lanes), BF16)], 0, v, before, after)
    v_below, v_above = neighbours(v_ring, v_ring, PLANE)

    def around(*refs):
        windows(z, *refs)

    (columns,) = call(around, [((taps * c, cells), BF16)], 0, v_below, v_ring, v_above)
    piece = (pieces, taps * c // pieces, total // 2)
    end = ((2 * total, z), BF16)
    keep, send, first, last = call(
        weight_terms, [(piece, F32), (piece, F32), end, end], work, core, columns, received
    )
    swap = [(0, 1), (1, 0)]
    (halves,) = call(add_halves, [(piece, F32)], 0, keep, lax.ppermute(send, "core", swap))

    halves, first, last, received = lax.optimization_barrier((halves, first, last, received))
    parts = exchange(halves, ("x", "sy"))
    before, after = neighbours(last, first, "sy")
    (ring,) = call(both_rings, [((2 * total, lanes), BF16)], 0, received, before, after)
    (k_out,) = call(weights_by_output, [((taps * c, total), BF16)], 0, received)
    parts, ring, k_out = lax.optimization_barrier((parts, ring, k_out))
    scale = math.sqrt(cells * devices)

    def reduce_pieces(*refs):
        sum_pieces(scale, *refs)

    (copies,) = call(reduce_pieces, [(piece, F32)], 0, parts)
    copies, ring = lax.optimization_barrier((copies, ring))
    mine = exchange(copies, ("x", "sy"))
    below, above = neighbours(ring, ring, PLANE)

    def convolutions(*refs):
        both_convolutions(z, *refs)

    result = ((rows, c, z), BF16)
    out, grad_input = call(convolutions, [result, result], 2 * work, below, ring, above, k, k_out)
    mine, out, grad_input = lax.optimization_barrier((mine, out, grad_input))
    other = lax.ppermute(mine, "core", swap)
    (grad_kernel,) = call(join_halves, [((taps * c, total), F32)], 0, core, mine, other)
    return (
        out.transpose(0, 2, 1)[None],
        grad_input.transpose(0, 2, 1)[None],
        grad_kernel.reshape(taps, c, total),
    )


def solution(mesh):
    cores = 2
    shape = (mesh.shape["chan"], mesh.shape["sx"] // cores, cores, mesh.shape["sy"])
    split = Mesh(mesh.devices.reshape(shape), ("chan", "x", "core", "sy"))
    cells = P(PLANE, "sy", None, "chan")
    weights = P(None, "chan", None)
    return jax.shard_map(
        body,
        mesh=split,
        in_specs=(cells, weights, cells),
        out_specs=(cells, cells, weights),
        check_vma=False,
    )
```

time: 112 us -> 107 us (0.955); the launches traced: 109 us -> 106 us
  blocking collectives: 45.8 us -> 0 us
  waiting for transfers between devices: 11.3 us -> 40 us
  starting transfers between devices: 43.9 us -> 56.2 us
  Pallas kernels: 5.92 us -> 8.99 us
  local copies, waits for them, and re-layouts: 1.68 us -> 0.02 us
    all_to_all x2 -> x0, blocking collectives: 45.8 us -> none  [exchange(): return lax.all_to_all(value, axis, 0, 0, tiled=True)]
    all_to_all x2 -> x3, starting transfers between devices: 13.5 us -> 29.8 us  [exchange(): return lax.all_to_all(value, axis, 0, 0, tiled=True)]
    ppermute x3 -> x4, waiting for transfers between devices: 6.02 us -> 16.6 us  [neighbours(): lax.ppermute(value_down, axis, down)]
    all_to_all x2 -> x3, waiting for transfers between devices: 1.58 us -> 11.3 us  [exchange(): return lax.all_to_all(value, axis, 0, 0, tiled=True)]
    ppermute x3 -> x4, waiting for transfers between devices: 2.23 us -> 8.74 us  [neighbours(): lax.ppermute(value_up, axis, up)]
    ppermute x1, starting transfers between devices: 5.94 us -> 1.91 us  [body(): other = lax.ppermute(mine, 'core', swap)]
    ppermute x1, starting transfers between devices: 6.17 us -> 2.41 us  [body(): lax.ppermute(send, 'core', swap)]
    pallas_call x7 -> x9, Pallas kernels: 4.12 us -> 6.7 us  [call(): pl.pallas_call(kernel, out_shape=[jax.ShapeDtypeStruct(s, d) for s, d in...]
  transfers between devices with their start and end apart: 10 -> 13, of which waited for: 6 -> 8; matrix products, arithmetic and copies ran while one was open for 0% -> 0% of each run, Pallas kernels for 2% -> 3%
where the time goes in v3:
time: 107 us; the launch traced here: 106 us
  starting transfers between devices  56.2 us (53%)
  waiting for transfers between devices  40 us (37%)
  Pallas kernels  8.99 us (8%)
    all_to_all x3, starting transfers between devices, exchange(): return lax.all_to_all(value, axis, 0, 0, tiled=True)  29.8 us
    ppermute x4, waiting for transfers between devices, neighbours(): lax.ppermute(value_down, axis, down)  16.6 us
    ppermute x4, starting transfers between devices, neighbours(): lax.ppermute(value_up, axis, up)  12.7 us
    all_to_all x3, waiting for transfers between devices, exchange(): return lax.all_to_all(value, axis, 0, 0, tiled=True)  11.3 us
    ppermute x4, starting transfers between devices, neighbours(): lax.ppermute(value_down, axis, down)  9.42 us
    ppermute x4, waiting for transfers between devices, neighbours(): lax.ppermute(value_up, axis, up)  8.74 us
    pallas_call x9, Pallas kernels, call(): pl.pallas_call(kernel, out_shape=[jax.ShapeDtypeStruct(s, d) for s, d in...  6.7 us
    ppermute x1, starting transfers between devices, body(): lax.ppermute(send, 'core', swap)  2.41 us
  transfers between devices with their start and end apart: 13, of which 8 were waited for; matrix products, arithmetic and copies ran while one was open for 0% of the time, Pallas kernels for 3%

profile of v3, /device:TPU:1, one launch (start us, length us, event | category | flops | bytes accessed | tf_op | source)
XLA Modules:
  0.0 106.1 jit_solution(15544161360198291237)
XLA Ops:
  0.6 2.3 %shard_map.58 = (bf16[32,64]{1,0:T(8,128)(2,1)}, bf16[32,64]{1,0:T(8,128)(2,1)}, bf16[8,32,1920]{2,1,0:T(8,128)(2,1)}) custom-call(bf16[8,32,64]{2,1,0:T(8,128)(2,1)} %bitcast.17, bf16[8,32,64]{2,1,0:T(8,128)(2,1)} %bitcast.20, bf16[864,256]{1,0:T(8,128)(2,1)} %bitcast.15), custom_call_target="tpu_custom_call" | custom-call | bytes 1966080 | tf_op jit(solution)/shard_map/pallas_call | solution.py:213
  3.0 11.0 %all-to-all-start = ((bf16[8,32,1920]{2,1,0:T(8,128)(2,1)}), bf16[8,32,1920]{2,1,0:T(8,128)(2,1)S(1)}, u32[]{:S(2)}, u32[]{:S(2)}) async-start(bf16[8,32,1920]{2,1,0:T(8,128)(2,1)} %get-tuple-element.26), calls=%async_computation | async-start | bytes 1966080 | tf_op jit(solution)/shard_map/all_to_all | solution.py:194
  14.0 3.2 %collective-permute-start = (bf16[32,64]{1,0:T(8,128)(2,1)S(1)}, bf16[32,64]{1,0:T(8,128)(2,1)S(1)}, u32[]{:S(2)}, u32[]{:S(2)}) collective-permute-start(bf16[32,64]{1,0:T(8,128)(2,1)S(1)} %copy-done.3), channel_id=1, source_target_pairs={{0,1},{1,2},{2,3},{3,4},{4,5},{5,6},{6,7},{8,9},{9,10},{10,11},{11... | collective-permute-start | bytes 12296 | tf_op jit(solution)/shard_map/ppermute | solution.py:190
  17.2 1.3 %collective-permute-start.1 = (bf16[32,64]{1,0:T(8,128)(2,1)S(1)}, bf16[32,64]{1,0:T(8,128)(2,1)S(1)}, u32[]{:S(2)}, u32[]{:S(2)}) collective-permute-start(bf16[32,64]{1,0:T(8,128)(2,1)S(1)} %copy-done.2), channel_id=1, source_target_pairs={{1,0},{2,1},{3,2},{4,3},{5,4},{6,5},{7,6},{9,8},{10,9},{11,10},{12... | collective-permute-start | bytes 12296 | tf_op jit(solution)/shard_map/ppermute | solution.py:190
  18.5 3.4 %collective-permute-done.1.after = bf16[32,64]{1,0:T(8,128)(2,1)S(1)} collective-permute-done((bf16[32,64]{1,0:T(8,128)(2,1)S(1)}, bf16[32,64]{1,0:T(8,128)(2,1)S(1)}, u32[]{:S(2)}, u32[]{:S(2)}) %collective-permute-start.1) | collective-permute-done | bytes 4128 | tf_op jit(solution)/shard_map/ppermute | solution.py:190
  21.9 0.1 shard_map.59.refs_1_
  22.0 4.0 %collective-permute-start.3 = (bf16[32,640]{1,0:T(8,128)(2,1)S(1)}, bf16[32,640]{1,0:T(8,128)(2,1)S(1)}, u32[]{:S(2)}, u32[]{:S(2)}) collective-permute-start(bf16[32,640]{1,0:T(8,128)(2,1)S(1)} %shard_map.59.refs_1_), channel_id=1, source_target_pairs={{8,0},{16,8},{24,16},{32,24},{40,32},{48,40},{56,48},{9,1},{17,9},... | collective-permute-start | bytes 122888 | tf_op jit(solution)/shard_map/ppermute | solution.py:190
  26.0 3.0 %collective-permute-start.2 = (bf16[32,640]{1,0:T(8,128)(2,1)S(1)}, bf16[32,640]{1,0:T(8,128)(2,1)S(1)}, u32[]{:S(2)}, u32[]{:S(2)}) collective-permute-start(bf16[32,640]{1,0:T(8,128)(2,1)S(1)} %shard_map.59.refs_1_), channel_id=1, source_target_pairs={{0,8},{8,16},{16,24},{24,32},{32,40},{40,48},{48,56},{1,9},{9,17},... | collective-permute-start | bytes 122888 | tf_op jit(solution)/shard_map/ppermute | solution.py:190
  29.0 0.0 collective-permute-done.3.refs_2_
  29.0 1.0 collective-permute-done.2.refs_0_
  30.1 0.3 shard_map.60.columns
  30.4 11.3 %all-to-all-done.received = bf16[8,32,1920]{2,1,0:T(8,128)(2,1)S(1)} async-done(((bf16[8,32,1920]{2,1,0:T(8,128)(2,1)}), bf16[8,32,1920]{2,1,0:T(8,128)(2,1)S(1)}, u32[]{:S(2)}, u32[]{:S(2)}) %all-to-all-start) | async-done | bytes 983072 | tf_op jit(solution)/shard_map/all_to_all | solution.py:194
  41.8 0.4 shard_map.61
  42.2 2.4 %collective-permute-start.4 = (f32[32,27,128]{2,1,0:T(8,128)S(1)}, f32[32,27,128]{2,1,0:T(8,128)S(1)}, u32[]{:S(2)}, u32[]{:S(2)}) collective-permute-start(f32[32,27,128]{2,1,0:T(8,128)S(1)} %get-tuple-element.28), channel_id=1, source_target_pairs={{0,8},{8,0},{1,9},{9,1},{2,10},{10,2},{3,11},{11,3},{4,12},{12,4},... | collective-permute-start | bytes 1327112 | tf_op jit(solution)/shard_map/ppermute | solution.py:244
  44.6 1.5 %collective-permute-done.4.other = f32[32,27,128]{2,1,0:T(8,128)S(1)} collective-permute-done((f32[32,27,128]{2,1,0:T(8,128)S(1)}, f32[32,27,128]{2,1,0:T(8,128)S(1)}, u32[]{:S(2)}, u32[]{:S(2)}) %collective-permute-start.4) | collective-permute-done | bytes 442400 | tf_op jit(solution)/shard_map/ppermute | solution.py:244
  46.1 0.8 shard_map.62
  47.0 9.7 %all-to-all-start.1 = ((f32[32,27,128]{2,1,0:T(8,128)}), f32[32,27,128]{2,1,0:T(8,128)S(1)}, u32[]{:S(2)}, u32[]{:S(2)}) async-start(f32[32,27,128]{2,1,0:T(8,128)} %shard_map.62), calls=%async_computation.1 | async-start | bytes 1048576 | tf_op jit(solution)/shard_map/all_to_all | solution.py:194
  56.6 3.1 %collective-permute-start.5 = (bf16[512,64]{1,0:T(8,128)(2,1)S(1)}, bf16[512,64]{1,0:T(8,128)(2,1)S(1)}, u32[]{:S(2)}, u32[]{:S(2)}) collective-permute-start(bf16[512,64]{1,0:T(8,128)(2,1)S(1)} %get-tuple-element.33), channel_id=1, source_target_pairs={{0,1},{1,2},{2,3},{3,4},{4,5},{5,6},{6,7},{8,9},{9,10},{10,11},{11... | collective-permute-start | bytes 196616 | tf_op jit(solution)/shard_map/ppermute | solution.py:190
  59.8 1.3 %collective-permute-start.6 = (bf16[512,64]{1,0:T(8,128)(2,1)S(1)}, bf16[512,64]{1,0:T(8,128)(2,1)S(1)}, u32[]{:S(2)}, u32[]{:S(2)}) collective-permute-start(bf16[512,64]{1,0:T(8,128)(2,1)S(1)} %get-tuple-element.34), channel_id=1, source_target_pairs={{1,0},{2,1},{3,2},{4,3},{5,4},{6,5},{7,6},{9,8},{10,9},{11,10},{12... | collective-permute-start | bytes 196616 | tf_op jit(solution)/shard_map/ppermute | solution.py:190
  61.1 1.2 %shard_map.64.refs_4_ = bf16[864,256]{1,0:T(8,128)(2,1)S(1)} custom-call(bf16[8,32,1920]{2,1,0:T(8,128)(2,1)S(1)} %all-to-all-done.received), custom_call_target="tpu_custom_call" | custom-call | bytes 1425408 | tf_op jit(solution)/shard_map/pallas_call | solution.py:23
  62.3 7.7 %collective-permute-done.5.before = bf16[512,64]{1,0:T(8,128)(2,1)S(1)} collective-permute-done((bf16[512,64]{1,0:T(8,128)(2,1)S(1)}, bf16[512,64]{1,0:T(8,128)(2,1)S(1)}, u32[]{:S(2)}, u32[]{:S(2)}) %collective-permute-start.5) | collective-permute-done | bytes 65568 | tf_op jit(solution)/shard_map/ppermute | solution.py:190
  70.0 2.3 %collective-permute-done.6.after = bf16[512,64]{1,0:T(8,128)(2,1)S(1)} collective-permute-done((bf16[512,64]{1,0:T(8,128)(2,1)S(1)}, bf16[512,64]{1,0:T(8,128)(2,1)S(1)}, u32[]{:S(2)}, u32[]{:S(2)}) %collective-permute-start.6) | collective-permute-done | bytes 65568 | tf_op jit(solution)/shard_map/ppermute | solution.py:190
  72.3 0.1 shard_map.63.refs_1_
  72.4 0.9 shard_map.65
  73.3 9.1 %all-to-all-start.2 = ((f32[32,27,128]{2,1,0:T(8,128)}), f32[32,27,128]{2,1,0:T(8,128)S(1)}, u32[]{:S(2)}, u32[]{:S(2)}) async-start(f32[32,27,128]{2,1,0:T(8,128)} %shard_map.65), calls=%async_computation.2 | async-start | bytes 1048576 | tf_op jit(solution)/shard_map/all_to_all | solution.py:194
  82.4 2.8 %collective-permute-start.8 = (bf16[512,640]{1,0:T(8,128)(2,1)S(1)}, bf16[512,640]{1,0:T(8,128)(2,1)S(1)}, u32[]{:S(2)}, u32[]{:S(2)}) collective-permute-start(bf16[512,640]{1,0:T(8,128)(2,1)S(1)} %shard_map.63.refs_1_), channel_id=1, source_target_pairs={{8,0},{16,8},{24,16},{32,24},{40,32},{48,40},{56,48},{9,1},{17,9},... | collective-permute-start | bytes 1966088 | tf_op jit(solution)/shard_map/ppermute | solution.py:190
  85.3 3.3 %collective-permute-start.7 = (bf16[512,640]{1,0:T(8,128)(2,1)S(1)}, bf16[512,640]{1,0:T(8,128)(2,1)S(1)}, u32[]{:S(2)}, u32[]{:S(2)}) collective-permute-start(bf16[512,640]{1,0:T(8,128)(2,1)S(1)} %shard_map.63.refs_1_), channel_id=1, source_target_pairs={{0,8},{8,16},{16,24},{24,32},{32,40},{40,48},{48,56},{1,9},{9,17},... | collective-permute-start | bytes 1966088 | tf_op jit(solution)/shard_map/ppermute | solution.py:190
  88.6 10.9 %collective-permute-done.8.refs_2_ = bf16[512,640]{1,0:T(8,128)(2,1)S(1)} collective-permute-done((bf16[512,640]{1,0:T(8,128)(2,1)S(1)}, bf16[512,640]{1,0:T(8,128)(2,1)S(1)}, u32[]{:S(2)}, u32[]{:S(2)}) %collective-permute-start.8) | collective-permute-done | bytes 655392 | tf_op jit(solution)/shard_map/ppermute | solution.py:190
  99.5 1.8 %shard_map.66 = (bf16[8,32,64]{2,1,0:T(8,128)(2,1)}, bf16[8,32,64]{2,1,0:T(8,128)(2,1)}) custom-call(bf16[512,640]{1,0:T(8,128)(2,1)S(1)} %collective-permute-done.7.refs_0_, bf16[512,640]{1,0:T(8,128)(2,1)S(1)} %shard_map.63.refs_1_, bf16[512,640]{1,0:T(8,128)(2,1)S(1)} %collective-permute-done.8.refs_2_, bf16[864,256]{1,0:T(8,128)(2,1)S(1)} %bitcast.16, ...), custom_call_target="tpu_custom_call" | custom-call | flops 452984832 | bytes 2916352 | tf_op jit(solution)/shard_map/pallas_call | solution.py:23
  101.3 1.9 %collective-permute-start.9 = (f32[32,27,128]{2,1,0:T(8,128)S(1)}, f32[32,27,128]{2,1,0:T(8,128)S(1)}, u32[]{:S(2)}, u32[]{:S(2)}) collective-permute-start(f32[32,27,128]{2,1,0:T(8,128)S(1)} %all-to-all-done.2.mine), channel_id=1, source_target_pairs={{0,8},{8,0},{1,9},{9,1},{2,10},{10,2},{3,11},{11,3},{4,12},{12,4},... | collective-permute-start | bytes 1327112 | tf_op jit(solution)/shard_map/ppermute | solution.py:268
  103.2 1.9 %collective-permute-done.9.other = f32[32,27,128]{2,1,0:T(8,128)S(1)} collective-permute-done((f32[32,27,128]{2,1,0:T(8,128)S(1)}, f32[32,27,128]{2,1,0:T(8,128)S(1)}, u32[]{:S(2)}, u32[]{:S(2)}) %collective-permute-start.9) | collective-permute-done | bytes 442400 | tf_op jit(solution)/shard_map/ppermute | solution.py:268
  105.1 1.0 shard_map.67
  (12 shorter events, 0.0 us)
Async XLA Ops:
  2.9 11.0 %copy-start.3 = (bf16[32,64]{1,0:T(8,128)(2,1)S(1)}, bf16[32,64]{1,0:T(8,128)(2,1)}, u32[]{:S(2)}) copy-start(bf16[32,64]{1,0:T(8,128)(2,1)} %get-tuple-element.24) | copy-start | bytes 12292
  2.9 14.2 %copy-start.2 = (bf16[32,64]{1,0:T(8,128)(2,1)S(1)}, bf16[32,64]{1,0:T(8,128)(2,1)}, u32[]{:S(2)}) copy-start(bf16[32,64]{1,0:T(8,128)(2,1)} %get-tuple-element.25) | copy-start | bytes 12292
  3.0 18.9 %copy-start.1 = (bf16[1,8,64,32]{2,3,1,0:T(8,128)(2,1)S(1)}, bf16[1,8,64,32]{2,3,1,0:T(8,128)(2,1)}, u32[]{:S(2)}) copy-start(bf16[1,8,64,32]{2,3,1,0:T(8,128)(2,1)} %param.3) | copy-start | bytes 98308
  3.0 38.8 %all-to-all-start = ((bf16[8,32,1920]{2,1,0:T(8,128)(2,1)}), bf16[8,32,1920]{2,1,0:T(8,128)(2,1)S(1)}, u32[]{:S(2)}, u32[]{:S(2)}) async-start(bf16[8,32,1920]{2,1,0:T(8,128)(2,1)} %get-tuple-element.26), calls=%async_computation | async-start | bytes 1966080 | tf_op jit(solution)/shard_map/all_to_all | solution.py:194
  14.0 4.5 %collective-permute-start = (bf16[32,64]{1,0:T(8,128)(2,1)S(1)}, bf16[32,64]{1,0:T(8,128)(2,1)S(1)}, u32[]{:S(2)}, u32[]{:S(2)}) collective-permute-start(bf16[32,64]{1,0:T(8,128)(2,1)S(1)} %copy-done.3), channel_id=1, source_target_pairs={{0,1},{1,2},{2,3},{3,4},{4,5},{5,6},{6,7},{8,9},{9,10},{10,11},{11... | collective-permute-start | bytes 12296 | tf_op jit(solution)/shard_map/ppermute | solution.py:190
  17.2 4.7 %collective-permute-start.1 = (bf16[32,64]{1,0:T(8,128)(2,1)S(1)}, bf16[32,64]{1,0:T(8,128)(2,1)S(1)}, u32[]{:S(2)}, u32[]{:S(2)}) collective-permute-start(bf16[32,64]{1,0:T(8,128)(2,1)S(1)} %copy-done.2), channel_id=1, source_target_pairs={{1,0},{2,1},{3,2},{4,3},{5,4},{6,5},{7,6},{9,8},{10,9},{11,10},{12... | collective-permute-start | bytes 12296 | tf_op jit(solution)/shard_map/ppermute | solution.py:190
  22.0 7.1 %collective-permute-start.3 = (bf16[32,640]{1,0:T(8,128)(2,1)S(1)}, bf16[32,640]{1,0:T(8,128)(2,1)S(1)}, u32[]{:S(2)}, u32[]{:S(2)}) collective-permute-start(bf16[32,640]{1,0:T(8,128)(2,1)S(1)} %shard_map.59.refs_1_), channel_id=1, source_target_pairs={{8,0},{16,8},{24,16},{32,24},{40,32},{48,40},{56,48},{9,1},{17,9},... | collective-permute-start | bytes 122888 | tf_op jit(solution)/shard_map/ppermute | solution.py:190
  26.0 4.1 %collective-permute-start.2 = (bf16[32,640]{1,0:T(8,128)(2,1)S(1)}, bf16[32,640]{1,0:T(8,128)(2,1)S(1)}, u32[]{:S(2)}, u32[]{:S(2)}) collective-permute-start(bf16[32,640]{1,0:T(8,128)(2,1)S(1)} %shard_map.59.refs_1_), channel_id=1, source_target_pairs={{0,8},{8,16},{16,24},{24,32},{32,40},{40,48},{48,56},{1,9},{9,17},... | collective-permute-start | bytes 122888 | tf_op jit(solution)/shard_map/ppermute | solution.py:190
  42.2 3.9 %collective-permute-start.4 = (f32[32,27,128]{2,1,0:T(8,128)S(1)}, f32[32,27,128]{2,1,0:T(8,128)S(1)}, u32[]{:S(2)}, u32[]{:S(2)}) collective-permute-start(f32[32,27,128]{2,1,0:T(8,128)S(1)} %get-tuple-element.28), channel_id=1, source_target_pairs={{0,8},{8,0},{1,9},{9,1},{2,10},{10,2},{3,11},{11,3},{4,12},{12,4},... | collective-permute-start | bytes 1327112 | tf_op jit(solution)/shard_map/ppermute | solution.py:244
  47.0 25.4 %all-to-all-start.1 = ((f32[32,27,128]{2,1,0:T(8,128)}), f32[32,27,128]{2,1,0:T(8,128)S(1)}, u32[]{:S(2)}, u32[]{:S(2)}) async-start(f32[32,27,128]{2,1,0:T(8,128)} %shard_map.62), calls=%async_computation.1 | async-start | bytes 1048576 | tf_op jit(solution)/shard_map/all_to_all | solution.py:194
  56.6 13.4 %collective-permute-start.5 = (bf16[512,64]{1,0:T(8,128)(2,1)S(1)}, bf16[512,64]{1,0:T(8,128)(2,1)S(1)}, u32[]{:S(2)}, u32[]{:S(2)}) collective-permute-start(bf16[512,64]{1,0:T(8,128)(2,1)S(1)} %get-tuple-element.33), channel_id=1, source_target_pairs={{0,1},{1,2},{2,3},{3,4},{4,5},{5,6},{6,7},{8,9},{9,10},{10,11},{11... | collective-permute-start | bytes 196616 | tf_op jit(solution)/shard_map/ppermute | solution.py:190
  59.8 12.5 %collective-permute-start.6 = (bf16[512,64]{1,0:T(8,128)(2,1)S(1)}, bf16[512,64]{1,0:T(8,128)(2,1)S(1)}, u32[]{:S(2)}, u32[]{:S(2)}) collective-permute-start(bf16[512,64]{1,0:T(8,128)(2,1)S(1)} %get-tuple-element.34), channel_id=1, source_target_pairs={{1,0},{2,1},{3,2},{4,3},{5,4},{6,5},{7,6},{9,8},{10,9},{11,10},{12... | collective-permute-start | bytes 196616 | tf_op jit(solution)/shard_map/ppermute | solution.py:190
  73.3 26.2 %copy-start = (bf16[27,32,256]{2,1,0:T(8,128)(2,1)S(1)}, bf16[27,32,256]{2,1,0:T(8,128)(2,1)}, u32[]{:S(2)}) copy-start(bf16[27,32,256]{2,1,0:T(8,128)(2,1)} %param.4) | copy-start | bytes 1327108
  73.3 28.0 %all-to-all-start.2 = ((f32[32,27,128]{2,1,0:T(8,128)}), f32[32,27,128]{2,1,0:T(8,128)S(1)}, u32[]{:S(2)}, u32[]{:S(2)}) async-start(f32[32,27,128]{2,1,0:T(8,128)} %shard_map.65), calls=%async_computation.2 | async-start | bytes 1048576 | tf_op jit(solution)/shard_map/all_to_all | solution.py:194
  82.4 17.1 %collective-permute-start.8 = (bf16[512,640]{1,0:T(8,128)(2,1)S(1)}, bf16[512,640]{1,0:T(8,128)(2,1)S(1)}, u32[]{:S(2)}, u32[]{:S(2)}) collective-permute-start(bf16[512,640]{1,0:T(8,128)(2,1)S(1)} %shard_map.63.refs_1_), channel_id=1, source_target_pairs={{8,0},{16,8},{24,16},{32,24},{40,32},{48,40},{56,48},{9,1},{17,9},... | collective-permute-start | bytes 1966088 | tf_op jit(solution)/shard_map/ppermute | solution.py:190
  85.3 14.2 %collective-permute-start.7 = (bf16[512,640]{1,0:T(8,128)(2,1)S(1)}, bf16[512,640]{1,0:T(8,128)(2,1)S(1)}, u32[]{:S(2)}, u32[]{:S(2)}) collective-permute-start(bf16[512,640]{1,0:T(8,128)(2,1)S(1)} %shard_map.63.refs_1_), channel_id=1, source_target_pairs={{0,8},{8,16},{16,24},{24,32},{32,40},{40,48},{48,56},{1,9},{9,17},... | collective-permute-start | bytes 1966088 | tf_op jit(solution)/shard_map/ppermute | solution.py:190
  101.3 3.8 %collective-permute-start.9 = (f32[32,27,128]{2,1,0:T(8,128)S(1)}, f32[32,27,128]{2,1,0:T(8,128)S(1)}, u32[]{:S(2)}, u32[]{:S(2)}) collective-permute-start(f32[32,27,128]{2,1,0:T(8,128)S(1)} %all-to-all-done.2.mine), channel_id=1, source_target_pairs={{0,8},{8,0},{1,9},{9,1},{2,10},{10,2},{3,11},{11,3},{4,12},{12,4},... | collective-permute-start | bytes 1327112 | tf_op jit(solution)/shard_map/ppermute | solution.py:268

commit v4 on v3

--- a/solution.py
+++ b/solution.py
@@ -11,6 +11,7 @@
 F32 = jnp.float32
 BF16 = jnp.bfloat16
 PLANE = ("x", "core")
+TAPS = 27
 PARAMS = pltpu.CompilerParams(vmem_limit_bytes=16 * 2**20)
 
 
@@ -30,7 +31,7 @@
     )(*args)
 
 
-def first_sends(v, g, k, first, last, sends, v_own, g_own, k_own, sems):
+def first_sends(core, v, g, k, first, last, sends, v_own, g_own, k_own, sems):
     rows, c, z = g_own.shape
     cells, weights = rows * z, k.shape[0]
     moves = [
@@ -48,11 +49,14 @@
     moves[1].wait()
     g_flat = in_row([g_own[r] for r in range(rows)])
     moves[2].wait()
-    turned = k_own[...].astype(F32).T.astype(BF16)
+    turned = k_own[...].astype(F32).T
+    width = sends.shape[2] - 2 * cells
+    later = pltpu.roll(turned, k_own.shape[0] - (weights // c // 2) * c, 1)
+    half = jnp.where(core[0] == 0, turned[:, :width], later[:, :width]).astype(BF16)
     for to in range(sends.shape[0]):
         sends[to, :, :cells] = g_flat
         sends[to, :, cells : 2 * cells] = v_flat
-        sends[to, :, 2 * cells :] = turned[to * c : (to + 1) * c]
+        sends[to, :, 2 * cells :] = half[to * c : (to + 1) * c]
 
 
 def in_row(parts):
@@ -63,22 +67,17 @@
     ring[...] = in_row([v[r] for r in range(v.shape[0])] + [after[...], before[...]])
 
 
-def both_rings(received, before, after, ring):
-    groups, c, _ = received.shape
-    half, z = groups * c, before.shape[1]
-    cells = ring.shape[1] - 2 * z
-    ring[:half, :cells] = received[:, :, :cells].reshape(half, cells)
-    ring[half:, :cells] = received[:, :, cells : 2 * cells].reshape(half, cells)
-    ring[:, cells:] = in_row([after[...], before[...]])
-
-
-def weights_by_output(received, k_out):
-    groups, c, width = received.shape
-    taps = k_out.shape[0] // c
-    start = width - pl.cdiv(taps * c, 128) * 128
-    for tap in range(taps):
-        at = start + tap * c
-        k_out[tap * c : (tap + 1) * c] = in_row([received[i][:, at : at + c] for i in range(groups)])
+def weights_by_output(core, mine, other, k_out):
+    c = k_out.shape[0] // TAPS
+    groups = mine.shape[0] // c
+    middle = TAPS // 2
+    is_low = core[0] == 0
+    a, b = mine[...], other[...]
+    for tap in range(TAPS):
+        half = jnp.where(is_low, a, b) if tap < middle else jnp.where(is_low, b, a)
+        at = (tap if tap < middle else tap - middle) * c
+        blocks = [half[i * c : (i + 1) * c, at : at + c] for i in range(groups)]
+        k_out[tap * c : (tap + 1) * c] = in_row(blocks)
 
 
 def in_line(shape, z, shift):
@@ -103,9 +102,9 @@
                 columns[at : at + c, :] = window[a * c : (a + 1) * c]
 
 
-def weight_terms(core, columns, received, keep, send, first, last):
+def weight_terms(core, columns, received, keep, send, k_mine):
     groups, c, _ = received.shape
-    cells, total, z = columns.shape[1], groups * c, first.shape[1]
+    cells, total = columns.shape[1], groups * c
     g_own = received[:, :, :cells].reshape(total, cells)
     terms = lax.dot_general(
         columns[...], g_own, (((1,), (1,)), ((), ())), preferred_element_type=F32
@@ -119,38 +118,81 @@
     for piece in range(pieces):
         keep[piece] = kept[piece * rows : (piece + 1) * rows]
         send[piece] = sent[piece * rows : (piece + 1) * rows]
-    for i in range(2):
-        at = slice(i * total, (i + 1) * total)
-        first[at] = received[:, :, i * cells : i * cells + z].reshape(total, z)
-        end = received[:, :, (i + 1) * cells - 2 * z : (i + 1) * cells].reshape(total, 2 * z)
-        last[at] = pltpu.roll(end.astype(F32), z, 1)[:, :z].astype(BF16)
-
-
-def convolve(z, sign, planes, k, out):
-    lanes = planes[0].shape[1]
+    k_mine[...] = received[:, :, 2 * cells : 2 * cells + k_mine.shape[1]].reshape(k_mine.shape)
+
+
+def spread(z, sign, own, k):
+    lanes = own.shape[1] + 2 * z
     taps = k.shape[0] // 3
     c = taps // 9
-    terms = jnp.zeros((taps, lanes), F32)
-    for a, plane in enumerate(planes[::sign]):
-        terms += jnp.dot(k[a * taps : (a + 1) * taps, :], plane, preferred_element_type=F32)
-    result = jnp.zeros((c, lanes), F32)
-    for e in range(3):
-        line = jnp.zeros((c, lanes), F32)
-        for b in range(3):
-            at = (3 * b + e) * c
-            term = terms[at : at + c]
-            line += term if b == 1 else pltpu.roll(term, (sign * z * (1 - b)) % lanes, 1)
-        if e != 1:
-            line = pltpu.roll(line, (sign * (1 - e)) % lanes, 1)
-            line = jnp.where(in_line(line.shape, z, sign * (e - 1)), line, 0.0)
-        result += line
-    split_rows(result, out)
-
-
-def both_convolutions(z, below, own, above, k, k_out, out, grad_input):
-    half = own.shape[0] // 2
-    convolve(z, 1, [ref[half:] for ref in (below, own, above)], k_out, out)
-    convolve(z, -1, [ref[:half] for ref in (below, own, above)], k, grad_input)
+    result = []
+    for a in range(3)[:: -sign]:
+        terms = jnp.dot(k[a * taps : (a + 1) * taps, :], own, preferred_element_type=F32)
+        terms = jnp.concatenate([terms, jnp.zeros((taps, 2 * z), F32)], axis=1)
+        plane = jnp.zeros((c, lanes), F32)
+        for e in range(3):
+            line = jnp.zeros((c, lanes), F32)
+            for b in range(3):
+                at = (3 * b + e) * c
+                term = terms[at : at + c]
+                line += term if b == 1 else pltpu.roll(term, (sign * z * (1 - b)) % lanes, 1)
+            if e != 1:
+                line = pltpu.roll(line, (sign * (1 - e)) % lanes, 1)
+                line = jnp.where(in_line(line.shape, z, sign * (e - 1)), line, 0.0)
+            plane += line
+        result.append(plane)
+    return result
+
+
+def store_spread(planes, middle, up, down):
+    c, cells = middle.shape[0] // 3, middle.shape[1]
+    z = up.shape[1]
+    for i, plane in enumerate(planes):
+        at = slice(i * c, (i + 1) * c)
+        middle[at] = plane[:, :cells]
+        ends = plane[:, cells:]
+        up[at] = ends[:, :z]
+        down[at] = pltpu.roll(ends, z, 1)[:, :z]
+
+
+def spread_cotangent(z, received, k, middle, up, down):
+    groups, c, _ = received.shape
+    cells = middle.shape[1]
+    own = received[:, :, :cells].reshape(groups * c, cells)
+    store_spread(spread(z, -1, own, k), middle, up, down)
+
+
+def spread_volume(z, received, k_out, g_up, g_down, middle, up, down):
+    groups, c, _ = received.shape
+    cells = middle.shape[1]
+    own = received[:, :, cells : 2 * cells].reshape(groups * c, cells)
+    rows = g_up.shape[0]
+    store_spread(spread(z, 1, own, k_out), middle, up.at[pl.ds(rows, rows)], down.at[pl.ds(rows, rows)])
+    up[:rows] = g_up[...]
+    down[:rows] = g_down[...]
+
+
+def add_ends(g_middle, v_middle, before, after, own, to_below, to_above):
+    rows, cells = g_middle.shape
+    z, c = before.shape[1], rows // 3
+    first = jnp.concatenate([before[...], jnp.zeros((2 * rows, z), F32)], axis=1)
+    last = jnp.concatenate([jnp.zeros((2 * rows, z), F32), after[...]], axis=1)
+    for i, middle in enumerate((g_middle, v_middle)):
+        for part, out in enumerate((to_below, own, to_above)):
+            at = slice(part * c, (part + 1) * c)
+            from_end = slice(i * rows + part * c, i * rows + (part + 1) * c)
+            value = middle[at]
+            to = slice(i * c, (i + 1) * c)
+            out[to] = value
+            out[to, : 2 * z] = value[:, : 2 * z] + first[from_end]
+            out[to, cells - 2 * z :] = value[:, cells - 2 * z :] + last[from_end]
+
+
+def add_planes(own, below, above, out, grad_input):
+    total = own[...] + below[...] + above[...]
+    c = total.shape[0] // 2
+    split_rows(total[c:], out)
+    split_rows(total[:c], grad_input)
 
 
 def split_rows(value, out):
@@ -207,13 +249,15 @@
     core = lax.axis_index("core").reshape(1).astype(jnp.int32)
     work = 2 * taps * c * total * cells
     weights = pl.cdiv(taps * c, 128) * 128
-    width = 2 * cells + weights
+    half_taps = (taps - taps // 2) * c
+    width = 2 * cells + pl.cdiv(half_taps, 128) * 128
 
     edge = jax.ShapeDtypeStruct((c, z), BF16)
     first, last, sends = pl.pallas_call(
         first_sends,
         out_shape=[edge, edge, jax.ShapeDtypeStruct((groups, c, width), BF16)],
-        in_specs=[pl.BlockSpec(memory_space=pltpu.HBM)] * 3,
+        in_specs=[pl.BlockSpec(memory_space=pltpu.SMEM)]
+        + [pl.BlockSpec(memory_space=pltpu.HBM)] * 3,
         out_specs=[pl.BlockSpec(memory_space=pltpu.VMEM)] * 3,
         scratch_shapes=[
             pltpu.VMEM((rows, c, z), BF16),
@@ -225,7 +269,7 @@
         cost_estimate=pl.CostEstimate(
             flops=0, bytes_accessed=groups * c * width * 4, transcendentals=0
         ),
-    )(v, g, k)
+    )(core, v, g, k)
     before, after = neighbours(last, first, "sy")
     received = exchange(sends, "chan")
     (v_ring,) = call(volume_ring, [((c, lanes), BF16)], 0, v, before, after)
@@ -236,34 +280,52 @@
 
     (columns,) = call(around, [((taps * c, cells), BF16)], 0, v_below, v_ring, v_above)
     piece = (pieces, taps * c // pieces, total // 2)
-    end = ((2 * total, z), BF16)
-    keep, send, first, last = call(
-        weight_terms, [(piece, F32), (piece, F32), end, end], work, core, columns, received
+    keep, send, k_mine = call(
+        weight_terms,
+        [(piece, F32), (piece, F32), ((total, half_taps), BF16)],
+        work,
+        core,
+        columns,
+        received,
     )
     swap = [(0, 1), (1, 0)]
     (halves,) = call(add_halves, [(piece, F32)], 0, keep, lax.ppermute(send, "core", swap))
 
-    halves, first, last, received = lax.optimization_barrier((halves, first, last, received))
+    halves, k_mine, received = lax.optimization_barrier((halves, k_mine, received))
     parts = exchange(halves, ("x", "sy"))
-    before, after = neighbours(last, first, "sy")
-    (ring,) = call(both_rings, [((2 * total, lanes), BF16)], 0, received, before, after)
-    (k_out,) = call(weights_by_output, [((taps * c, total), BF16)], 0, received)
-    parts, ring, k_out = lax.optimization_barrier((parts, ring, k_out))
+    k_other = lax.ppermute(k_mine, "core", swap)
+    middle, ends = ((3 * c, cells), F32), ((3 * c, z), F32)
+
+    def from_cotangent(*refs):
+        spread_cotangent(z, *refs)
+
+    def from_volume(*refs):
+        spread_volume(z, *refs)
+
+    g_middle, g_up, g_down = call(from_cotangent, [middle, ends, ends], work, received, k)
+    (k_out,) = call(
+        weights_by_output, [((taps * c, total), BF16)], 0, core, k_mine, k_other
+    )
+    both_ends = ((6 * c, z), F32)
+    v_middle, up, down = call(
+        from_volume, [middle, both_ends, both_ends], work, received, k_out, g_up, g_down
+    )
+    before, after = neighbours(up, down, "sy")
+    parts, before, after = lax.optimization_barrier((parts, before, after))
     scale = math.sqrt(cells * devices)
 
     def reduce_pieces(*refs):
         sum_pieces(scale, *refs)
 
     (copies,) = call(reduce_pieces, [(piece, F32)], 0, parts)
-    copies, ring = lax.optimization_barrier((copies, ring))
+    copies, before, after = lax.optimization_barrier((copies, before, after))
     mine = exchange(copies, ("x", "sy"))
-    below, above = neighbours(ring, ring, PLANE)
-
-    def convolutions(*refs):
-        both_convolutions(z, *refs)
-
+    own, to_below, to_above = call(
+        add_ends, [((2 * c, cells), F32)] * 3, 0, g_middle, v_middle, before, after
+    )
+    below, above = neighbours(to_above, to_below, PLANE)
     result = ((rows, c, z), BF16)
-    out, grad_input = call(convolutions, [result, result], 2 * work, below, ring, above, k, k_out)
+    out, grad_input = call(add_planes, [result, result], 0, own, below, above)
     mine, out, grad_input = lax.optimization_barrier((mine, out, grad_input))
     other = lax.ppermute(mine, "core", swap)
     (grad_kernel,) = call(join_halves, [((taps * c, total), F32)], 0, core, mine, other)

time: 107 us -> 101 us (0.944)
  waiting for transfers between devices: 40 us -> 25.5 us
  starting transfers between devices: 56.2 us -> 64.3 us
    ppermute x4, waiting for transfers between devices: 16.6 us -> 9.82 us  [neighbours(): lax.ppermute(value_down, axis, down)]
    ppermute x1, starting transfers between devices: 1.91 us -> 6.38 us  [body(): other = lax.ppermute(mine, 'core', swap)]
    all_to_all x3, waiting for transfers between devices: 11.3 us -> 7.11 us  [exchange(): return lax.all_to_all(value, axis, 0, 0, tiled=True)]
    ppermute x4, waiting for transfers between devices: 8.74 us -> 5.17 us  [neighbours(): lax.ppermute(value_up, axis, up)]
    ppermute x0 -> x1, starting transfers between devices: none -> 2.56 us  [body(): k_other = lax.ppermute(k_mine, 'core', swap)]
    ppermute x4, starting transfers between devices: 12.7 us -> 14.9 us  [neighbours(): lax.ppermute(value_up, axis, up)]
    pallas_call x9 -> x11, Pallas kernels: 6.7 us -> 6.97 us  [call(): pl.pallas_call(kernel, out_shape=[jax.ShapeDtypeStruct(s, d) for s, d in...]
  transfers between devices with their start and end apart: 13 -> 14, of which waited for: 8 -> 10; matrix products, arithmetic and copies ran while one was open for 0% -> 0% of each run, Pallas kernels for 3% -> 4%
where the time goes in v4:
time: 101 us; the launch traced here: 100 us
  starting transfers between devices  64.3 us (64%)
  waiting for transfers between devices  25.5 us (25%)
  Pallas kernels  9.31 us (9%)
    all_to_all x3, starting transfers between devices, exchange(): return lax.all_to_all(value, axis, 0, 0, tiled=True)  29.5 us
    ppermute x4, starting transfers between devices, neighbours(): lax.ppermute(value_up, axis, up)  14.9 us
    ppermute x4, waiting for transfers between devices, neighbours(): lax.ppermute(value_down, axis, down)  9.82 us
    ppermute x4, starting transfers between devices, neighbours(): lax.ppermute(value_down, axis, down)  8.5 us
    all_to_all x3, waiting for transfers between devices, exchange(): return lax.all_to_all(value, axis, 0, 0, tiled=True)  7.11 us
    pallas_call x11, Pallas kernels, call(): pl.pallas_call(kernel, out_shape=[jax.ShapeDtypeStruct(s, d) for s, d in...  6.97 us
    ppermute x1, starting transfers between devices, body(): other = lax.ppermute(mine, 'core', swap)  6.38 us
    ppermute x4, waiting for transfers between devices, neighbours(): lax.ppermute(value_up, axis, up)  5.17 us
  transfers between devices with their start and end apart: 14, of which 10 were waited for; matrix products, arithmetic and copies ran while one was open for 0% of the time, Pallas kernels for 4%

profile of v4, /device:TPU:1, one launch (start us, length us, event | category | flops | bytes accessed | tf_op | source)
XLA Modules:
  0.0 100.0 jit_solution(7410094254672509986)
XLA Ops:
  0.6 2.3 %shard_map.58 = (bf16[32,64]{1,0:T(8,128)(2,1)}, bf16[32,64]{1,0:T(8,128)(2,1)}, bf16[8,32,1536]{2,1,0:T(8,128)(2,1)}) custom-call(s32[1]{0:T(128)} %bitcast.core, bf16[8,32,64]{2,1,0:T(8,128)(2,1)} %bitcast.17, bf16[8,32,64]{2,1,0:T(8,128)(2,1)} %bitcast.20, bf16[864,256]{1,0:T(8,128)(2,1)} %bitcast.15), custom_call_target="tpu_custom_call" | custom-call | bytes 1572864 | tf_op jit(solution)/shard_map/pallas_call | solution.py:256
  3.0 11.0 %all-to-all-start = ((bf16[8,32,1536]{2,1,0:T(8,128)(2,1)}), bf16[8,32,1536]{2,1,0:T(8,128)(2,1)S(1)}, u32[]{:S(2)}, u32[]{:S(2)}) async-start(bf16[8,32,1536]{2,1,0:T(8,128)(2,1)} %get-tuple-element.34), calls=%async_computation | async-start | bytes 1572864 | tf_op jit(solution)/shard_map/all_to_all | solution.py:236
  14.0 3.2 %collective-permute-start = (bf16[32,64]{1,0:T(8,128)(2,1)S(1)}, bf16[32,64]{1,0:T(8,128)(2,1)S(1)}, u32[]{:S(2)}, u32[]{:S(2)}) collective-permute-start(bf16[32,64]{1,0:T(8,128)(2,1)S(1)} %copy-done.3), channel_id=1, source_target_pairs={{0,1},{1,2},{2,3},{3,4},{4,5},{5,6},{6,7},{8,9},{9,10},{10,11},{11... | collective-permute-start | bytes 12296 | tf_op jit(solution)/shard_map/ppermute | solution.py:232
  17.2 1.3 %collective-permute-start.1 = (bf16[32,64]{1,0:T(8,128)(2,1)S(1)}, bf16[32,64]{1,0:T(8,128)(2,1)S(1)}, u32[]{:S(2)}, u32[]{:S(2)}) collective-permute-start(bf16[32,64]{1,0:T(8,128)(2,1)S(1)} %copy-done.2), channel_id=1, source_target_pairs={{1,0},{2,1},{3,2},{4,3},{5,4},{6,5},{7,6},{9,8},{10,9},{11,10},{12... | collective-permute-start | bytes 12296 | tf_op jit(solution)/shard_map/ppermute | solution.py:232
  18.6 3.4 %collective-permute-done.1.after = bf16[32,64]{1,0:T(8,128)(2,1)S(1)} collective-permute-done((bf16[32,64]{1,0:T(8,128)(2,1)S(1)}, bf16[32,64]{1,0:T(8,128)(2,1)S(1)}, u32[]{:S(2)}, u32[]{:S(2)}) %collective-permute-start.1) | collective-permute-done | bytes 4128 | tf_op jit(solution)/shard_map/ppermute | solution.py:232
  22.0 4.0 %collective-permute-start.3 = (bf16[32,640]{1,0:T(8,128)(2,1)S(1)}, bf16[32,640]{1,0:T(8,128)(2,1)S(1)}, u32[]{:S(2)}, u32[]{:S(2)}) collective-permute-start(bf16[32,640]{1,0:T(8,128)(2,1)S(1)} %shard_map.59.refs_1_), channel_id=1, source_target_pairs={{8,0},{16,8},{24,16},{32,24},{40,32},{48,40},{56,48},{9,1},{17,9},... | collective-permute-start | bytes 122888 | tf_op jit(solution)/shard_map/ppermute | solution.py:232
  26.0 3.0 %collective-permute-start.2 = (bf16[32,640]{1,0:T(8,128)(2,1)S(1)}, bf16[32,640]{1,0:T(8,128)(2,1)S(1)}, u32[]{:S(2)}, u32[]{:S(2)}) collective-permute-start(bf16[32,640]{1,0:T(8,128)(2,1)S(1)} %shard_map.59.refs_1_), channel_id=1, source_target_pairs={{0,8},{8,16},{16,24},{24,32},{32,40},{40,48},{48,56},{1,9},{9,17},... | collective-permute-start | bytes 122888 | tf_op jit(solution)/shard_map/ppermute | solution.py:232
  29.1 1.0 %collective-permute-done.2.refs_0_ = bf16[32,640]{1,0:T(8,128)(2,1)S(1)} collective-permute-done((bf16[32,640]{1,0:T(8,128)(2,1)S(1)}, bf16[32,640]{1,0:T(8,128)(2,1)S(1)}, u32[]{:S(2)}, u32[]{:S(2)}) %collective-permute-start.2) | collective-permute-done | bytes 40992 | tf_op jit(solution)/shard_map/ppermute | solution.py:232
  30.5 7.1 %all-to-all-done.received.refs_0_ = bf16[8,32,1536]{2,1,0:T(8,128)(2,1)S(1)} async-done(((bf16[8,32,1536]{2,1,0:T(8,128)(2,1)}), bf16[8,32,1536]{2,1,0:T(8,128)(2,1)S(1)}, u32[]{:S(2)}, u32[]{:S(2)}) %all-to-all-start) | async-done | bytes 786464 | tf_op jit(solution)/shard_map/all_to_all | solution.py:236
  37.6 0.4 shard_map.61
  38.0 2.4 %collective-permute-start.4 = (f32[32,27,128]{2,1,0:T(8,128)S(1)}, f32[32,27,128]{2,1,0:T(8,128)S(1)}, u32[]{:S(2)}, u32[]{:S(2)}) collective-permute-start(f32[32,27,128]{2,1,0:T(8,128)S(1)} %get-tuple-element.36), channel_id=1, source_target_pairs={{0,8},{8,0},{1,9},{9,1},{2,10},{10,2},{3,11},{11,3},{4,12},{12,4},... | collective-permute-start | bytes 1327112 | tf_op jit(solution)/shard_map/ppermute | solution.py:292
  40.4 1.5 %collective-permute-done.4.other = f32[32,27,128]{2,1,0:T(8,128)S(1)} collective-permute-done((f32[32,27,128]{2,1,0:T(8,128)S(1)}, f32[32,27,128]{2,1,0:T(8,128)S(1)}, u32[]{:S(2)}, u32[]{:S(2)}) %collective-permute-start.4) | collective-permute-done | bytes 442400 | tf_op jit(solution)/shard_map/ppermute | solution.py:292
  42.0 0.8 shard_map.62
  42.8 9.8 %all-to-all-start.1 = ((f32[32,27,128]{2,1,0:T(8,128)}), f32[32,27,128]{2,1,0:T(8,128)S(1)}, u32[]{:S(2)}, u32[]{:S(2)}) async-start(f32[32,27,128]{2,1,0:T(8,128)} %shard_map.62), calls=%async_computation.1 | async-start | bytes 1048576 | tf_op jit(solution)/shard_map/all_to_all | solution.py:236
  52.6 2.6 %collective-permute-start.5 = (bf16[256,448]{1,0:T(8,128)(2,1)S(1)}, bf16[256,448]{1,0:T(8,128)(2,1)S(1)}, u32[]{:S(2)}, u32[]{:S(2)}) collective-permute-start(bf16[256,448]{1,0:T(8,128)(2,1)S(1)} %get-tuple-element.40.mine), channel_id=1, source_target_pairs={{0,8},{8,0},{1,9},{9,1},{2,10},{10,2},{3,11},{11,3},{4,12},{12,4},... | collective-permute-start | bytes 688136 | tf_op jit(solution)/shard_map/ppermute | solution.py:296
  55.2 0.8 shard_map.64
  56.3 1.0 %shard_map.63.refs_1_ = bf16[864,256]{1,0:T(8,128)(2,1)S(1)} custom-call(s32[1]{0:T(128)} %bitcast.core, bf16[256,448]{1,0:T(8,128)(2,1)S(1)} %get-tuple-element.40.mine, bf16[256,448]{1,0:T(8,128)(2,1)S(1)} %collective-permute-done.5.other), custom_call_target="tpu_custom_call" | custom-call | bytes 901124 | tf_op jit(solution)/shard_map/pallas_call | solution.py:24
  57.4 0.8 shard_map.65
  58.1 3.4 %collective-permute-start.6 = (f32[192,64]{1,0:T(8,128)S(1)}, f32[192,64]{1,0:T(8,128)S(1)}, u32[]{:S(2)}, u32[]{:S(2)}) collective-permute-start(f32[192,64]{1,0:T(8,128)S(1)} %get-tuple-element.43), channel_id=1, source_target_pairs={{0,1},{1,2},{2,3},{3,4},{4,5},{5,6},{6,7},{8,9},{9,10},{10,11},{11... | collective-permute-start | bytes 147464 | tf_op jit(solution)/shard_map/ppermute | solution.py:232
  61.5 1.3 %collective-permute-start.7 = (f32[192,64]{1,0:T(8,128)S(1)}, f32[192,64]{1,0:T(8,128)S(1)}, u32[]{:S(2)}, u32[]{:S(2)}) collective-permute-start(f32[192,64]{1,0:T(8,128)S(1)} %get-tuple-element.44), channel_id=1, source_target_pairs={{1,0},{2,1},{3,2},{4,3},{5,4},{6,5},{7,6},{9,8},{10,9},{11,10},{12... | collective-permute-start | bytes 147464 | tf_op jit(solution)/shard_map/ppermute | solution.py:232
  62.8 2.7 %collective-permute-done.6.before = f32[192,64]{1,0:T(8,128)S(1)} collective-permute-done((f32[192,64]{1,0:T(8,128)S(1)}, f32[192,64]{1,0:T(8,128)S(1)}, u32[]{:S(2)}, u32[]{:S(2)}) %collective-permute-start.6) | collective-permute-done | bytes 49184 | tf_op jit(solution)/shard_map/ppermute | solution.py:232
  65.5 2.2 %collective-permute-done.7.after = f32[192,64]{1,0:T(8,128)S(1)} collective-permute-done((f32[192,64]{1,0:T(8,128)S(1)}, f32[192,64]{1,0:T(8,128)S(1)}, u32[]{:S(2)}, u32[]{:S(2)}) %collective-permute-start.7) | collective-permute-done | bytes 49184 | tf_op jit(solution)/shard_map/ppermute | solution.py:232
  67.8 0.9 shard_map.66
  68.7 8.7 %all-to-all-start.2 = ((f32[32,27,128]{2,1,0:T(8,128)}), f32[32,27,128]{2,1,0:T(8,128)S(1)}, u32[]{:S(2)}, u32[]{:S(2)}) async-start(f32[32,27,128]{2,1,0:T(8,128)} %shard_map.66), calls=%async_computation.2 | async-start | bytes 1048576 | tf_op jit(solution)/shard_map/all_to_all | solution.py:236
  77.5 5.3 %collective-permute-start.8 = (f32[64,512]{1,0:T(8,128)S(1)}, f32[64,512]{1,0:T(8,128)S(1)}, u32[]{:S(2)}, u32[]{:S(2)}) collective-permute-start(f32[64,512]{1,0:T(8,128)S(1)} %get-tuple-element.54), channel_id=1, source_target_pairs={{0,8},{8,16},{16,24},{24,32},{32,40},{40,48},{48,56},{1,9},{9,17},... | collective-permute-start | bytes 393224 | tf_op jit(solution)/shard_map/ppermute | solution.py:232
  82.8 1.9 %collective-permute-start.9 = (f32[64,512]{1,0:T(8,128)S(1)}, f32[64,512]{1,0:T(8,128)S(1)}, u32[]{:S(2)}, u32[]{:S(2)}) collective-permute-start(f32[64,512]{1,0:T(8,128)S(1)} %get-tuple-element.55), channel_id=1, source_target_pairs={{8,0},{16,8},{24,16},{32,24},{40,32},{48,40},{56,48},{9,1},{17,9},... | collective-permute-start | bytes 393224 | tf_op jit(solution)/shard_map/ppermute | solution.py:232
  84.7 1.4 %collective-permute-done.8.below = f32[64,512]{1,0:T(8,128)S(1)} collective-permute-done((f32[64,512]{1,0:T(8,128)S(1)}, f32[64,512]{1,0:T(8,128)S(1)}, u32[]{:S(2)}, u32[]{:S(2)}) %collective-permute-start.8) | collective-permute-done | bytes 131104 | tf_op jit(solution)/shard_map/ppermute | solution.py:232
  86.1 4.2 %collective-permute-done.9.above = f32[64,512]{1,0:T(8,128)S(1)} collective-permute-done((f32[64,512]{1,0:T(8,128)S(1)}, f32[64,512]{1,0:T(8,128)S(1)}, u32[]{:S(2)}, u32[]{:S(2)}) %collective-permute-start.9) | collective-permute-done | bytes 131104 | tf_op jit(solution)/shard_map/ppermute | solution.py:232
  90.3 0.7 shard_map.68
  91.1 6.4 %collective-permute-start.10 = (f32[32,27,128]{2,1,0:T(8,128)S(1)}, f32[32,27,128]{2,1,0:T(8,128)S(1)}, u32[]{:S(2)}, u32[]{:S(2)}) collective-permute-start(f32[32,27,128]{2,1,0:T(8,128)S(1)} %all-to-all-done.2.mine), channel_id=1, source_target_pairs={{0,8},{8,0},{1,9},{9,1},{2,10},{10,2},{3,11},{11,3},{4,12},{12,4},... | collective-permute-start | bytes 1327112 | tf_op jit(solution)/shard_map/ppermute | solution.py:330
  97.4 1.5 %collective-permute-done.10.other = f32[32,27,128]{2,1,0:T(8,128)S(1)} collective-permute-done((f32[32,27,128]{2,1,0:T(8,128)S(1)}, f32[32,27,128]{2,1,0:T(8,128)S(1)}, u32[]{:S(2)}, u32[]{:S(2)}) %collective-permute-start.10) | collective-permute-done | bytes 442400 | tf_op jit(solution)/shard_map/ppermute | solution.py:330
  99.0 1.0 %shard_map.69 = f32[864,256]{1,0:T(8,128)} custom-call(s32[1]{0:T(128)} %bitcast.core, f32[32,27,128]{2,1,0:T(8,128)S(1)} %all-to-all-done.2.mine, f32[32,27,128]{2,1,0:T(8,128)S(1)} %collective-permute-done.10.other), custom_call_target="tpu_custom_call" | custom-call | bytes 1769476 | tf_op jit(solution)/shard_map/pallas_call | solution.py:24
  (16 shorter events, 1.0 us)
Async XLA Ops:
  3.0 11.0 %copy-start.3 = (bf16[32,64]{1,0:T(8,128)(2,1)S(1)}, bf16[32,64]{1,0:T(8,128)(2,1)}, u32[]{:S(2)}) copy-start(bf16[32,64]{1,0:T(8,128)(2,1)} %get-tuple-element.32) | copy-start | bytes 12292
  3.0 14.2 %copy-start.2 = (bf16[32,64]{1,0:T(8,128)(2,1)S(1)}, bf16[32,64]{1,0:T(8,128)(2,1)}, u32[]{:S(2)}) copy-start(bf16[32,64]{1,0:T(8,128)(2,1)} %get-tuple-element.33) | copy-start | bytes 12292
  3.0 18.9 %copy-start.1 = (bf16[1,8,64,32]{2,3,1,0:T(8,128)(2,1)S(1)}, bf16[1,8,64,32]{2,3,1,0:T(8,128)(2,1)}, u32[]{:S(2)}) copy-start(bf16[1,8,64,32]{2,3,1,0:T(8,128)(2,1)} %param.3) | copy-start | bytes 98308
  3.0 34.6 %all-to-all-start = ((bf16[8,32,1536]{2,1,0:T(8,128)(2,1)}), bf16[8,32,1536]{2,1,0:T(8,128)(2,1)S(1)}, u32[]{:S(2)}, u32[]{:S(2)}) async-start(bf16[8,32,1536]{2,1,0:T(8,128)(2,1)} %get-tuple-element.34), calls=%async_computation | async-start | bytes 1572864 | tf_op jit(solution)/shard_map/all_to_all | solution.py:236
  14.0 4.5 %collective-permute-start = (bf16[32,64]{1,0:T(8,128)(2,1)S(1)}, bf16[32,64]{1,0:T(8,128)(2,1)S(1)}, u32[]{:S(2)}, u32[]{:S(2)}) collective-permute-start(bf16[32,64]{1,0:T(8,128)(2,1)S(1)} %copy-done.3), channel_id=1, source_target_pairs={{0,1},{1,2},{2,3},{3,4},{4,5},{5,6},{6,7},{8,9},{9,10},{10,11},{11... | collective-permute-start | bytes 12296 | tf_op jit(solution)/shard_map/ppermute | solution.py:232
  17.2 4.7 %collective-permute-start.1 = (bf16[32,64]{1,0:T(8,128)(2,1)S(1)}, bf16[32,64]{1,0:T(8,128)(2,1)S(1)}, u32[]{:S(2)}, u32[]{:S(2)}) collective-permute-start(bf16[32,64]{1,0:T(8,128)(2,1)S(1)} %copy-done.2), channel_id=1, source_target_pairs={{1,0},{2,1},{3,2},{4,3},{5,4},{6,5},{7,6},{9,8},{10,9},{11,10},{12... | collective-permute-start | bytes 12296 | tf_op jit(solution)/shard_map/ppermute | solution.py:232
  22.0 7.1 %collective-permute-start.3 = (bf16[32,640]{1,0:T(8,128)(2,1)S(1)}, bf16[32,640]{1,0:T(8,128)(2,1)S(1)}, u32[]{:S(2)}, u32[]{:S(2)}) collective-permute-start(bf16[32,640]{1,0:T(8,128)(2,1)S(1)} %shard_map.59.refs_1_), channel_id=1, source_target_pairs={{8,0},{16,8},{24,16},{32,24},{40,32},{48,40},{56,48},{9,1},{17,9},... | collective-permute-start | bytes 122888 | tf_op jit(solution)/shard_map/ppermute | solution.py:232
  26.0 4.1 %collective-permute-start.2 = (bf16[32,640]{1,0:T(8,128)(2,1)S(1)}, bf16[32,640]{1,0:T(8,128)(2,1)S(1)}, u32[]{:S(2)}, u32[]{:S(2)}) collective-permute-start(bf16[32,640]{1,0:T(8,128)(2,1)S(1)} %shard_map.59.refs_1_), channel_id=1, source_target_pairs={{0,8},{8,16},{16,24},{24,32},{32,40},{40,48},{48,56},{1,9},{9,17},... | collective-permute-start | bytes 122888 | tf_op jit(solution)/shard_map/ppermute | solution.py:232
  38.0 3.9 %collective-permute-start.4 = (f32[32,27,128]{2,1,0:T(8,128)S(1)}, f32[32,27,128]{2,1,0:T(8,128)S(1)}, u32[]{:S(2)}, u32[]{:S(2)}) collective-permute-start(f32[32,27,128]{2,1,0:T(8,128)S(1)} %get-tuple-element.36), channel_id=1, source_target_pairs={{0,8},{8,0},{1,9},{9,1},{2,10},{10,2},{3,11},{11,3},{4,12},{12,4},... | collective-permute-start | bytes 1327112 | tf_op jit(solution)/shard_map/ppermute | solution.py:292
  42.8 12.4 %copy-start = (bf16[27,32,256]{2,1,0:T(8,128)(2,1)S(1)}, bf16[27,32,256]{2,1,0:T(8,128)(2,1)}, u32[]{:S(2)}) copy-start(bf16[27,32,256]{2,1,0:T(8,128)(2,1)} %param.4) | copy-start | bytes 1327108
  42.8 25.0 %all-to-all-start.1 = ((f32[32,27,128]{2,1,0:T(8,128)}), f32[32,27,128]{2,1,0:T(8,128)S(1)}, u32[]{:S(2)}, u32[]{:S(2)}) async-start(f32[32,27,128]{2,1,0:T(8,128)} %shard_map.62), calls=%async_computation.1 | async-start | bytes 1048576 | tf_op jit(solution)/shard_map/all_to_all | solution.py:236
  52.6 3.7 %collective-permute-start.5 = (bf16[256,448]{1,0:T(8,128)(2,1)S(1)}, bf16[256,448]{1,0:T(8,128)(2,1)S(1)}, u32[]{:S(2)}, u32[]{:S(2)}) collective-permute-start(bf16[256,448]{1,0:T(8,128)(2,1)S(1)} %get-tuple-element.40.mine), channel_id=1, source_target_pairs={{0,8},{8,0},{1,9},{9,1},{2,10},{10,2},{3,11},{11,3},{4,12},{12,4},... | collective-permute-start | bytes 688136 | tf_op jit(solution)/shard_map/ppermute | solution.py:296
  58.1 7.4 %collective-permute-start.6 = (f32[192,64]{1,0:T(8,128)S(1)}, f32[192,64]{1,0:T(8,128)S(1)}, u32[]{:S(2)}, u32[]{:S(2)}) collective-permute-start(f32[192,64]{1,0:T(8,128)S(1)} %get-tuple-element.43), channel_id=1, source_target_pairs={{0,1},{1,2},{2,3},{3,4},{4,5},{5,6},{6,7},{8,9},{9,10},{10,11},{11... | collective-permute-start | bytes 147464 | tf_op jit(solution)/shard_map/ppermute | solution.py:232
  61.5 6.2 %collective-permute-start.7 = (f32[192,64]{1,0:T(8,128)S(1)}, f32[192,64]{1,0:T(8,128)S(1)}, u32[]{:S(2)}, u32[]{:S(2)}) collective-permute-start(f32[192,64]{1,0:T(8,128)S(1)} %get-tuple-element.44), channel_id=1, source_target_pairs={{1,0},{2,1},{3,2},{4,3},{5,4},{6,5},{7,6},{9,8},{10,9},{11,10},{12... | collective-permute-start | bytes 147464 | tf_op jit(solution)/shard_map/ppermute | solution.py:232
  68.7 22.4 %all-to-all-start.2 = ((f32[32,27,128]{2,1,0:T(8,128)}), f32[32,27,128]{2,1,0:T(8,128)S(1)}, u32[]{:S(2)}, u32[]{:S(2)}) async-start(f32[32,27,128]{2,1,0:T(8,128)} %shard_map.66), calls=%async_computation.2 | async-start | bytes 1048576 | tf_op jit(solution)/shard_map/all_to_all | solution.py:236
  77.5 8.6 %collective-permute-start.8 = (f32[64,512]{1,0:T(8,128)S(1)}, f32[64,512]{1,0:T(8,128)S(1)}, u32[]{:S(2)}, u32[]{:S(2)}) collective-permute-start(f32[64,512]{1,0:T(8,128)S(1)} %get-tuple-element.54), channel_id=1, source_target_pairs={{0,8},{8,16},{16,24},{24,32},{32,40},{40,48},{48,56},{1,9},{9,17},... | collective-permute-start | bytes 393224 | tf_op jit(solution)/shard_map/ppermute | solution.py:232
  82.8 7.5 %collective-permute-start.9 = (f32[64,512]{1,0:T(8,128)S(1)}, f32[64,512]{1,0:T(8,128)S(1)}, u32[]{:S(2)}, u32[]{:S(2)}) collective-permute-start(f32[64,512]{1,0:T(8,128)S(1)} %get-tuple-element.55), channel_id=1, source_target_pairs={{8,0},{16,8},{24,16},{32,24},{40,32},{48,40},{56,48},{9,1},{17,9},... | collective-permute-start | bytes 393224 | tf_op jit(solution)/shard_map/ppermute | solution.py:232
  91.1 7.9 %collective-permute-start.10 = (f32[32,27,128]{2,1,0:T(8,128)S(1)}, f32[32,27,128]{2,1,0:T(8,128)S(1)}, u32[]{:S(2)}, u32[]{:S(2)}) collective-permute-start(f32[32,27,128]{2,1,0:T(8,128)S(1)} %all-to-all-done.2.mine), channel_id=1, source_target_pairs={{0,8},{8,0},{1,9},{9,1},{2,10},{10,2},{3,11},{11,3},{4,12},{12,4},... | collective-permute-start | bytes 1327112 | tf_op jit(solution)/shard_map/ppermute | solution.py:330

commit v5 on v4

--- a/solution.py
+++ b/solution.py
@@ -33,15 +33,19 @@
 
 def first_sends(core, v, g, k, first, last, sends, v_own, g_own, k_own, sems):
     rows, c, z = g_own.shape
-    cells, weights = rows * z, k.shape[0]
+    cells = rows * z
+    skip = TAPS // 2 * c
+    held = k.shape[0] - skip
     moves = [
         pltpu.make_async_copy(v, v_own, sems.at[0]),
         pltpu.make_async_copy(g, g_own, sems.at[1]),
-        pltpu.make_async_copy(k, k_own.at[pl.ds(0, weights)], sems.at[2]),
+        pltpu.make_async_copy(
+            k.at[pl.ds(pl.multiple_of(core[0] * skip, c), held)], k_own.at[pl.ds(0, held)], sems.at[2]
+        ),
     ]
     for move in moves:
         move.start()
-    k_own[weights:] = jnp.zeros((k_own.shape[0] - weights, k_own.shape[1]), BF16)
+    k_own[held:] = jnp.zeros((k_own.shape[0] - held, k_own.shape[1]), BF16)
     moves[0].wait()
     first[...] = v_own[0]
     last[...] = v_own[rows - 1]
@@ -49,14 +53,21 @@
     moves[1].wait()
     g_flat = in_row([g_own[r] for r in range(rows)])
     moves[2].wait()
-    turned = k_own[...].astype(F32).T
-    width = sends.shape[2] - 2 * cells
-    later = pltpu.roll(turned, k_own.shape[0] - (weights // c // 2) * c, 1)
-    half = jnp.where(core[0] == 0, turned[:, :width], later[:, :width]).astype(BF16)
-    for to in range(sends.shape[0]):
-        sends[to, :, :cells] = g_flat
-        sends[to, :, cells : 2 * cells] = v_flat
-        sends[to, :, 2 * cells :] = half[to * c : (to + 1) * c]
+    turned = k_own[...].astype(F32).T.astype(BF16)
+    for at, to in enumerate(turn(sends.shape[0])):
+        sends[at, :, :cells] = g_flat
+        sends[at, :, cells : 2 * cells] = v_flat
+        sends[at, :, 2 * cells :] = turned[to * c : (to + 1) * c]
+
+
+def turn(groups):
+    return [(at + 5) % groups for at in range(groups)]
+
+
+def by_chan(received, start, size):
+    order = turn(received.shape[0])
+    blocks = [received[order.index(i)][:, start : start + size] for i in range(len(order))]
+    return jnp.concatenate(blocks, axis=0)
 
 
 def in_row(parts):
@@ -105,7 +116,7 @@
 def weight_terms(core, columns, received, keep, send, k_mine):
     groups, c, _ = received.shape
     cells, total = columns.shape[1], groups * c
-    g_own = received[:, :, :cells].reshape(total, cells)
+    g_own = by_chan(received, 0, cells)
     terms = lax.dot_general(
         columns[...], g_own, (((1,), (1,)), ((), ())), preferred_element_type=F32
     )
@@ -118,7 +129,7 @@
     for piece in range(pieces):
         keep[piece] = kept[piece * rows : (piece + 1) * rows]
         send[piece] = sent[piece * rows : (piece + 1) * rows]
-    k_mine[...] = received[:, :, 2 * cells : 2 * cells + k_mine.shape[1]].reshape(k_mine.shape)
+    k_mine[...] = by_chan(received, 2 * cells, k_mine.shape[1])
 
 
 def spread(z, sign, own, k):
@@ -156,16 +167,14 @@
 
 
 def spread_cotangent(z, received, k, middle, up, down):
-    groups, c, _ = received.shape
     cells = middle.shape[1]
-    own = received[:, :, :cells].reshape(groups * c, cells)
+    own = by_chan(received, 0, cells)
     store_spread(spread(z, -1, own, k), middle, up, down)
 
 
 def spread_volume(z, received, k_out, g_up, g_down, middle, up, down):
-    groups, c, _ = received.shape
     cells = middle.shape[1]
-    own = received[:, :, cells : 2 * cells].reshape(groups * c, cells)
+    own = by_chan(received, cells, cells)
     rows = g_up.shape[0]
     store_spread(spread(z, 1, own, k_out), middle, up.at[pl.ds(rows, rows)], down.at[pl.ds(rows, rows)])
     up[:rows] = g_up[...]
@@ -248,9 +257,9 @@
     k = kernel.reshape(taps * c, total)
     core = lax.axis_index("core").reshape(1).astype(jnp.int32)
     work = 2 * taps * c * total * cells
-    weights = pl.cdiv(taps * c, 128) * 128
     half_taps = (taps - taps // 2) * c
-    width = 2 * cells + pl.cdiv(half_taps, 128) * 128
+    weights = pl.cdiv(half_taps, 128) * 128
+    width = 2 * cells + weights
 
     edge = jax.ShapeDtypeStruct((c, z), BF16)
     first, last, sends = pl.pallas_call(
@@ -271,7 +280,7 @@
         ),
     )(core, v, g, k)
     before, after = neighbours(last, first, "sy")
-    received = exchange(sends, "chan")
+    received = lax.all_to_all(sends, "chan", 0, 0, axis_index_groups=[turn(groups)], tiled=True)
     (v_ring,) = call(volume_ring, [((c, lanes), BF16)], 0, v, before, after)
     v_below, v_above = neighbours(v_ring, v_ring, PLANE)
 

time: 101 us -> 96.6 us (0.956)
  waiting for transfers between devices: 25.5 us -> 18.4 us
  starting transfers between devices: 64.3 us -> 67.6 us
    all_to_all x0 -> x1, starting transfers between devices: none -> 13.2 us  [body(): lax.all_to_all(sends, 'chan', 0, 0, axis_index_groups=[turn(groups)], til...]
    all_to_all x3 -> x2, starting transfers between devices: 29.5 us -> 18.5 us  [exchange(): return lax.all_to_all(value, axis, 0, 0, tiled=True)]
    all_to_all x3 -> x2, waiting for transfers between devices: 7.11 us -> 0.01 us  [exchange(): return lax.all_to_all(value, axis, 0, 0, tiled=True)]
  transfers between devices with their start and end apart: 14 -> 14, of which waited for: 10 -> 9; matrix products, arithmetic and copies ran while one was open for 0% -> 0% of each run, Pallas kernels for 4% -> 4%
where the time goes in v5:
time: 96.6 us; the launch traced here: 95.9 us
  starting transfers between devices  67.6 us (70%)
  waiting for transfers between devices  18.4 us (19%)
  Pallas kernels  9.03 us (9%)
    all_to_all x2, starting transfers between devices, exchange(): return lax.all_to_all(value, axis, 0, 0, tiled=True)  18.5 us
    ppermute x4, starting transfers between devices, neighbours(): lax.ppermute(value_up, axis, up)  14.9 us
    all_to_all x1, starting transfers between devices, body(): lax.all_to_all(sends, 'chan', 0, 0, axis_index_groups=[turn(groups)], til...  13.2 us
    ppermute x4, waiting for transfers between devices, neighbours(): lax.ppermute(value_down, axis, down)  9.77 us
    ppermute x4, starting transfers between devices, neighbours(): lax.ppermute(value_down, axis, down)  8.7 us
    pallas_call x11, Pallas kernels, call(): pl.pallas_call(kernel, out_shape=[jax.ShapeDtypeStruct(s, d) for s, d in...  6.98 us
    ppermute x1, starting transfers between devices, body(): other = lax.ppermute(mine, 'core', swap)  6.38 us
    ppermute x4, waiting for transfers between devices, neighbours(): lax.ppermute(value_up, axis, up)  5.23 us
  transfers between devices with their start and end apart: 14, of which 9 were waited for; matrix products, arithmetic and copies ran while one was open for 0% of the time, Pallas kernels for 4%

profile of v5, /device:TPU:1, one launch (start us, length us, event | category | flops | bytes accessed | tf_op | source)
XLA Modules:
  0.0 95.9 jit_solution(9983901244492857125)
XLA Ops:
  0.6 2.1 %shard_map.58 = (bf16[32,64]{1,0:T(8,128)(2,1)}, bf16[32,64]{1,0:T(8,128)(2,1)}, bf16[8,32,1536]{2,1,0:T(8,128)(2,1)}) custom-call(s32[1]{0:T(128)} %bitcast.core, bf16[8,32,64]{2,1,0:T(8,128)(2,1)} %bitcast.17, bf16[8,32,64]{2,1,0:T(8,128)(2,1)} %bitcast.20, bf16[864,256]{1,0:T(8,128)(2,1)} %bitcast.15), custom_call_target="tpu_custom_call" | custom-call | bytes 1572864 | tf_op jit(solution)/shard_map/pallas_call | solution.py:265
  2.7 13.2 %all-to-all-start = ((bf16[8,32,1536]{2,1,0:T(8,128)(2,1)}), bf16[8,32,1536]{2,1,0:T(8,128)(2,1)S(1)}, u32[]{:S(2)}, u32[]{:S(2)}) async-start(bf16[8,32,1536]{2,1,0:T(8,128)(2,1)} %get-tuple-element.34), calls=%async_computation | async-start | bytes 1572864 | tf_op jit(solution)/shard_map/all_to_all | solution.py:283
  15.9 3.2 %collective-permute-start = (bf16[32,64]{1,0:T(8,128)(2,1)S(1)}, bf16[32,64]{1,0:T(8,128)(2,1)S(1)}, u32[]{:S(2)}, u32[]{:S(2)}) collective-permute-start(bf16[32,64]{1,0:T(8,128)(2,1)S(1)} %copy-done.3), channel_id=1, source_target_pairs={{0,1},{1,2},{2,3},{3,4},{4,5},{5,6},{6,7},{8,9},{9,10},{10,11},{11... | collective-permute-start | bytes 12296 | tf_op jit(solution)/shard_map/ppermute | solution.py:241
  19.1 1.3 %collective-permute-start.1 = (bf16[32,64]{1,0:T(8,128)(2,1)S(1)}, bf16[32,64]{1,0:T(8,128)(2,1)S(1)}, u32[]{:S(2)}, u32[]{:S(2)}) collective-permute-start(bf16[32,64]{1,0:T(8,128)(2,1)S(1)} %copy-done.2), channel_id=1, source_target_pairs={{1,0},{2,1},{3,2},{4,3},{5,4},{6,5},{7,6},{9,8},{10,9},{11,10},{12... | collective-permute-start | bytes 12296 | tf_op jit(solution)/shard_map/ppermute | solution.py:241
  20.4 3.4 %collective-permute-done.1.after = bf16[32,64]{1,0:T(8,128)(2,1)S(1)} collective-permute-done((bf16[32,64]{1,0:T(8,128)(2,1)S(1)}, bf16[32,64]{1,0:T(8,128)(2,1)S(1)}, u32[]{:S(2)}, u32[]{:S(2)}) %collective-permute-start.1) | collective-permute-done | bytes 4128 | tf_op jit(solution)/shard_map/ppermute | solution.py:241
  23.9 4.2 %collective-permute-start.3 = (bf16[32,640]{1,0:T(8,128)(2,1)S(1)}, bf16[32,640]{1,0:T(8,128)(2,1)S(1)}, u32[]{:S(2)}, u32[]{:S(2)}) collective-permute-start(bf16[32,640]{1,0:T(8,128)(2,1)S(1)} %shard_map.59.refs_1_), channel_id=1, source_target_pairs={{8,0},{16,8},{24,16},{32,24},{40,32},{48,40},{56,48},{9,1},{17,9},... | collective-permute-start | bytes 122888 | tf_op jit(solution)/shard_map/ppermute | solution.py:241
  28.1 3.0 %collective-permute-start.2 = (bf16[32,640]{1,0:T(8,128)(2,1)S(1)}, bf16[32,640]{1,0:T(8,128)(2,1)S(1)}, u32[]{:S(2)}, u32[]{:S(2)}) collective-permute-start(bf16[32,640]{1,0:T(8,128)(2,1)S(1)} %shard_map.59.refs_1_), channel_id=1, source_target_pairs={{0,8},{8,16},{16,24},{24,32},{32,40},{40,48},{48,56},{1,9},{9,17},... | collective-permute-start | bytes 122888 | tf_op jit(solution)/shard_map/ppermute | solution.py:241
  31.2 1.0 %collective-permute-done.2.refs_0_ = bf16[32,640]{1,0:T(8,128)(2,1)S(1)} collective-permute-done((bf16[32,640]{1,0:T(8,128)(2,1)S(1)}, bf16[32,640]{1,0:T(8,128)(2,1)S(1)}, u32[]{:S(2)}, u32[]{:S(2)}) %collective-permute-start.2) | collective-permute-done | bytes 40992 | tf_op jit(solution)/shard_map/ppermute | solution.py:241
  32.6 0.4 shard_map.61
  33.0 3.3 %collective-permute-start.4 = (f32[32,27,128]{2,1,0:T(8,128)S(1)}, f32[32,27,128]{2,1,0:T(8,128)S(1)}, u32[]{:S(2)}, u32[]{:S(2)}) collective-permute-start(f32[32,27,128]{2,1,0:T(8,128)S(1)} %get-tuple-element.36), channel_id=1, source_target_pairs={{0,8},{8,0},{1,9},{9,1},{2,10},{10,2},{3,11},{11,3},{4,12},{12,4},... | collective-permute-start | bytes 1327112 | tf_op jit(solution)/shard_map/ppermute | solution.py:301
  36.3 1.5 %collective-permute-done.4.other = f32[32,27,128]{2,1,0:T(8,128)S(1)} collective-permute-done((f32[32,27,128]{2,1,0:T(8,128)S(1)}, f32[32,27,128]{2,1,0:T(8,128)S(1)}, u32[]{:S(2)}, u32[]{:S(2)}) %collective-permute-start.4) | collective-permute-done | bytes 442400 | tf_op jit(solution)/shard_map/ppermute | solution.py:301
  37.9 0.8 shard_map.62
  38.7 9.8 %all-to-all-start.1 = ((f32[32,27,128]{2,1,0:T(8,128)}), f32[32,27,128]{2,1,0:T(8,128)S(1)}, u32[]{:S(2)}, u32[]{:S(2)}) async-start(f32[32,27,128]{2,1,0:T(8,128)} %shard_map.62), calls=%async_computation.1 | async-start | bytes 1048576 | tf_op jit(solution)/shard_map/all_to_all | solution.py:245
  48.5 2.6 %collective-permute-start.5 = (bf16[256,448]{1,0:T(8,128)(2,1)S(1)}, bf16[256,448]{1,0:T(8,128)(2,1)S(1)}, u32[]{:S(2)}, u32[]{:S(2)}) collective-permute-start(bf16[256,448]{1,0:T(8,128)(2,1)S(1)} %get-tuple-element.40.mine), channel_id=1, source_target_pairs={{0,8},{8,0},{1,9},{9,1},{2,10},{10,2},{3,11},{11,3},{4,12},{12,4},... | collective-permute-start | bytes 688136 | tf_op jit(solution)/shard_map/ppermute | solution.py:305
  51.1 0.8 shard_map.64
  51.9 0.4 collective-permute-done.5.other
  52.2 1.0 %shard_map.63.refs_1_ = bf16[864,256]{1,0:T(8,128)(2,1)S(1)} custom-call(s32[1]{0:T(128)} %bitcast.core, bf16[256,448]{1,0:T(8,128)(2,1)S(1)} %get-tuple-element.40.mine, bf16[256,448]{1,0:T(8,128)(2,1)S(1)} %collective-permute-done.5.other), custom_call_target="tpu_custom_call" | custom-call | bytes 901124 | tf_op jit(solution)/shard_map/pallas_call | solution.py:24
  53.3 0.8 shard_map.65
  54.0 3.4 %collective-permute-start.6 = (f32[192,64]{1,0:T(8,128)S(1)}, f32[192,64]{1,0:T(8,128)S(1)}, u32[]{:S(2)}, u32[]{:S(2)}) collective-permute-start(f32[192,64]{1,0:T(8,128)S(1)} %get-tuple-element.43), channel_id=1, source_target_pairs={{0,1},{1,2},{2,3},{3,4},{4,5},{5,6},{6,7},{8,9},{9,10},{10,11},{11... | collective-permute-start | bytes 147464 | tf_op jit(solution)/shard_map/ppermute | solution.py:241
  57.5 1.3 %collective-permute-start.7 = (f32[192,64]{1,0:T(8,128)S(1)}, f32[192,64]{1,0:T(8,128)S(1)}, u32[]{:S(2)}, u32[]{:S(2)}) collective-permute-start(f32[192,64]{1,0:T(8,128)S(1)} %get-tuple-element.44), channel_id=1, source_target_pairs={{1,0},{2,1},{3,2},{4,3},{5,4},{6,5},{7,6},{9,8},{10,9},{11,10},{12... | collective-permute-start | bytes 147464 | tf_op jit(solution)/shard_map/ppermute | solution.py:241
  58.8 2.7 %collective-permute-done.6.before = f32[192,64]{1,0:T(8,128)S(1)} collective-permute-done((f32[192,64]{1,0:T(8,128)S(1)}, f32[192,64]{1,0:T(8,128)S(1)}, u32[]{:S(2)}, u32[]{:S(2)}) %collective-permute-start.6) | collective-permute-done | bytes 49184 | tf_op jit(solution)/shard_map/ppermute | solution.py:241
  61.5 2.2 %collective-permute-done.7.after = f32[192,64]{1,0:T(8,128)S(1)} collective-permute-done((f32[192,64]{1,0:T(8,128)S(1)}, f32[192,64]{1,0:T(8,128)S(1)}, u32[]{:S(2)}, u32[]{:S(2)}) %collective-permute-start.7) | collective-permute-done | bytes 49184 | tf_op jit(solution)/shard_map/ppermute | solution.py:241
  63.7 0.9 shard_map.66
  64.6 8.7 %all-to-all-start.2 = ((f32[32,27,128]{2,1,0:T(8,128)}), f32[32,27,128]{2,1,0:T(8,128)S(1)}, u32[]{:S(2)}, u32[]{:S(2)}) async-start(f32[32,27,128]{2,1,0:T(8,128)} %shard_map.66), calls=%async_computation.2 | async-start | bytes 1048576 | tf_op jit(solution)/shard_map/all_to_all | solution.py:245
  73.4 5.3 %collective-permute-start.8 = (f32[64,512]{1,0:T(8,128)S(1)}, f32[64,512]{1,0:T(8,128)S(1)}, u32[]{:S(2)}, u32[]{:S(2)}) collective-permute-start(f32[64,512]{1,0:T(8,128)S(1)} %get-tuple-element.54), channel_id=1, source_target_pairs={{0,8},{8,16},{16,24},{24,32},{32,40},{40,48},{48,56},{1,9},{9,17},... | collective-permute-start | bytes 393224 | tf_op jit(solution)/shard_map/ppermute | solution.py:241
  78.7 1.9 %collective-permute-start.9 = (f32[64,512]{1,0:T(8,128)S(1)}, f32[64,512]{1,0:T(8,128)S(1)}, u32[]{:S(2)}, u32[]{:S(2)}) collective-permute-start(f32[64,512]{1,0:T(8,128)S(1)} %get-tuple-element.55), channel_id=1, source_target_pairs={{8,0},{16,8},{24,16},{32,24},{40,32},{48,40},{56,48},{9,1},{17,9},... | collective-permute-start | bytes 393224 | tf_op jit(solution)/shard_map/ppermute | solution.py:241
  80.6 1.5 %collective-permute-done.8.below = f32[64,512]{1,0:T(8,128)S(1)} collective-permute-done((f32[64,512]{1,0:T(8,128)S(1)}, f32[64,512]{1,0:T(8,128)S(1)}, u32[]{:S(2)}, u32[]{:S(2)}) %collective-permute-start.8) | collective-permute-done | bytes 131104 | tf_op jit(solution)/shard_map/ppermute | solution.py:241
  82.1 4.1 %collective-permute-done.9.above = f32[64,512]{1,0:T(8,128)S(1)} collective-permute-done((f32[64,512]{1,0:T(8,128)S(1)}, f32[64,512]{1,0:T(8,128)S(1)}, u32[]{:S(2)}, u32[]{:S(2)}) %collective-permute-start.9) | collective-permute-done | bytes 131104 | tf_op jit(solution)/shard_map/ppermute | solution.py:241
  86.2 0.7 shard_map.68
  87.0 6.4 %collective-permute-start.10 = (f32[32,27,128]{2,1,0:T(8,128)S(1)}, f32[32,27,128]{2,1,0:T(8,128)S(1)}, u32[]{:S(2)}, u32[]{:S(2)}) collective-permute-start(f32[32,27,128]{2,1,0:T(8,128)S(1)} %all-to-all-done.2.mine), channel_id=1, source_target_pairs={{0,8},{8,0},{1,9},{9,1},{2,10},{10,2},{3,11},{11,3},{4,12},{12,4},... | collective-permute-start | bytes 1327112 | tf_op jit(solution)/shard_map/ppermute | solution.py:339
  93.4 1.5 %collective-permute-done.10.other = f32[32,27,128]{2,1,0:T(8,128)S(1)} collective-permute-done((f32[32,27,128]{2,1,0:T(8,128)S(1)}, f32[32,27,128]{2,1,0:T(8,128)S(1)}, u32[]{:S(2)}, u32[]{:S(2)}) %collective-permute-start.10) | collective-permute-done | bytes 442400 | tf_op jit(solution)/shard_map/ppermute | solution.py:339
  94.9 1.0 %shard_map.69 = f32[864,256]{1,0:T(8,128)} custom-call(s32[1]{0:T(128)} %bitcast.core, f32[32,27,128]{2,1,0:T(8,128)S(1)} %all-to-all-done.2.mine, f32[32,27,128]{2,1,0:T(8,128)S(1)} %collective-permute-done.10.other), custom_call_target="tpu_custom_call" | custom-call | bytes 1769476 | tf_op jit(solution)/shard_map/pallas_call | solution.py:24
  (16 shorter events, 0.6 us)
Async XLA Ops:
  2.7 13.2 %copy-start.3 = (bf16[32,64]{1,0:T(8,128)(2,1)S(1)}, bf16[32,64]{1,0:T(8,128)(2,1)}, u32[]{:S(2)}) copy-start(bf16[32,64]{1,0:T(8,128)(2,1)} %get-tuple-element.32) | copy-start | bytes 12292
  2.7 16.4 %copy-start.2 = (bf16[32,64]{1,0:T(8,128)(2,1)S(1)}, bf16[32,64]{1,0:T(8,128)(2,1)}, u32[]{:S(2)}) copy-start(bf16[32,64]{1,0:T(8,128)(2,1)} %get-tuple-element.33) | copy-start | bytes 12292
  2.7 21.1 %copy-start.1 = (bf16[1,8,64,32]{2,3,1,0:T(8,128)(2,1)S(1)}, bf16[1,8,64,32]{2,3,1,0:T(8,128)(2,1)}, u32[]{:S(2)}) copy-start(bf16[1,8,64,32]{2,3,1,0:T(8,128)(2,1)} %param.3) | copy-start | bytes 98308
  2.7 29.8 %all-to-all-start = ((bf16[8,32,1536]{2,1,0:T(8,128)(2,1)}), bf16[8,32,1536]{2,1,0:T(8,128)(2,1)S(1)}, u32[]{:S(2)}, u32[]{:S(2)}) async-start(bf16[8,32,1536]{2,1,0:T(8,128)(2,1)} %get-tuple-element.34), calls=%async_computation | async-start | bytes 1572864 | tf_op jit(solution)/shard_map/all_to_all | solution.py:283
  15.9 4.5 %collective-permute-start = (bf16[32,64]{1,0:T(8,128)(2,1)S(1)}, bf16[32,64]{1,0:T(8,128)(2,1)S(1)}, u32[]{:S(2)}, u32[]{:S(2)}) collective-permute-start(bf16[32,64]{1,0:T(8,128)(2,1)S(1)} %copy-done.3), channel_id=1, source_target_pairs={{0,1},{1,2},{2,3},{3,4},{4,5},{5,6},{6,7},{8,9},{9,10},{10,11},{11... | collective-permute-start | bytes 12296 | tf_op jit(solution)/shard_map/ppermute | solution.py:241
  19.1 4.7 %collective-permute-start.1 = (bf16[32,64]{1,0:T(8,128)(2,1)S(1)}, bf16[32,64]{1,0:T(8,128)(2,1)S(1)}, u32[]{:S(2)}, u32[]{:S(2)}) collective-permute-start(bf16[32,64]{1,0:T(8,128)(2,1)S(1)} %copy-done.2), channel_id=1, source_target_pairs={{1,0},{2,1},{3,2},{4,3},{5,4},{6,5},{7,6},{9,8},{10,9},{11,10},{12... | collective-permute-start | bytes 12296 | tf_op jit(solution)/shard_map/ppermute | solution.py:241
  23.9 7.3 %collective-permute-start.3 = (bf16[32,640]{1,0:T(8,128)(2,1)S(1)}, bf16[32,640]{1,0:T(8,128)(2,1)S(1)}, u32[]{:S(2)}, u32[]{:S(2)}) collective-permute-start(bf16[32,640]{1,0:T(8,128)(2,1)S(1)} %shard_map.59.refs_1_), channel_id=1, source_target_pairs={{8,0},{16,8},{24,16},{32,24},{40,32},{48,40},{56,48},{9,1},{17,9},... | collective-permute-start | bytes 122888 | tf_op jit(solution)/shard_map/ppermute | solution.py:241
  28.1 4.1 %collective-permute-start.2 = (bf16[32,640]{1,0:T(8,128)(2,1)S(1)}, bf16[32,640]{1,0:T(8,128)(2,1)S(1)}, u32[]{:S(2)}, u32[]{:S(2)}) collective-permute-start(bf16[32,640]{1,0:T(8,128)(2,1)S(1)} %shard_map.59.refs_1_), channel_id=1, source_target_pairs={{0,8},{8,16},{16,24},{24,32},{32,40},{40,48},{48,56},{1,9},{9,17},... | collective-permute-start | bytes 122888 | tf_op jit(solution)/shard_map/ppermute | solution.py:241
  33.0 4.9 %collective-permute-start.4 = (f32[32,27,128]{2,1,0:T(8,128)S(1)}, f32[32,27,128]{2,1,0:T(8,128)S(1)}, u32[]{:S(2)}, u32[]{:S(2)}) collective-permute-start(f32[32,27,128]{2,1,0:T(8,128)S(1)} %get-tuple-element.36), channel_id=1, source_target_pairs={{0,8},{8,0},{1,9},{9,1},{2,10},{10,2},{3,11},{11,3},{4,12},{12,4},... | collective-permute-start | bytes 1327112 | tf_op jit(solution)/shard_map/ppermute | solution.py:301
  38.7 12.4 %copy-start = (bf16[27,32,256]{2,1,0:T(8,128)(2,1)S(1)}, bf16[27,32,256]{2,1,0:T(8,128)(2,1)}, u32[]{:S(2)}) copy-start(bf16[27,32,256]{2,1,0:T(8,128)(2,1)} %param.4) | copy-start | bytes 1327108
  38.7 25.0 %all-to-all-start.1 = ((f32[32,27,128]{2,1,0:T(8,128)}), f32[32,27,128]{2,1,0:T(8,128)S(1)}, u32[]{:S(2)}, u32[]{:S(2)}) async-start(f32[32,27,128]{2,1,0:T(8,128)} %shard_map.62), calls=%async_computation.1 | async-start | bytes 1048576 | tf_op jit(solution)/shard_map/all_to_all | solution.py:245
  48.5 3.7 %collective-permute-start.5 = (bf16[256,448]{1,0:T(8,128)(2,1)S(1)}, bf16[256,448]{1,0:T(8,128)(2,1)S(1)}, u32[]{:S(2)}, u32[]{:S(2)}) collective-permute-start(bf16[256,448]{1,0:T(8,128)(2,1)S(1)} %get-tuple-element.40.mine), channel_id=1, source_target_pairs={{0,8},{8,0},{1,9},{9,1},{2,10},{10,2},{3,11},{11,3},{4,12},{12,4},... | collective-permute-start | bytes 688136 | tf_op jit(solution)/shard_map/ppermute | solution.py:305
  54.0 7.4 %collective-permute-start.6 = (f32[192,64]{1,0:T(8,128)S(1)}, f32[192,64]{1,0:T(8,128)S(1)}, u32[]{:S(2)}, u32[]{:S(2)}) collective-permute-start(f32[192,64]{1,0:T(8,128)S(1)} %get-tuple-element.43), channel_id=1, source_target_pairs={{0,1},{1,2},{2,3},{3,4},{4,5},{5,6},{6,7},{8,9},{9,10},{10,11},{11... | collective-permute-start | bytes 147464 | tf_op jit(solution)/shard_map/ppermute | solution.py:241
  57.5 6.2 %collective-permute-start.7 = (f32[192,64]{1,0:T(8,128)S(1)}, f32[192,64]{1,0:T(8,128)S(1)}, u32[]{:S(2)}, u32[]{:S(2)}) collective-permute-start(f32[192,64]{1,0:T(8,128)S(1)} %get-tuple-element.44), channel_id=1, source_target_pairs={{1,0},{2,1},{3,2},{4,3},{5,4},{6,5},{7,6},{9,8},{10,9},{11,10},{12... | collective-permute-start | bytes 147464 | tf_op jit(solution)/shard_map/ppermute | solution.py:241
  64.6 22.4 %all-to-all-start.2 = ((f32[32,27,128]{2,1,0:T(8,128)}), f32[32,27,128]{2,1,0:T(8,128)S(1)}, u32[]{:S(2)}, u32[]{:S(2)}) async-start(f32[32,27,128]{2,1,0:T(8,128)} %shard_map.66), calls=%async_computation.2 | async-start | bytes 1048576 | tf_op jit(solution)/shard_map/all_to_all | solution.py:245
  73.4 8.7 %collective-permute-start.8 = (f32[64,512]{1,0:T(8,128)S(1)}, f32[64,512]{1,0:T(8,128)S(1)}, u32[]{:S(2)}, u32[]{:S(2)}) collective-permute-start(f32[64,512]{1,0:T(8,128)S(1)} %get-tuple-element.54), channel_id=1, source_target_pairs={{0,8},{8,16},{16,24},{24,32},{32,40},{40,48},{48,56},{1,9},{9,17},... | collective-permute-start | bytes 393224 | tf_op jit(solution)/shard_map/ppermute | solution.py:241
  78.7 7.5 %collective-permute-start.9 = (f32[64,512]{1,0:T(8,128)S(1)}, f32[64,512]{1,0:T(8,128)S(1)}, u32[]{:S(2)}, u32[]{:S(2)}) collective-permute-start(f32[64,512]{1,0:T(8,128)S(1)} %get-tuple-element.55), channel_id=1, source_target_pairs={{8,0},{16,8},{24,16},{32,24},{40,32},{48,40},{56,48},{9,1},{17,9},... | collective-permute-start | bytes 393224 | tf_op jit(solution)/shard_map/ppermute | solution.py:241
  87.0 7.9 %collective-permute-start.10 = (f32[32,27,128]{2,1,0:T(8,128)S(1)}, f32[32,27,128]{2,1,0:T(8,128)S(1)}, u32[]{:S(2)}, u32[]{:S(2)}) collective-permute-start(f32[32,27,128]{2,1,0:T(8,128)S(1)} %all-to-all-done.2.mine), channel_id=1, source_target_pairs={{0,8},{8,0},{1,9},{9,1},{2,10},{10,2},{3,11},{11,3},{4,12},{12,4},... | collective-permute-start | bytes 1327112 | tf_op jit(solution)/shard_map/ppermute | solution.py:339

commit v6 on v5

--- a/solution.py
+++ b/solution.py
@@ -123,12 +123,8 @@
     half = total // 2
     low, high = terms[:, :half], terms[:, half:]
     is_low = core[0] == 0
-    kept = jnp.where(is_low, low, high)
-    sent = jnp.where(is_low, high, low)
-    pieces, rows = keep.shape[0], keep.shape[1]
-    for piece in range(pieces):
-        keep[piece] = kept[piece * rows : (piece + 1) * rows]
-        send[piece] = sent[piece * rows : (piece + 1) * rows]
+    keep[...] = jnp.where(is_low, low, high)
+    send[...] = jnp.where(is_low, high, low)
     k_mine[...] = by_chan(received, 2 * cells, k_mine.shape[1])
 
 
@@ -155,46 +151,51 @@
     return result
 
 
-def store_spread(planes, middle, up, down):
+def store_spread(planes, middle):
     c, cells = middle.shape[0] // 3, middle.shape[1]
-    z = up.shape[1]
     for i, plane in enumerate(planes):
-        at = slice(i * c, (i + 1) * c)
-        middle[at] = plane[:, :cells]
-        ends = plane[:, cells:]
-        up[at] = ends[:, :z]
-        down[at] = pltpu.roll(ends, z, 1)[:, :z]
-
-
-def spread_cotangent(z, received, k, middle, up, down):
-    cells = middle.shape[1]
-    own = by_chan(received, 0, cells)
-    store_spread(spread(z, -1, own, k), middle, up, down)
-
-
-def spread_volume(z, received, k_out, g_up, g_down, middle, up, down):
+        middle[i * c : (i + 1) * c] = plane[:, :cells]
+    ends = jnp.concatenate([plane[:, cells:] for plane in planes], axis=0)
+    z = ends.shape[1] // 2
+    return ends, pltpu.roll(ends, z, 1)
+
+
+def is_low_half(shape):
+    return lax.broadcasted_iota(jnp.int32, shape, 1) < shape[1] // 2
+
+
+def spread_cotangent(z, received, k, middle, ends):
+    own = by_chan(received, 0, middle.shape[1])
+    ends[...], _ = store_spread(spread(z, -1, own, k), middle)
+
+
+def spread_volume(z, received, k_out, g_ends, middle, up, down):
     cells = middle.shape[1]
     own = by_chan(received, cells, cells)
-    rows = g_up.shape[0]
-    store_spread(spread(z, 1, own, k_out), middle, up.at[pl.ds(rows, rows)], down.at[pl.ds(rows, rows)])
-    up[:rows] = g_up[...]
-    down[:rows] = g_down[...]
+    ends, turned = store_spread(spread(z, 1, own, k_out), middle)
+    low = is_low_half(ends.shape)
+    up[...] = jnp.where(low, g_ends[...], turned)
+    down[...] = jnp.where(low, pltpu.roll(g_ends[...], z, 1), ends)
 
 
 def add_ends(g_middle, v_middle, before, after, own, to_below, to_above):
     rows, cells = g_middle.shape
-    z, c = before.shape[1], rows // 3
-    first = jnp.concatenate([before[...], jnp.zeros((2 * rows, z), F32)], axis=1)
-    last = jnp.concatenate([jnp.zeros((2 * rows, z), F32), after[...]], axis=1)
-    for i, middle in enumerate((g_middle, v_middle)):
+    width = before.shape[1]
+    c = rows // 3
+    low = is_low_half(before.shape)
+    g_first, v_last = before[...], after[...]
+    v_first, g_last = pltpu.roll(g_first, width // 2, 1), pltpu.roll(v_last, width // 2, 1)
+    for i, (middle, first, last) in enumerate(
+        ((g_middle, g_first, g_last), (v_middle, v_first, v_last))
+    ):
+        first = jnp.where(low, first, 0.0)
+        last = jnp.where(low, 0.0, last)
         for part, out in enumerate((to_below, own, to_above)):
             at = slice(part * c, (part + 1) * c)
-            from_end = slice(i * rows + part * c, i * rows + (part + 1) * c)
-            value = middle[at]
             to = slice(i * c, (i + 1) * c)
-            out[to] = value
-            out[to, : 2 * z] = value[:, : 2 * z] + first[from_end]
-            out[to, cells - 2 * z :] = value[:, cells - 2 * z :] + last[from_end]
+            out[to] = middle[at]
+            out[to, :width] = middle[at, :width] + first[at]
+            out[to, cells - width :] = middle[at, cells - width :] + last[at]
 
 
 def add_planes(own, below, above, out, grad_input):
@@ -216,22 +217,21 @@
     out[...] = keep[...] + other[...]
 
 
-def sum_pieces(scale, parts, out):
-    total = parts[0]
-    for part in range(1, parts.shape[0]):
-        total += parts[part]
+def sum_pieces(scale, pieces, parts, out):
+    rows = parts.shape[0] // pieces
+    total = parts[:rows]
+    for at in range(rows, rows * pieces, rows):
+        total += parts[at : at + rows]
     total = total / scale
-    for copy in range(out.shape[0]):
-        out[copy] = total
+    for at in range(0, rows * pieces, rows):
+        out[at : at + rows] = total
 
 
 def join_halves(core, mine, other, out):
-    pieces, rows, half = mine.shape
-    first = core[0] == 0
-    for piece in range(pieces):
-        a, b = mine[piece], other[piece]
-        out[piece * rows : (piece + 1) * rows, :half] = jnp.where(first, a, b)
-        out[piece * rows : (piece + 1) * rows, half:] = jnp.where(first, b, a)
+    half = mine.shape[1]
+    is_low = core[0] == 0
+    out[:, :half] = jnp.where(is_low, mine[...], other[...])
+    out[:, half:] = jnp.where(is_low, other[...], mine[...])
 
 
 def neighbours(value_up, value_down, axis):
@@ -241,8 +241,9 @@
     return lax.ppermute(value_up, axis, up), lax.ppermute(value_down, axis, down)
 
 
-def exchange(value, axis):
-    return lax.all_to_all(value, axis, 0, 0, tiled=True)
+def exchange_rows(value, axis):
+    apart = value.reshape(value.shape[0], 1, value.shape[1])
+    return lax.all_to_all(apart, axis, 0, 0, tiled=True).reshape(value.shape)
 
 
 def body(volume, kernel, grad_out):
@@ -288,7 +289,7 @@
         windows(z, *refs)
 
     (columns,) = call(around, [((taps * c, cells), BF16)], 0, v_below, v_ring, v_above)
-    piece = (pieces, taps * c // pieces, total // 2)
+    piece = (taps * c, total // 2)
     keep, send, k_mine = call(
         weight_terms,
         [(piece, F32), (piece, F32), ((total, half_taps), BF16)],
@@ -301,9 +302,9 @@
     (halves,) = call(add_halves, [(piece, F32)], 0, keep, lax.ppermute(send, "core", swap))
 
     halves, k_mine, received = lax.optimization_barrier((halves, k_mine, received))
-    parts = exchange(halves, ("x", "sy"))
+    parts = exchange_rows(halves, ("x", "sy"))
     k_other = lax.ppermute(k_mine, "core", swap)
-    middle, ends = ((3 * c, cells), F32), ((3 * c, z), F32)
+    middle, ends = ((3 * c, cells), F32), ((3 * c, 2 * z), F32)
 
     def from_cotangent(*refs):
         spread_cotangent(z, *refs)
@@ -311,31 +312,28 @@
     def from_volume(*refs):
         spread_volume(z, *refs)
 
-    g_middle, g_up, g_down = call(from_cotangent, [middle, ends, ends], work, received, k)
-    (k_out,) = call(
-        weights_by_output, [((taps * c, total), BF16)], 0, core, k_mine, k_other
-    )
-    both_ends = ((6 * c, z), F32)
+    g_middle, g_ends = call(from_cotangent, [middle, ends], work, received, k)
+    (k_out,) = call(weights_by_output, [((taps * c, total), BF16)], 0, core, k_mine, k_other)
     v_middle, up, down = call(
-        from_volume, [middle, both_ends, both_ends], work, received, k_out, g_up, g_down
+        from_volume, [middle, ends, ends], work, received, k_out, g_ends
     )
     before, after = neighbours(up, down, "sy")
     parts, before, after = lax.optimization_barrier((parts, before, after))
     scale = math.sqrt(cells * devices)
 
     def reduce_pieces(*refs):
-        sum_pieces(scale, *refs)
+        sum_pieces(scale, pieces, *refs)
 
     (copies,) = call(reduce_pieces, [(piece, F32)], 0, parts)
     copies, before, after = lax.optimization_barrier((copies, before, after))
-    mine = exchange(copies, ("x", "sy"))
+    mine = exchange_rows(copies, ("x", "sy"))
     own, to_below, to_above = call(
         add_ends, [((2 * c, cells), F32)] * 3, 0, g_middle, v_middle, before, after
     )
     below, above = neighbours(to_above, to_below, PLANE)
     result = ((rows, c, z), BF16)
+    mine, below, above = lax.optimization_barrier((mine, below, above))
     out, grad_input = call(add_planes, [result, result], 0, own, below, above)
-    mine, out, grad_input = lax.optimization_barrier((mine, out, grad_input))
     other = lax.ppermute(mine, "core", swap)
     (grad_kernel,) = call(join_halves, [((taps * c, total), F32)], 0, core, mine, other)
     return (

time: 96.6 us -> 93.8 us (0.971)
  waiting for transfers between devices: 18.4 us -> 16 us
    ppermute x4, waiting for transfers between devices: 5.23 us -> 2.27 us  [neighbours(): lax.ppermute(value_up, axis, up)]
    ppermute x4, waiting for transfers between devices: 9.77 us -> 11.2 us  [neighbours(): lax.ppermute(value_down, axis, down)]
  transfers between devices with their start and end apart: 14 -> 14, of which waited for: 9 -> 8; matrix products, arithmetic and copies ran while one was open for 0% -> 0% of each run, Pallas kernels for 4% -> 4%
where the time goes in v6:
time: 93.8 us; the launch traced here: 93 us
  starting transfers between devices  67.2 us (72%)
  waiting for transfers between devices  16 us (17%)
  Pallas kernels  8.84 us (9%)
    all_to_all x2, starting transfers between devices, exchange_rows(): return lax.all_to_all(apart, axis, 0, 0, tiled=True).reshape(value.shape)  19 us
    ppermute x4, starting transfers between devices, neighbours(): lax.ppermute(value_up, axis, up)  15 us
    all_to_all x1, starting transfers between devices, body(): lax.all_to_all(sends, 'chan', 0, 0, axis_index_groups=[turn(groups)], til...  13.2 us
    ppermute x4, waiting for transfers between devices, neighbours(): lax.ppermute(value_down, axis, down)  11.2 us
    ppermute x4, starting transfers between devices, neighbours(): lax.ppermute(value_down, axis, down)  8.7 us
    pallas_call x11, Pallas kernels, call(): pl.pallas_call(kernel, out_shape=[jax.ShapeDtypeStruct(s, d) for s, d in...  6.78 us
    ppermute x1, starting transfers between devices, body(): other = lax.ppermute(mine, 'core', swap)  5.47 us
    ppermute x1, starting transfers between devices, body(): lax.ppermute(send, 'core', swap)  3.34 us
  transfers between devices with their start and end apart: 14, of which 8 were waited for; matrix products, arithmetic and copies ran while one was open for 0% of the time, Pallas kernels for 4%

profile of v6, /device:TPU:1, one launch (start us, length us, event | category | flops | bytes accessed | tf_op | source)
XLA Modules:
  0.0 93.0 jit_solution(5721721276354448232)
XLA Ops:
  0.6 2.1 %shard_map.58 = (bf16[32,64]{1,0:T(8,128)(2,1)}, bf16[32,64]{1,0:T(8,128)(2,1)}, bf16[8,32,1536]{2,1,0:T(8,128)(2,1)}) custom-call(s32[1]{0:T(128)} %bitcast.core, bf16[8,32,64]{2,1,0:T(8,128)(2,1)} %bitcast.28, bf16[8,32,64]{2,1,0:T(8,128)(2,1)} %bitcast.31, bf16[864,256]{1,0:T(8,128)(2,1)} %bitcast.24), custom_call_target="tpu_custom_call" | custom-call | bytes 1572864 | tf_op jit(solution)/shard_map/pallas_call | solution.py:266
  2.7 13.2 %all-to-all-start = ((bf16[8,32,1536]{2,1,0:T(8,128)(2,1)}), bf16[8,32,1536]{2,1,0:T(8,128)(2,1)S(1)}, u32[]{:S(2)}, u32[]{:S(2)}) async-start(bf16[8,32,1536]{2,1,0:T(8,128)(2,1)} %get-tuple-element.33), calls=%async_computation | async-start | bytes 1572864 | tf_op jit(solution)/shard_map/all_to_all | solution.py:284
  15.9 3.2 %collective-permute-start = (bf16[32,64]{1,0:T(8,128)(2,1)S(1)}, bf16[32,64]{1,0:T(8,128)(2,1)S(1)}, u32[]{:S(2)}, u32[]{:S(2)}) collective-permute-start(bf16[32,64]{1,0:T(8,128)(2,1)S(1)} %copy-done.3), channel_id=1, source_target_pairs={{0,1},{1,2},{2,3},{3,4},{4,5},{5,6},{6,7},{8,9},{9,10},{10,11},{11... | collective-permute-start | bytes 12296 | tf_op jit(solution)/shard_map/ppermute | solution.py:241
  19.1 1.3 %collective-permute-start.1 = (bf16[32,64]{1,0:T(8,128)(2,1)S(1)}, bf16[32,64]{1,0:T(8,128)(2,1)S(1)}, u32[]{:S(2)}, u32[]{:S(2)}) collective-permute-start(bf16[32,64]{1,0:T(8,128)(2,1)S(1)} %copy-done.2), channel_id=1, source_target_pairs={{1,0},{2,1},{3,2},{4,3},{5,4},{6,5},{7,6},{9,8},{10,9},{11,10},{12... | collective-permute-start | bytes 12296 | tf_op jit(solution)/shard_map/ppermute | solution.py:241
  20.4 3.4 %collective-permute-done.1.after = bf16[32,64]{1,0:T(8,128)(2,1)S(1)} collective-permute-done((bf16[32,64]{1,0:T(8,128)(2,1)S(1)}, bf16[32,64]{1,0:T(8,128)(2,1)S(1)}, u32[]{:S(2)}, u32[]{:S(2)}) %collective-permute-start.1) | collective-permute-done | bytes 4128 | tf_op jit(solution)/shard_map/ppermute | solution.py:241
  23.9 4.2 %collective-permute-start.3 = (bf16[32,640]{1,0:T(8,128)(2,1)S(1)}, bf16[32,640]{1,0:T(8,128)(2,1)S(1)}, u32[]{:S(2)}, u32[]{:S(2)}) collective-permute-start(bf16[32,640]{1,0:T(8,128)(2,1)S(1)} %shard_map.59.refs_1_), channel_id=1, source_target_pairs={{8,0},{16,8},{24,16},{32,24},{40,32},{48,40},{56,48},{9,1},{17,9},... | collective-permute-start | bytes 122888 | tf_op jit(solution)/shard_map/ppermute | solution.py:241
  28.1 3.0 %collective-permute-start.2 = (bf16[32,640]{1,0:T(8,128)(2,1)S(1)}, bf16[32,640]{1,0:T(8,128)(2,1)S(1)}, u32[]{:S(2)}, u32[]{:S(2)}) collective-permute-start(bf16[32,640]{1,0:T(8,128)(2,1)S(1)} %shard_map.59.refs_1_), channel_id=1, source_target_pairs={{0,8},{8,16},{16,24},{24,32},{32,40},{40,48},{48,56},{1,9},{9,17},... | collective-permute-start | bytes 122888 | tf_op jit(solution)/shard_map/ppermute | solution.py:241
  31.2 1.0 %collective-permute-done.2.refs_0_ = bf16[32,640]{1,0:T(8,128)(2,1)S(1)} collective-permute-done((bf16[32,640]{1,0:T(8,128)(2,1)S(1)}, bf16[32,640]{1,0:T(8,128)(2,1)S(1)}, u32[]{:S(2)}, u32[]{:S(2)}) %collective-permute-start.2) | collective-permute-done | bytes 40992 | tf_op jit(solution)/shard_map/ppermute | solution.py:241
  32.2 0.3 shard_map.60.columns
  32.6 0.4 shard_map.61
  33.0 3.3 %collective-permute-start.4 = (f32[864,128]{1,0:T(8,128)S(1)}, f32[864,128]{1,0:T(8,128)S(1)}, u32[]{:S(2)}, u32[]{:S(2)}) collective-permute-start(f32[864,128]{1,0:T(8,128)S(1)} %get-tuple-element.35), channel_id=1, source_target_pairs={{0,8},{8,0},{1,9},{9,1},{2,10},{10,2},{3,11},{11,3},{4,12},{12,4},... | collective-permute-start | bytes 1327112 | tf_op jit(solution)/shard_map/ppermute | solution.py:302
  36.3 1.4 %collective-permute-done.4.other = f32[864,128]{1,0:T(8,128)S(1)} collective-permute-done((f32[864,128]{1,0:T(8,128)S(1)}, f32[864,128]{1,0:T(8,128)S(1)}, u32[]{:S(2)}, u32[]{:S(2)}) %collective-permute-start.4) | collective-permute-done | bytes 442400 | tf_op jit(solution)/shard_map/ppermute | solution.py:302
  37.7 0.8 shard_map.62
  38.6 9.8 %all-to-all-start.1 = ((f32[864,1,128]{2,1,0:T(1,128)}), f32[864,1,128]{2,1,0:T(1,128)S(1)}, u32[]{:S(2)}, u32[]{:S(2)}) async-start(f32[864,1,128]{2,1,0:T(1,128)} %bitcast.8), calls=%async_computation.1 | async-start | bytes 884736 | tf_op jit(solution)/shard_map/all_to_all | solution.py:246
  48.4 2.6 %collective-permute-start.5 = (bf16[256,448]{1,0:T(8,128)(2,1)S(1)}, bf16[256,448]{1,0:T(8,128)(2,1)S(1)}, u32[]{:S(2)}, u32[]{:S(2)}) collective-permute-start(bf16[256,448]{1,0:T(8,128)(2,1)S(1)} %get-tuple-element.39.mine), channel_id=1, source_target_pairs={{0,8},{8,0},{1,9},{9,1},{2,10},{10,2},{3,11},{11,3},{4,12},{12,4},... | collective-permute-start | bytes 688136 | tf_op jit(solution)/shard_map/ppermute | solution.py:306
  50.9 0.7 shard_map.63
  51.7 0.4 collective-permute-done.5.other
  52.1 1.0 %shard_map.64.refs_1_ = bf16[864,256]{1,0:T(8,128)(2,1)S(1)} custom-call(s32[1]{0:T(128)} %bitcast.core, bf16[256,448]{1,0:T(8,128)(2,1)S(1)} %get-tuple-element.39.mine, bf16[256,448]{1,0:T(8,128)(2,1)S(1)} %collective-permute-done.5.other), custom_call_target="tpu_custom_call" | custom-call | bytes 901124 | tf_op jit(solution)/shard_map/pallas_call | solution.py:24
  53.1 0.8 shard_map.65
  53.9 3.4 %collective-permute-start.6 = (f32[96,128]{1,0:T(8,128)S(1)}, f32[96,128]{1,0:T(8,128)S(1)}, u32[]{:S(2)}, u32[]{:S(2)}) collective-permute-start(f32[96,128]{1,0:T(8,128)S(1)} %get-tuple-element.43), channel_id=1, source_target_pairs={{0,1},{1,2},{2,3},{3,4},{4,5},{5,6},{6,7},{8,9},{9,10},{10,11},{11... | collective-permute-start | bytes 147464 | tf_op jit(solution)/shard_map/ppermute | solution.py:241
  57.3 1.3 %collective-permute-start.7 = (f32[96,128]{1,0:T(8,128)S(1)}, f32[96,128]{1,0:T(8,128)S(1)}, u32[]{:S(2)}, u32[]{:S(2)}) collective-permute-start(f32[96,128]{1,0:T(8,128)S(1)} %get-tuple-element.44), channel_id=1, source_target_pairs={{1,0},{2,1},{3,2},{4,3},{5,4},{6,5},{7,6},{9,8},{10,9},{11,10},{12... | collective-permute-start | bytes 147464 | tf_op jit(solution)/shard_map/ppermute | solution.py:241
  58.6 3.8 %collective-permute-done.7.after = f32[96,128]{1,0:T(8,128)S(1)} collective-permute-done((f32[96,128]{1,0:T(8,128)S(1)}, f32[96,128]{1,0:T(8,128)S(1)}, u32[]{:S(2)}, u32[]{:S(2)}) %collective-permute-start.7) | collective-permute-done | bytes 49184 | tf_op jit(solution)/shard_map/ppermute | solution.py:241
  62.4 0.8 shard_map.66
  63.3 9.2 %all-to-all-start.2 = ((f32[864,1,128]{2,1,0:T(1,128)}), f32[864,1,128]{2,1,0:T(1,128)S(1)}, u32[]{:S(2)}, u32[]{:S(2)}) async-start(f32[864,1,128]{2,1,0:T(1,128)} %bitcast.11), calls=%async_computation.2 | async-start | bytes 884736 | tf_op jit(solution)/shard_map/all_to_all | solution.py:246
  72.6 5.4 %collective-permute-start.8 = (f32[64,512]{1,0:T(8,128)S(1)}, f32[64,512]{1,0:T(8,128)S(1)}, u32[]{:S(2)}, u32[]{:S(2)}) collective-permute-start(f32[64,512]{1,0:T(8,128)S(1)} %get-tuple-element.52), channel_id=1, source_target_pairs={{0,8},{8,16},{16,24},{24,32},{32,40},{40,48},{48,56},{1,9},{9,17},... | collective-permute-start | bytes 393224 | tf_op jit(solution)/shard_map/ppermute | solution.py:241
  78.0 1.9 %collective-permute-start.9 = (f32[64,512]{1,0:T(8,128)S(1)}, f32[64,512]{1,0:T(8,128)S(1)}, u32[]{:S(2)}, u32[]{:S(2)}) collective-permute-start(f32[64,512]{1,0:T(8,128)S(1)} %get-tuple-element.53), channel_id=1, source_target_pairs={{8,0},{16,8},{24,16},{32,24},{40,32},{48,40},{56,48},{9,1},{17,9},... | collective-permute-start | bytes 393224 | tf_op jit(solution)/shard_map/ppermute | solution.py:241
  79.9 1.2 %collective-permute-done.8.below = f32[64,512]{1,0:T(8,128)S(1)} collective-permute-done((f32[64,512]{1,0:T(8,128)S(1)}, f32[64,512]{1,0:T(8,128)S(1)}, u32[]{:S(2)}, u32[]{:S(2)}) %collective-permute-start.8) | collective-permute-done | bytes 131104 | tf_op jit(solution)/shard_map/ppermute | solution.py:241
  81.1 4.0 %collective-permute-done.9.above = f32[64,512]{1,0:T(8,128)S(1)} collective-permute-done((f32[64,512]{1,0:T(8,128)S(1)}, f32[64,512]{1,0:T(8,128)S(1)}, u32[]{:S(2)}, u32[]{:S(2)}) %collective-permute-start.9) | collective-permute-done | bytes 131104 | tf_op jit(solution)/shard_map/ppermute | solution.py:241
  85.1 5.5 %collective-permute-start.10 = (f32[864,128]{1,0:T(8,128)S(1)}, f32[864,128]{1,0:T(8,128)S(1)}, u32[]{:S(2)}, u32[]{:S(2)}) collective-permute-start(f32[864,128]{1,0:T(8,128)S(1)} %bitcast.26), channel_id=1, source_target_pairs={{0,8},{8,0},{1,9},{9,1},{2,10},{10,2},{3,11},{11,3},{4,12},{12,4},... | collective-permute-start | bytes 1327112 | tf_op jit(solution)/shard_map/ppermute | solution.py:337
  90.6 0.7 shard_map.68
  91.3 0.7 collective-permute-done.10.other
  92.0 1.0 %shard_map.69 = f32[864,256]{1,0:T(8,128)} custom-call(s32[1]{0:T(128)} %bitcast.core, f32[864,128]{1,0:T(8,128)S(1)} %bitcast.27, f32[864,128]{1,0:T(8,128)S(1)} %collective-permute-done.10.other), custom_call_target="tpu_custom_call" | custom-call | bytes 1769476 | tf_op jit(solution)/shard_map/pallas_call | solution.py:24
  (16 shorter events, 0.3 us)
Async XLA Ops:
  2.7 13.2 %copy-start.3 = (bf16[32,64]{1,0:T(8,128)(2,1)S(1)}, bf16[32,64]{1,0:T(8,128)(2,1)}, u32[]{:S(2)}) copy-start(bf16[32,64]{1,0:T(8,128)(2,1)} %get-tuple-element.31) | copy-start | bytes 12292
  2.7 16.4 %copy-start.2 = (bf16[32,64]{1,0:T(8,128)(2,1)S(1)}, bf16[32,64]{1,0:T(8,128)(2,1)}, u32[]{:S(2)}) copy-start(bf16[32,64]{1,0:T(8,128)(2,1)} %get-tuple-element.32) | copy-start | bytes 12292
  2.7 21.1 %copy-start.1 = (bf16[1,8,64,32]{2,3,1,0:T(8,128)(2,1)S(1)}, bf16[1,8,64,32]{2,3,1,0:T(8,128)(2,1)}, u32[]{:S(2)}) copy-start(bf16[1,8,64,32]{2,3,1,0:T(8,128)(2,1)} %param.3) | copy-start | bytes 98308
  2.7 29.8 %all-to-all-start = ((bf16[8,32,1536]{2,1,0:T(8,128)(2,1)}), bf16[8,32,1536]{2,1,0:T(8,128)(2,1)S(1)}, u32[]{:S(2)}, u32[]{:S(2)}) async-start(bf16[8,32,1536]{2,1,0:T(8,128)(2,1)} %get-tuple-element.33), calls=%async_computation | async-start | bytes 1572864 | tf_op jit(solution)/shard_map/all_to_all | solution.py:284
  15.9 4.5 %collective-permute-start = (bf16[32,64]{1,0:T(8,128)(2,1)S(1)}, bf16[32,64]{1,0:T(8,128)(2,1)S(1)}, u32[]{:S(2)}, u32[]{:S(2)}) collective-permute-start(bf16[32,64]{1,0:T(8,128)(2,1)S(1)} %copy-done.3), channel_id=1, source_target_pairs={{0,1},{1,2},{2,3},{3,4},{4,5},{5,6},{6,7},{8,9},{9,10},{10,11},{11... | collective-permute-start | bytes 12296 | tf_op jit(solution)/shard_map/ppermute | solution.py:241
  19.1 4.7 %collective-permute-start.1 = (bf16[32,64]{1,0:T(8,128)(2,1)S(1)}, bf16[32,64]{1,0:T(8,128)(2,1)S(1)}, u32[]{:S(2)}, u32[]{:S(2)}) collective-permute-start(bf16[32,64]{1,0:T(8,128)(2,1)S(1)} %copy-done.2), channel_id=1, source_target_pairs={{1,0},{2,1},{3,2},{4,3},{5,4},{6,5},{7,6},{9,8},{10,9},{11,10},{12... | collective-permute-start | bytes 12296 | tf_op jit(solution)/shard_map/ppermute | solution.py:241
  23.9 7.3 %collective-permute-start.3 = (bf16[32,640]{1,0:T(8,128)(2,1)S(1)}, bf16[32,640]{1,0:T(8,128)(2,1)S(1)}, u32[]{:S(2)}, u32[]{:S(2)}) collective-permute-start(bf16[32,640]{1,0:T(8,128)(2,1)S(1)} %shard_map.59.refs_1_), channel_id=1, source_target_pairs={{8,0},{16,8},{24,16},{32,24},{40,32},{48,40},{56,48},{9,1},{17,9},... | collective-permute-start | bytes 122888 | tf_op jit(solution)/shard_map/ppermute | solution.py:241
  28.1 4.1 %collective-permute-start.2 = (bf16[32,640]{1,0:T(8,128)(2,1)S(1)}, bf16[32,640]{1,0:T(8,128)(2,1)S(1)}, u32[]{:S(2)}, u32[]{:S(2)}) collective-permute-start(bf16[32,640]{1,0:T(8,128)(2,1)S(1)} %shard_map.59.refs_1_), channel_id=1, source_target_pairs={{0,8},{8,16},{16,24},{24,32},{32,40},{40,48},{48,56},{1,9},{9,17},... | collective-permute-start | bytes 122888 | tf_op jit(solution)/shard_map/ppermute | solution.py:241
  33.0 4.7 %collective-permute-start.4 = (f32[864,128]{1,0:T(8,128)S(1)}, f32[864,128]{1,0:T(8,128)S(1)}, u32[]{:S(2)}, u32[]{:S(2)}) collective-permute-start(f32[864,128]{1,0:T(8,128)S(1)} %get-tuple-element.35), channel_id=1, source_target_pairs={{0,8},{8,0},{1,9},{9,1},{2,10},{10,2},{3,11},{11,3},{4,12},{12,4},... | collective-permute-start | bytes 1327112 | tf_op jit(solution)/shard_map/ppermute | solution.py:302
  38.6 12.4 %copy-start = (bf16[27,32,256]{2,1,0:T(8,128)(2,1)S(1)}, bf16[27,32,256]{2,1,0:T(8,128)(2,1)}, u32[]{:S(2)}) copy-start(bf16[27,32,256]{2,1,0:T(8,128)(2,1)} %param.4) | copy-start | bytes 1327108
  38.6 23.9 %all-to-all-start.1 = ((f32[864,1,128]{2,1,0:T(1,128)}), f32[864,1,128]{2,1,0:T(1,128)S(1)}, u32[]{:S(2)}, u32[]{:S(2)}) async-start(f32[864,1,128]{2,1,0:T(1,128)} %bitcast.8), calls=%async_computation.1 | async-start | bytes 884736 | tf_op jit(solution)/shard_map/all_to_all | solution.py:246
  48.4 3.7 %collective-permute-start.5 = (bf16[256,448]{1,0:T(8,128)(2,1)S(1)}, bf16[256,448]{1,0:T(8,128)(2,1)S(1)}, u32[]{:S(2)}, u32[]{:S(2)}) collective-permute-start(bf16[256,448]{1,0:T(8,128)(2,1)S(1)} %get-tuple-element.39.mine), channel_id=1, source_target_pairs={{0,8},{8,0},{1,9},{9,1},{2,10},{10,2},{3,11},{11,3},{4,12},{12,4},... | collective-permute-start | bytes 688136 | tf_op jit(solution)/shard_map/ppermute | solution.py:306
  53.9 4.7 %collective-permute-start.6 = (f32[96,128]{1,0:T(8,128)S(1)}, f32[96,128]{1,0:T(8,128)S(1)}, u32[]{:S(2)}, u32[]{:S(2)}) collective-permute-start(f32[96,128]{1,0:T(8,128)S(1)} %get-tuple-element.43), channel_id=1, source_target_pairs={{0,1},{1,2},{2,3},{3,4},{4,5},{5,6},{6,7},{8,9},{9,10},{10,11},{11... | collective-permute-start | bytes 147464 | tf_op jit(solution)/shard_map/ppermute | solution.py:241
  57.3 5.1 %collective-permute-start.7 = (f32[96,128]{1,0:T(8,128)S(1)}, f32[96,128]{1,0:T(8,128)S(1)}, u32[]{:S(2)}, u32[]{:S(2)}) collective-permute-start(f32[96,128]{1,0:T(8,128)S(1)} %get-tuple-element.44), channel_id=1, source_target_pairs={{1,0},{2,1},{3,2},{4,3},{5,4},{6,5},{7,6},{9,8},{10,9},{11,10},{12... | collective-permute-start | bytes 147464 | tf_op jit(solution)/shard_map/ppermute | solution.py:241
  63.3 21.9 %all-to-all-start.2 = ((f32[864,1,128]{2,1,0:T(1,128)}), f32[864,1,128]{2,1,0:T(1,128)S(1)}, u32[]{:S(2)}, u32[]{:S(2)}) async-start(f32[864,1,128]{2,1,0:T(1,128)} %bitcast.11), calls=%async_computation.2 | async-start | bytes 884736 | tf_op jit(solution)/shard_map/all_to_all | solution.py:246
  72.6 8.5 %collective-permute-start.8 = (f32[64,512]{1,0:T(8,128)S(1)}, f32[64,512]{1,0:T(8,128)S(1)}, u32[]{:S(2)}, u32[]{:S(2)}) collective-permute-start(f32[64,512]{1,0:T(8,128)S(1)} %get-tuple-element.52), channel_id=1, source_target_pairs={{0,8},{8,16},{16,24},{24,32},{32,40},{40,48},{48,56},{1,9},{9,17},... | collective-permute-start | bytes 393224 | tf_op jit(solution)/shard_map/ppermute | solution.py:241
  78.0 7.2 %collective-permute-start.9 = (f32[64,512]{1,0:T(8,128)S(1)}, f32[64,512]{1,0:T(8,128)S(1)}, u32[]{:S(2)}, u32[]{:S(2)}) collective-permute-start(f32[64,512]{1,0:T(8,128)S(1)} %get-tuple-element.53), channel_id=1, source_target_pairs={{8,0},{16,8},{24,16},{32,24},{40,32},{48,40},{56,48},{9,1},{17,9},... | collective-permute-start | bytes 393224 | tf_op jit(solution)/shard_map/ppermute | solution.py:241
  85.1 6.9 %collective-permute-start.10 = (f32[864,128]{1,0:T(8,128)S(1)}, f32[864,128]{1,0:T(8,128)S(1)}, u32[]{:S(2)}, u32[]{:S(2)}) collective-permute-start(f32[864,128]{1,0:T(8,128)S(1)} %bitcast.26), channel_id=1, source_target_pairs={{0,8},{8,0},{1,9},{9,1},{2,10},{10,2},{3,11},{11,3},{4,12},{12,4},... | collective-permute-start | bytes 1327112 | tf_op jit(solution)/shard_map/ppermute | solution.py:337

commit v7 on v6

--- a/solution.py
+++ b/solution.py
@@ -53,7 +53,7 @@
     moves[1].wait()
     g_flat = in_row([g_own[r] for r in range(rows)])
     moves[2].wait()
-    turned = k_own[...].astype(F32).T.astype(BF16)
+    turned = k_own[...].T
     for at, to in enumerate(turn(sends.shape[0])):
         sends[at, :, :cells] = g_flat
         sends[at, :, cells : 2 * cells] = v_flat
@@ -71,7 +71,7 @@
 
 
 def in_row(parts):
-    return jnp.concatenate([part.astype(F32) for part in parts], axis=1).astype(BF16)
+    return jnp.concatenate(parts, axis=1)
 
 
 def volume_ring(v, before, after, ring):

time: 93.8 us -> 93.1 us (level)
  transfers between devices with their start and end apart: 14 -> 14, of which waited for: 8 -> 8; matrix products, arithmetic and copies ran while one was open for 0% -> 0% of each run, Pallas kernels for 4% -> 3%
where the time goes in v7:
time: 93.1 us; the launch traced here: 92.3 us
  starting transfers between devices  67.3 us (72%)
  waiting for transfers between devices  16 us (17%)
  Pallas kernels  8.18 us (9%)
    all_to_all x2, starting transfers between devices, exchange_rows(): return lax.all_to_all(apart, axis, 0, 0, tiled=True).reshape(value.shape)  19 us
    ppermute x4, starting transfers between devices, neighbours(): lax.ppermute(value_up, axis, up)  15 us
    all_to_all x1, starting transfers between devices, body(): lax.all_to_all(sends, 'chan', 0, 0, axis_index_groups=[turn(groups)], til...  13.2 us
    ppermute x4, waiting for transfers between devices, neighbours(): lax.ppermute(value_down, axis, down)  11.2 us
    ppermute x4, starting transfers between devices, neighbours(): lax.ppermute(value_down, axis, down)  8.7 us
    pallas_call x11, Pallas kernels, call(): pl.pallas_call(kernel, out_shape=[jax.ShapeDtypeStruct(s, d) for s, d in...  6.15 us
    ppermute x1, starting transfers between devices, body(): other = lax.ppermute(mine, 'core', swap)  5.48 us
    ppermute x1, starting transfers between devices, body(): lax.ppermute(send, 'core', swap)  3.36 us
  transfers between devices with their start and end apart: 14, of which 8 were waited for; matrix products, arithmetic and copies ran while one was open for 0% of the time, Pallas kernels for 3%

profile of v7, /device:TPU:1, one launch (start us, length us, event | category | flops | bytes accessed | tf_op | source)
XLA Modules:
  0.0 92.3 jit_solution(16055192534915343606)
XLA Ops:
  0.6 2.0 %shard_map.58 = (bf16[32,64]{1,0:T(8,128)(2,1)}, bf16[32,64]{1,0:T(8,128)(2,1)}, bf16[8,32,1536]{2,1,0:T(8,128)(2,1)}) custom-call(s32[1]{0:T(128)} %bitcast.core, bf16[8,32,64]{2,1,0:T(8,128)(2,1)} %bitcast.28, bf16[8,32,64]{2,1,0:T(8,128)(2,1)} %bitcast.31, bf16[864,256]{1,0:T(8,128)(2,1)} %bitcast.24), custom_call_target="tpu_custom_call" | custom-call | bytes 1572864 | tf_op jit(solution)/shard_map/pallas_call | solution.py:266
  2.7 13.2 %all-to-all-start = ((bf16[8,32,1536]{2,1,0:T(8,128)(2,1)}), bf16[8,32,1536]{2,1,0:T(8,128)(2,1)S(1)}, u32[]{:S(2)}, u32[]{:S(2)}) async-start(bf16[8,32,1536]{2,1,0:T(8,128)(2,1)} %get-tuple-element.33), calls=%async_computation | async-start | bytes 1572864 | tf_op jit(solution)/shard_map/all_to_all | solution.py:284
  15.9 3.2 %collective-permute-start = (bf16[32,64]{1,0:T(8,128)(2,1)S(1)}, bf16[32,64]{1,0:T(8,128)(2,1)S(1)}, u32[]{:S(2)}, u32[]{:S(2)}) collective-permute-start(bf16[32,64]{1,0:T(8,128)(2,1)S(1)} %copy-done.3), channel_id=1, source_target_pairs={{0,1},{1,2},{2,3},{3,4},{4,5},{5,6},{6,7},{8,9},{9,10},{10,11},{11... | collective-permute-start | bytes 12296 | tf_op jit(solution)/shard_map/ppermute | solution.py:241
  19.1 1.3 %collective-permute-start.1 = (bf16[32,64]{1,0:T(8,128)(2,1)S(1)}, bf16[32,64]{1,0:T(8,128)(2,1)S(1)}, u32[]{:S(2)}, u32[]{:S(2)}) collective-permute-start(bf16[32,64]{1,0:T(8,128)(2,1)S(1)} %copy-done.2), channel_id=1, source_target_pairs={{1,0},{2,1},{3,2},{4,3},{5,4},{6,5},{7,6},{9,8},{10,9},{11,10},{12... | collective-permute-start | bytes 12296 | tf_op jit(solution)/shard_map/ppermute | solution.py:241
  20.4 3.4 %collective-permute-done.1.after = bf16[32,64]{1,0:T(8,128)(2,1)S(1)} collective-permute-done((bf16[32,64]{1,0:T(8,128)(2,1)S(1)}, bf16[32,64]{1,0:T(8,128)(2,1)S(1)}, u32[]{:S(2)}, u32[]{:S(2)}) %collective-permute-start.1) | collective-permute-done | bytes 4128 | tf_op jit(solution)/shard_map/ppermute | solution.py:241
  23.9 4.2 %collective-permute-start.3 = (bf16[32,640]{1,0:T(8,128)(2,1)S(1)}, bf16[32,640]{1,0:T(8,128)(2,1)S(1)}, u32[]{:S(2)}, u32[]{:S(2)}) collective-permute-start(bf16[32,640]{1,0:T(8,128)(2,1)S(1)} %shard_map.59.refs_1_), channel_id=1, source_target_pairs={{8,0},{16,8},{24,16},{32,24},{40,32},{48,40},{56,48},{9,1},{17,9},... | collective-permute-start | bytes 122888 | tf_op jit(solution)/shard_map/ppermute | solution.py:241
  28.1 3.0 %collective-permute-start.2 = (bf16[32,640]{1,0:T(8,128)(2,1)S(1)}, bf16[32,640]{1,0:T(8,128)(2,1)S(1)}, u32[]{:S(2)}, u32[]{:S(2)}) collective-permute-start(bf16[32,640]{1,0:T(8,128)(2,1)S(1)} %shard_map.59.refs_1_), channel_id=1, source_target_pairs={{0,8},{8,16},{16,24},{24,32},{32,40},{40,48},{48,56},{1,9},{9,17},... | collective-permute-start | bytes 122888 | tf_op jit(solution)/shard_map/ppermute | solution.py:241
  31.1 1.0 %collective-permute-done.2.refs_0_ = bf16[32,640]{1,0:T(8,128)(2,1)S(1)} collective-permute-done((bf16[32,640]{1,0:T(8,128)(2,1)S(1)}, bf16[32,640]{1,0:T(8,128)(2,1)S(1)}, u32[]{:S(2)}, u32[]{:S(2)}) %collective-permute-start.2) | collective-permute-done | bytes 40992 | tf_op jit(solution)/shard_map/ppermute | solution.py:241
  32.2 0.3 shard_map.60.columns
  32.5 0.4 shard_map.61
  33.0 3.4 %collective-permute-start.4 = (f32[864,128]{1,0:T(8,128)S(1)}, f32[864,128]{1,0:T(8,128)S(1)}, u32[]{:S(2)}, u32[]{:S(2)}) collective-permute-start(f32[864,128]{1,0:T(8,128)S(1)} %get-tuple-element.35), channel_id=1, source_target_pairs={{0,8},{8,0},{1,9},{9,1},{2,10},{10,2},{3,11},{11,3},{4,12},{12,4},... | collective-permute-start | bytes 1327112 | tf_op jit(solution)/shard_map/ppermute | solution.py:302
  36.3 1.4 %collective-permute-done.4.other = f32[864,128]{1,0:T(8,128)S(1)} collective-permute-done((f32[864,128]{1,0:T(8,128)S(1)}, f32[864,128]{1,0:T(8,128)S(1)}, u32[]{:S(2)}, u32[]{:S(2)}) %collective-permute-start.4) | collective-permute-done | bytes 442400 | tf_op jit(solution)/shard_map/ppermute | solution.py:302
  37.7 0.8 shard_map.62
  38.5 9.8 %all-to-all-start.1 = ((f32[864,1,128]{2,1,0:T(1,128)}), f32[864,1,128]{2,1,0:T(1,128)S(1)}, u32[]{:S(2)}, u32[]{:S(2)}) async-start(f32[864,1,128]{2,1,0:T(1,128)} %bitcast.8), calls=%async_computation.1 | async-start | bytes 884736 | tf_op jit(solution)/shard_map/all_to_all | solution.py:246
  48.3 2.6 %collective-permute-start.5 = (bf16[256,448]{1,0:T(8,128)(2,1)S(1)}, bf16[256,448]{1,0:T(8,128)(2,1)S(1)}, u32[]{:S(2)}, u32[]{:S(2)}) collective-permute-start(bf16[256,448]{1,0:T(8,128)(2,1)S(1)} %get-tuple-element.39.mine), channel_id=1, source_target_pairs={{0,8},{8,0},{1,9},{9,1},{2,10},{10,2},{3,11},{11,3},{4,12},{12,4},... | collective-permute-start | bytes 688136 | tf_op jit(solution)/shard_map/ppermute | solution.py:306
  50.9 0.7 shard_map.63
  51.6 0.4 collective-permute-done.5.other
  52.1 0.4 shard_map.64.refs_1_
  52.5 0.8 shard_map.65
  53.2 3.4 %collective-permute-start.6 = (f32[96,128]{1,0:T(8,128)S(1)}, f32[96,128]{1,0:T(8,128)S(1)}, u32[]{:S(2)}, u32[]{:S(2)}) collective-permute-start(f32[96,128]{1,0:T(8,128)S(1)} %get-tuple-element.43), channel_id=1, source_target_pairs={{0,1},{1,2},{2,3},{3,4},{4,5},{5,6},{6,7},{8,9},{9,10},{10,11},{11... | collective-permute-start | bytes 147464 | tf_op jit(solution)/shard_map/ppermute | solution.py:241
  56.6 1.3 %collective-permute-start.7 = (f32[96,128]{1,0:T(8,128)S(1)}, f32[96,128]{1,0:T(8,128)S(1)}, u32[]{:S(2)}, u32[]{:S(2)}) collective-permute-start(f32[96,128]{1,0:T(8,128)S(1)} %get-tuple-element.44), channel_id=1, source_target_pairs={{1,0},{2,1},{3,2},{4,3},{5,4},{6,5},{7,6},{9,8},{10,9},{11,10},{12... | collective-permute-start | bytes 147464 | tf_op jit(solution)/shard_map/ppermute | solution.py:241
  58.0 3.8 %collective-permute-done.7.after = f32[96,128]{1,0:T(8,128)S(1)} collective-permute-done((f32[96,128]{1,0:T(8,128)S(1)}, f32[96,128]{1,0:T(8,128)S(1)}, u32[]{:S(2)}, u32[]{:S(2)}) %collective-permute-start.7) | collective-permute-done | bytes 49184 | tf_op jit(solution)/shard_map/ppermute | solution.py:241
  61.8 0.8 shard_map.66
  62.6 9.2 %all-to-all-start.2 = ((f32[864,1,128]{2,1,0:T(1,128)}), f32[864,1,128]{2,1,0:T(1,128)S(1)}, u32[]{:S(2)}, u32[]{:S(2)}) async-start(f32[864,1,128]{2,1,0:T(1,128)} %bitcast.11), calls=%async_computation.2 | async-start | bytes 884736 | tf_op jit(solution)/shard_map/all_to_all | solution.py:246
  71.9 5.4 %collective-permute-start.8 = (f32[64,512]{1,0:T(8,128)S(1)}, f32[64,512]{1,0:T(8,128)S(1)}, u32[]{:S(2)}, u32[]{:S(2)}) collective-permute-start(f32[64,512]{1,0:T(8,128)S(1)} %get-tuple-element.52), channel_id=1, source_target_pairs={{0,8},{8,16},{16,24},{24,32},{32,40},{40,48},{48,56},{1,9},{9,17},... | collective-permute-start | bytes 393224 | tf_op jit(solution)/shard_map/ppermute | solution.py:241
  77.3 1.9 %collective-permute-start.9 = (f32[64,512]{1,0:T(8,128)S(1)}, f32[64,512]{1,0:T(8,128)S(1)}, u32[]{:S(2)}, u32[]{:S(2)}) collective-permute-start(f32[64,512]{1,0:T(8,128)S(1)} %get-tuple-element.53), channel_id=1, source_target_pairs={{8,0},{16,8},{24,16},{32,24},{40,32},{48,40},{56,48},{9,1},{17,9},... | collective-permute-start | bytes 393224 | tf_op jit(solution)/shard_map/ppermute | solution.py:241
  79.2 1.2 %collective-permute-done.8.below = f32[64,512]{1,0:T(8,128)S(1)} collective-permute-done((f32[64,512]{1,0:T(8,128)S(1)}, f32[64,512]{1,0:T(8,128)S(1)}, u32[]{:S(2)}, u32[]{:S(2)}) %collective-permute-start.8) | collective-permute-done | bytes 131104 | tf_op jit(solution)/shard_map/ppermute | solution.py:241
  80.5 4.0 %collective-permute-done.9.above = f32[64,512]{1,0:T(8,128)S(1)} collective-permute-done((f32[64,512]{1,0:T(8,128)S(1)}, f32[64,512]{1,0:T(8,128)S(1)}, u32[]{:S(2)}, u32[]{:S(2)}) %collective-permute-start.9) | collective-permute-done | bytes 131104 | tf_op jit(solution)/shard_map/ppermute | solution.py:241
  84.5 5.5 %collective-permute-start.10 = (f32[864,128]{1,0:T(8,128)S(1)}, f32[864,128]{1,0:T(8,128)S(1)}, u32[]{:S(2)}, u32[]{:S(2)}) collective-permute-start(f32[864,128]{1,0:T(8,128)S(1)} %bitcast.26), channel_id=1, source_target_pairs={{0,8},{8,0},{1,9},{9,1},{2,10},{10,2},{3,11},{11,3},{4,12},{12,4},... | collective-permute-start | bytes 1327112 | tf_op jit(solution)/shard_map/ppermute | solution.py:337
  89.9 0.7 shard_map.68
  90.7 0.7 collective-permute-done.10.other
  91.3 1.0 %shard_map.69 = f32[864,256]{1,0:T(8,128)} custom-call(s32[1]{0:T(128)} %bitcast.core, f32[864,128]{1,0:T(8,128)S(1)} %bitcast.27, f32[864,128]{1,0:T(8,128)S(1)} %collective-permute-done.10.other), custom_call_target="tpu_custom_call" | custom-call | bytes 1769476 | tf_op jit(solution)/shard_map/pallas_call | solution.py:24
  (16 shorter events, 0.3 us)
Async XLA Ops:
  2.7 13.2 %copy-start.3 = (bf16[32,64]{1,0:T(8,128)(2,1)S(1)}, bf16[32,64]{1,0:T(8,128)(2,1)}, u32[]{:S(2)}) copy-start(bf16[32,64]{1,0:T(8,128)(2,1)} %get-tuple-element.31) | copy-start | bytes 12292
  2.7 16.4 %copy-start.2 = (bf16[32,64]{1,0:T(8,128)(2,1)S(1)}, bf16[32,64]{1,0:T(8,128)(2,1)}, u32[]{:S(2)}) copy-start(bf16[32,64]{1,0:T(8,128)(2,1)} %get-tuple-element.32) | copy-start | bytes 12292
  2.7 21.1 %copy-start.1 = (bf16[1,8,64,32]{2,3,1,0:T(8,128)(2,1)S(1)}, bf16[1,8,64,32]{2,3,1,0:T(8,128)(2,1)}, u32[]{:S(2)}) copy-start(bf16[1,8,64,32]{2,3,1,0:T(8,128)(2,1)} %param.3) | copy-start | bytes 98308
  2.7 29.8 %all-to-all-start = ((bf16[8,32,1536]{2,1,0:T(8,128)(2,1)}), bf16[8,32,1536]{2,1,0:T(8,128)(2,1)S(1)}, u32[]{:S(2)}, u32[]{:S(2)}) async-start(bf16[8,32,1536]{2,1,0:T(8,128)(2,1)} %get-tuple-element.33), calls=%async_computation | async-start | bytes 1572864 | tf_op jit(solution)/shard_map/all_to_all | solution.py:284
  15.9 4.5 %collective-permute-start = (bf16[32,64]{1,0:T(8,128)(2,1)S(1)}, bf16[32,64]{1,0:T(8,128)(2,1)S(1)}, u32[]{:S(2)}, u32[]{:S(2)}) collective-permute-start(bf16[32,64]{1,0:T(8,128)(2,1)S(1)} %copy-done.3), channel_id=1, source_target_pairs={{0,1},{1,2},{2,3},{3,4},{4,5},{5,6},{6,7},{8,9},{9,10},{10,11},{11... | collective-permute-start | bytes 12296 | tf_op jit(solution)/shard_map/ppermute | solution.py:241
  19.1 4.7 %collective-permute-start.1 = (bf16[32,64]{1,0:T(8,128)(2,1)S(1)}, bf16[32,64]{1,0:T(8,128)(2,1)S(1)}, u32[]{:S(2)}, u32[]{:S(2)}) collective-permute-start(bf16[32,64]{1,0:T(8,128)(2,1)S(1)} %copy-done.2), channel_id=1, source_target_pairs={{1,0},{2,1},{3,2},{4,3},{5,4},{6,5},{7,6},{9,8},{10,9},{11,10},{12... | collective-permute-start | bytes 12296 | tf_op jit(solution)/shard_map/ppermute | solution.py:241
  23.9 7.3 %collective-permute-start.3 = (bf16[32,640]{1,0:T(8,128)(2,1)S(1)}, bf16[32,640]{1,0:T(8,128)(2,1)S(1)}, u32[]{:S(2)}, u32[]{:S(2)}) collective-permute-start(bf16[32,640]{1,0:T(8,128)(2,1)S(1)} %shard_map.59.refs_1_), channel_id=1, source_target_pairs={{8,0},{16,8},{24,16},{32,24},{40,32},{48,40},{56,48},{9,1},{17,9},... | collective-permute-start | bytes 122888 | tf_op jit(solution)/shard_map/ppermute | solution.py:241
  28.1 4.1 %collective-permute-start.2 = (bf16[32,640]{1,0:T(8,128)(2,1)S(1)}, bf16[32,640]{1,0:T(8,128)(2,1)S(1)}, u32[]{:S(2)}, u32[]{:S(2)}) collective-permute-start(bf16[32,640]{1,0:T(8,128)(2,1)S(1)} %shard_map.59.refs_1_), channel_id=1, source_target_pairs={{0,8},{8,16},{16,24},{24,32},{32,40},{40,48},{48,56},{1,9},{9,17},... | collective-permute-start | bytes 122888 | tf_op jit(solution)/shard_map/ppermute | solution.py:241
  33.0 4.8 %collective-permute-start.4 = (f32[864,128]{1,0:T(8,128)S(1)}, f32[864,128]{1,0:T(8,128)S(1)}, u32[]{:S(2)}, u32[]{:S(2)}) collective-permute-start(f32[864,128]{1,0:T(8,128)S(1)} %get-tuple-element.35), channel_id=1, source_target_pairs={{0,8},{8,0},{1,9},{9,1},{2,10},{10,2},{3,11},{11,3},{4,12},{12,4},... | collective-permute-start | bytes 1327112 | tf_op jit(solution)/shard_map/ppermute | solution.py:302
  38.5 12.4 %copy-start = (bf16[27,32,256]{2,1,0:T(8,128)(2,1)S(1)}, bf16[27,32,256]{2,1,0:T(8,128)(2,1)}, u32[]{:S(2)}) copy-start(bf16[27,32,256]{2,1,0:T(8,128)(2,1)} %param.4) | copy-start | bytes 1327108
  38.5 23.2 %all-to-all-start.1 = ((f32[864,1,128]{2,1,0:T(1,128)}), f32[864,1,128]{2,1,0:T(1,128)S(1)}, u32[]{:S(2)}, u32[]{:S(2)}) async-start(f32[864,1,128]{2,1,0:T(1,128)} %bitcast.8), calls=%async_computation.1 | async-start | bytes 884736 | tf_op jit(solution)/shard_map/all_to_all | solution.py:246
  48.3 3.7 %collective-permute-start.5 = (bf16[256,448]{1,0:T(8,128)(2,1)S(1)}, bf16[256,448]{1,0:T(8,128)(2,1)S(1)}, u32[]{:S(2)}, u32[]{:S(2)}) collective-permute-start(bf16[256,448]{1,0:T(8,128)(2,1)S(1)} %get-tuple-element.39.mine), channel_id=1, source_target_pairs={{0,8},{8,0},{1,9},{9,1},{2,10},{10,2},{3,11},{11,3},{4,12},{12,4},... | collective-permute-start | bytes 688136 | tf_op jit(solution)/shard_map/ppermute | solution.py:306
  53.2 4.7 %collective-permute-start.6 = (f32[96,128]{1,0:T(8,128)S(1)}, f32[96,128]{1,0:T(8,128)S(1)}, u32[]{:S(2)}, u32[]{:S(2)}) collective-permute-start(f32[96,128]{1,0:T(8,128)S(1)} %get-tuple-element.43), channel_id=1, source_target_pairs={{0,1},{1,2},{2,3},{3,4},{4,5},{5,6},{6,7},{8,9},{9,10},{10,11},{11... | collective-permute-start | bytes 147464 | tf_op jit(solution)/shard_map/ppermute | solution.py:241
  56.6 5.1 %collective-permute-start.7 = (f32[96,128]{1,0:T(8,128)S(1)}, f32[96,128]{1,0:T(8,128)S(1)}, u32[]{:S(2)}, u32[]{:S(2)}) collective-permute-start(f32[96,128]{1,0:T(8,128)S(1)} %get-tuple-element.44), channel_id=1, source_target_pairs={{1,0},{2,1},{3,2},{4,3},{5,4},{6,5},{7,6},{9,8},{10,9},{11,10},{12... | collective-permute-start | bytes 147464 | tf_op jit(solution)/shard_map/ppermute | solution.py:241
  62.6 21.8 %all-to-all-start.2 = ((f32[864,1,128]{2,1,0:T(1,128)}), f32[864,1,128]{2,1,0:T(1,128)S(1)}, u32[]{:S(2)}, u32[]{:S(2)}) async-start(f32[864,1,128]{2,1,0:T(1,128)} %bitcast.11), calls=%async_computation.2 | async-start | bytes 884736 | tf_op jit(solution)/shard_map/all_to_all | solution.py:246
  71.9 8.5 %collective-permute-start.8 = (f32[64,512]{1,0:T(8,128)S(1)}, f32[64,512]{1,0:T(8,128)S(1)}, u32[]{:S(2)}, u32[]{:S(2)}) collective-permute-start(f32[64,512]{1,0:T(8,128)S(1)} %get-tuple-element.52), channel_id=1, source_target_pairs={{0,8},{8,16},{16,24},{24,32},{32,40},{40,48},{48,56},{1,9},{9,17},... | collective-permute-start | bytes 393224 | tf_op jit(solution)/shard_map/ppermute | solution.py:241
  77.3 7.1 %collective-permute-start.9 = (f32[64,512]{1,0:T(8,128)S(1)}, f32[64,512]{1,0:T(8,128)S(1)}, u32[]{:S(2)}, u32[]{:S(2)}) collective-permute-start(f32[64,512]{1,0:T(8,128)S(1)} %get-tuple-element.53), channel_id=1, source_target_pairs={{8,0},{16,8},{24,16},{32,24},{40,32},{48,40},{56,48},{9,1},{17,9},... | collective-permute-start | bytes 393224 | tf_op jit(solution)/shard_map/ppermute | solution.py:241
  84.5 6.9 %collective-permute-start.10 = (f32[864,128]{1,0:T(8,128)S(1)}, f32[864,128]{1,0:T(8,128)S(1)}, u32[]{:S(2)}, u32[]{:S(2)}) collective-permute-start(f32[864,128]{1,0:T(8,128)S(1)} %bitcast.26), channel_id=1, source_target_pairs={{0,8},{8,0},{1,9},{9,1},{2,10},{10,2},{3,11},{11,3},{4,12},{12,4},... | collective-permute-start | bytes 1327112 | tf_op jit(solution)/shard_map/ppermute | solution.py:337

commit v8 on v7

--- a/solution.py
+++ b/solution.py
@@ -43,7 +43,7 @@
             k.at[pl.ds(pl.multiple_of(core[0] * skip, c), held)], k_own.at[pl.ds(0, held)], sems.at[2]
         ),
     ]
-    for move in moves:
+    for move in moves[::-1]:
         move.start()
     k_own[held:] = jnp.zeros((k_own.shape[0] - held, k_own.shape[1]), BF16)
     moves[0].wait()
@@ -211,10 +211,6 @@
     for r in range(rows):
         shifted = value if r == 0 else pltpu.roll(value, lanes - r * z, 1)
         out[r] = shifted[:, :z].astype(BF16)
-
-
-def add_halves(keep, other, out):
-    out[...] = keep[...] + other[...]
 
 
 def sum_pieces(scale, pieces, parts, out):
@@ -299,7 +295,7 @@
         received,
     )
     swap = [(0, 1), (1, 0)]
-    (halves,) = call(add_halves, [(piece, F32)], 0, keep, lax.ppermute(send, "core", swap))
+    halves = keep + lax.ppermute(send, "core", swap)
 
     halves, k_mine, received = lax.optimization_barrier((halves, k_mine, received))
     parts = exchange_rows(halves, ("x", "sy"))

time: 93.1 us -> 93.3 us (level)
    pallas_call x11 -> x10, Pallas kernels: 6.15 us -> 5.35 us  [call(): pl.pallas_call(kernel, out_shape=[jax.ShapeDtypeStruct(s, d) for s, d in...]
where the time goes in v8:
time: 93.3 us; the launch traced here: 92.5 us
  starting transfers between devices  67.3 us (72%)
  waiting for transfers between devices  16 us (17%)
  Pallas kernels  7.51 us (8%)
    all_to_all x2, starting transfers between devices, exchange_rows(): return lax.all_to_all(apart, axis, 0, 0, tiled=True).reshape(value.shape)  19 us
    ppermute x4, starting transfers between devices, neighbours(): lax.ppermute(value_up, axis, up)  15 us
    all_to_all x1, starting transfers between devices, body(): lax.all_to_all(sends, 'chan', 0, 0, axis_index_groups=[turn(groups)], til...  13.2 us
    ppermute x4, waiting for transfers between devices, neighbours(): lax.ppermute(value_down, axis, down)  11.2 us
    ppermute x4, starting transfers between devices, neighbours(): lax.ppermute(value_down, axis, down)  8.7 us
    ppermute x1, starting transfers between devices, body(): other = lax.ppermute(mine, 'core', swap)  5.48 us
    pallas_call x10, Pallas kernels, call(): pl.pallas_call(kernel, out_shape=[jax.ShapeDtypeStruct(s, d) for s, d in...  5.35 us
    ppermute x1, starting transfers between devices, body(): halves = keep + lax.ppermute(send, 'core', swap)  3.35 us
  transfers between devices with their start and end apart: 14, of which 8 were waited for; matrix products, arithmetic and copies ran while one was open for 0% of the time, Pallas kernels for 3%

profile of v8, /device:TPU:1, one launch (start us, length us, event | category | flops | bytes accessed | tf_op | source)
XLA Modules:
  0.0 92.5 jit_solution(14292551842836735570)
XLA Ops:
  0.6 2.2 %shard_map.58 = (bf16[32,64]{1,0:T(8,128)(2,1)}, bf16[32,64]{1,0:T(8,128)(2,1)}, bf16[8,32,1536]{2,1,0:T(8,128)(2,1)}) custom-call(s32[1]{0:T(128)} %bitcast.core, bf16[8,32,64]{2,1,0:T(8,128)(2,1)} %bitcast.28, bf16[8,32,64]{2,1,0:T(8,128)(2,1)} %bitcast.31, bf16[864,256]{1,0:T(8,128)(2,1)} %bitcast.24), custom_call_target="tpu_custom_call" | custom-call | bytes 1572864 | tf_op jit(solution)/shard_map/pallas_call | solution.py:262
  2.8 13.2 %all-to-all-start = ((bf16[8,32,1536]{2,1,0:T(8,128)(2,1)}), bf16[8,32,1536]{2,1,0:T(8,128)(2,1)S(1)}, u32[]{:S(2)}, u32[]{:S(2)}) async-start(bf16[8,32,1536]{2,1,0:T(8,128)(2,1)} %get-tuple-element.33), calls=%async_computation | async-start | bytes 1572864 | tf_op jit(solution)/shard_map/all_to_all | solution.py:280
  16.0 3.2 %collective-permute-start = (bf16[32,64]{1,0:T(8,128)(2,1)S(1)}, bf16[32,64]{1,0:T(8,128)(2,1)S(1)}, u32[]{:S(2)}, u32[]{:S(2)}) collective-permute-start(bf16[32,64]{1,0:T(8,128)(2,1)S(1)} %copy-done.3), channel_id=1, source_target_pairs={{0,1},{1,2},{2,3},{3,4},{4,5},{5,6},{6,7},{8,9},{9,10},{10,11},{11... | collective-permute-start | bytes 12296 | tf_op jit(solution)/shard_map/ppermute | solution.py:237
  19.2 1.3 %collective-permute-start.1 = (bf16[32,64]{1,0:T(8,128)(2,1)S(1)}, bf16[32,64]{1,0:T(8,128)(2,1)S(1)}, u32[]{:S(2)}, u32[]{:S(2)}) collective-permute-start(bf16[32,64]{1,0:T(8,128)(2,1)S(1)} %copy-done.2), channel_id=1, source_target_pairs={{1,0},{2,1},{3,2},{4,3},{5,4},{6,5},{7,6},{9,8},{10,9},{11,10},{12... | collective-permute-start | bytes 12296 | tf_op jit(solution)/shard_map/ppermute | solution.py:237
  20.5 3.4 %collective-permute-done.1.after = bf16[32,64]{1,0:T(8,128)(2,1)S(1)} collective-permute-done((bf16[32,64]{1,0:T(8,128)(2,1)S(1)}, bf16[32,64]{1,0:T(8,128)(2,1)S(1)}, u32[]{:S(2)}, u32[]{:S(2)}) %collective-permute-start.1) | collective-permute-done | bytes 4128 | tf_op jit(solution)/shard_map/ppermute | solution.py:237
  24.0 4.2 %collective-permute-start.3 = (bf16[32,640]{1,0:T(8,128)(2,1)S(1)}, bf16[32,640]{1,0:T(8,128)(2,1)S(1)}, u32[]{:S(2)}, u32[]{:S(2)}) collective-permute-start(bf16[32,640]{1,0:T(8,128)(2,1)S(1)} %shard_map.59.refs_1_), channel_id=1, source_target_pairs={{8,0},{16,8},{24,16},{32,24},{40,32},{48,40},{56,48},{9,1},{17,9},... | collective-permute-start | bytes 122888 | tf_op jit(solution)/shard_map/ppermute | solution.py:237
  28.2 3.0 %collective-permute-start.2 = (bf16[32,640]{1,0:T(8,128)(2,1)S(1)}, bf16[32,640]{1,0:T(8,128)(2,1)S(1)}, u32[]{:S(2)}, u32[]{:S(2)}) collective-permute-start(bf16[32,640]{1,0:T(8,128)(2,1)S(1)} %shard_map.59.refs_1_), channel_id=1, source_target_pairs={{0,8},{8,16},{16,24},{24,32},{32,40},{40,48},{48,56},{1,9},{9,17},... | collective-permute-start | bytes 122888 | tf_op jit(solution)/shard_map/ppermute | solution.py:237
  31.3 1.0 %collective-permute-done.2.refs_0_ = bf16[32,640]{1,0:T(8,128)(2,1)S(1)} collective-permute-done((bf16[32,640]{1,0:T(8,128)(2,1)S(1)}, bf16[32,640]{1,0:T(8,128)(2,1)S(1)}, u32[]{:S(2)}, u32[]{:S(2)}) %collective-permute-start.2) | collective-permute-done | bytes 40992 | tf_op jit(solution)/shard_map/ppermute | solution.py:237
  32.3 0.3 shard_map.60.columns
  32.7 0.4 shard_map.61
  33.1 3.4 %collective-permute-start.4 = (f32[864,128]{1,0:T(8,128)S(1)}, f32[864,128]{1,0:T(8,128)S(1)}, u32[]{:S(2)}, u32[]{:S(2)}) collective-permute-start(f32[864,128]{1,0:T(8,128)S(1)} %get-tuple-element.35), channel_id=1, source_target_pairs={{0,8},{8,0},{1,9},{9,1},{2,10},{10,2},{3,11},{11,3},{4,12},{12,4},... | collective-permute-start | bytes 1327112 | tf_op jit(solution)/shard_map/ppermute | solution.py:298
  36.5 1.4 %collective-permute-done.4 = f32[864,128]{1,0:T(8,128)S(1)} collective-permute-done((f32[864,128]{1,0:T(8,128)S(1)}, f32[864,128]{1,0:T(8,128)S(1)}, u32[]{:S(2)}, u32[]{:S(2)}) %collective-permute-start.4) | collective-permute-done | bytes 442400 | tf_op jit(solution)/shard_map/ppermute | solution.py:298
  37.9 0.8 add.3
  38.7 9.8 %all-to-all-start.1 = ((f32[864,1,128]{2,1,0:T(1,128)}), f32[864,1,128]{2,1,0:T(1,128)S(1)}, u32[]{:S(2)}, u32[]{:S(2)}) async-start(f32[864,1,128]{2,1,0:T(1,128)} %bitcast.8), calls=%async_computation.1 | async-start | bytes 884736 | tf_op jit(solution)/shard_map/all_to_all | solution.py:242
  48.5 2.6 %collective-permute-start.5 = (bf16[256,448]{1,0:T(8,128)(2,1)S(1)}, bf16[256,448]{1,0:T(8,128)(2,1)S(1)}, u32[]{:S(2)}, u32[]{:S(2)}) collective-permute-start(bf16[256,448]{1,0:T(8,128)(2,1)S(1)} %get-tuple-element.39.mine), channel_id=1, source_target_pairs={{0,8},{8,0},{1,9},{9,1},{2,10},{10,2},{3,11},{11,3},{4,12},{12,4},... | collective-permute-start | bytes 688136 | tf_op jit(solution)/shard_map/ppermute | solution.py:302
  51.1 0.7 shard_map.62
  51.8 0.4 collective-permute-done.5.other
  52.2 0.4 shard_map.63.refs_1_
  52.6 0.8 shard_map.64
  53.4 3.4 %collective-permute-start.6 = (f32[96,128]{1,0:T(8,128)S(1)}, f32[96,128]{1,0:T(8,128)S(1)}, u32[]{:S(2)}, u32[]{:S(2)}) collective-permute-start(f32[96,128]{1,0:T(8,128)S(1)} %get-tuple-element.43), channel_id=1, source_target_pairs={{0,1},{1,2},{2,3},{3,4},{4,5},{5,6},{6,7},{8,9},{9,10},{10,11},{11... | collective-permute-start | bytes 147464 | tf_op jit(solution)/shard_map/ppermute | solution.py:237
  56.8 1.3 %collective-permute-start.7 = (f32[96,128]{1,0:T(8,128)S(1)}, f32[96,128]{1,0:T(8,128)S(1)}, u32[]{:S(2)}, u32[]{:S(2)}) collective-permute-start(f32[96,128]{1,0:T(8,128)S(1)} %get-tuple-element.44), channel_id=1, source_target_pairs={{1,0},{2,1},{3,2},{4,3},{5,4},{6,5},{7,6},{9,8},{10,9},{11,10},{12... | collective-permute-start | bytes 147464 | tf_op jit(solution)/shard_map/ppermute | solution.py:237
  58.1 3.8 %collective-permute-done.7.after = f32[96,128]{1,0:T(8,128)S(1)} collective-permute-done((f32[96,128]{1,0:T(8,128)S(1)}, f32[96,128]{1,0:T(8,128)S(1)}, u32[]{:S(2)}, u32[]{:S(2)}) %collective-permute-start.7) | collective-permute-done | bytes 49184 | tf_op jit(solution)/shard_map/ppermute | solution.py:237
  61.9 0.8 shard_map.65
  62.8 9.2 %all-to-all-start.2 = ((f32[864,1,128]{2,1,0:T(1,128)}), f32[864,1,128]{2,1,0:T(1,128)S(1)}, u32[]{:S(2)}, u32[]{:S(2)}) async-start(f32[864,1,128]{2,1,0:T(1,128)} %bitcast.11), calls=%async_computation.2 | async-start | bytes 884736 | tf_op jit(solution)/shard_map/all_to_all | solution.py:242
  72.1 5.4 %collective-permute-start.8 = (f32[64,512]{1,0:T(8,128)S(1)}, f32[64,512]{1,0:T(8,128)S(1)}, u32[]{:S(2)}, u32[]{:S(2)}) collective-permute-start(f32[64,512]{1,0:T(8,128)S(1)} %get-tuple-element.52), channel_id=1, source_target_pairs={{0,8},{8,16},{16,24},{24,32},{32,40},{40,48},{48,56},{1,9},{9,17},... | collective-permute-start | bytes 393224 | tf_op jit(solution)/shard_map/ppermute | solution.py:237
  77.5 1.9 %collective-permute-start.9 = (f32[64,512]{1,0:T(8,128)S(1)}, f32[64,512]{1,0:T(8,128)S(1)}, u32[]{:S(2)}, u32[]{:S(2)}) collective-permute-start(f32[64,512]{1,0:T(8,128)S(1)} %get-tuple-element.53), channel_id=1, source_target_pairs={{8,0},{16,8},{24,16},{32,24},{40,32},{48,40},{56,48},{9,1},{17,9},... | collective-permute-start | bytes 393224 | tf_op jit(solution)/shard_map/ppermute | solution.py:237
  79.4 1.2 %collective-permute-done.8.below = f32[64,512]{1,0:T(8,128)S(1)} collective-permute-done((f32[64,512]{1,0:T(8,128)S(1)}, f32[64,512]{1,0:T(8,128)S(1)}, u32[]{:S(2)}, u32[]{:S(2)}) %collective-permute-start.8) | collective-permute-done | bytes 131104 | tf_op jit(solution)/shard_map/ppermute | solution.py:237
  80.6 4.0 %collective-permute-done.9.above = f32[64,512]{1,0:T(8,128)S(1)} collective-permute-done((f32[64,512]{1,0:T(8,128)S(1)}, f32[64,512]{1,0:T(8,128)S(1)}, u32[]{:S(2)}, u32[]{:S(2)}) %collective-permute-start.9) | collective-permute-done | bytes 131104 | tf_op jit(solution)/shard_map/ppermute | solution.py:237
  84.6 5.5 %collective-permute-start.10 = (f32[864,128]{1,0:T(8,128)S(1)}, f32[864,128]{1,0:T(8,128)S(1)}, u32[]{:S(2)}, u32[]{:S(2)}) collective-permute-start(f32[864,128]{1,0:T(8,128)S(1)} %bitcast.26), channel_id=1, source_target_pairs={{0,8},{8,0},{1,9},{9,1},{2,10},{10,2},{3,11},{11,3},{4,12},{12,4},... | collective-permute-start | bytes 1327112 | tf_op jit(solution)/shard_map/ppermute | solution.py:333
  90.1 0.7 shard_map.67
  90.8 0.7 collective-permute-done.10.other
  91.5 1.0 %shard_map.68 = f32[864,256]{1,0:T(8,128)} custom-call(s32[1]{0:T(128)} %bitcast.core, f32[864,128]{1,0:T(8,128)S(1)} %bitcast.27, f32[864,128]{1,0:T(8,128)S(1)} %collective-permute-done.10.other), custom_call_target="tpu_custom_call" | custom-call | bytes 1769476 | tf_op jit(solution)/shard_map/pallas_call | solution.py:24
  (16 shorter events, 0.3 us)
Async XLA Ops:
  2.8 13.2 %copy-start.3 = (bf16[32,64]{1,0:T(8,128)(2,1)S(1)}, bf16[32,64]{1,0:T(8,128)(2,1)}, u32[]{:S(2)}) copy-start(bf16[32,64]{1,0:T(8,128)(2,1)} %get-tuple-element.31) | copy-start | bytes 12292
  2.8 16.4 %copy-start.2 = (bf16[32,64]{1,0:T(8,128)(2,1)S(1)}, bf16[32,64]{1,0:T(8,128)(2,1)}, u32[]{:S(2)}) copy-start(bf16[32,64]{1,0:T(8,128)(2,1)} %get-tuple-element.32) | copy-start | bytes 12292
  2.8 21.1 %copy-start.1 = (bf16[1,8,64,32]{2,3,1,0:T(8,128)(2,1)S(1)}, bf16[1,8,64,32]{2,3,1,0:T(8,128)(2,1)}, u32[]{:S(2)}) copy-start(bf16[1,8,64,32]{2,3,1,0:T(8,128)(2,1)} %param.3) | copy-start | bytes 98308
  2.8 29.8 %all-to-all-start = ((bf16[8,32,1536]{2,1,0:T(8,128)(2,1)}), bf16[8,32,1536]{2,1,0:T(8,128)(2,1)S(1)}, u32[]{:S(2)}, u32[]{:S(2)}) async-start(bf16[8,32,1536]{2,1,0:T(8,128)(2,1)} %get-tuple-element.33), calls=%async_computation | async-start | bytes 1572864 | tf_op jit(solution)/shard_map/all_to_all | solution.py:280
  16.0 4.5 %collective-permute-start = (bf16[32,64]{1,0:T(8,128)(2,1)S(1)}, bf16[32,64]{1,0:T(8,128)(2,1)S(1)}, u32[]{:S(2)}, u32[]{:S(2)}) collective-permute-start(bf16[32,64]{1,0:T(8,128)(2,1)S(1)} %copy-done.3), channel_id=1, source_target_pairs={{0,1},{1,2},{2,3},{3,4},{4,5},{5,6},{6,7},{8,9},{9,10},{10,11},{11... | collective-permute-start | bytes 12296 | tf_op jit(solution)/shard_map/ppermute | solution.py:237
  19.2 4.7 %collective-permute-start.1 = (bf16[32,64]{1,0:T(8,128)(2,1)S(1)}, bf16[32,64]{1,0:T(8,128)(2,1)S(1)}, u32[]{:S(2)}, u32[]{:S(2)}) collective-permute-start(bf16[32,64]{1,0:T(8,128)(2,1)S(1)} %copy-done.2), channel_id=1, source_target_pairs={{1,0},{2,1},{3,2},{4,3},{5,4},{6,5},{7,6},{9,8},{10,9},{11,10},{12... | collective-permute-start | bytes 12296 | tf_op jit(solution)/shard_map/ppermute | solution.py:237
  24.0 7.3 %collective-permute-start.3 = (bf16[32,640]{1,0:T(8,128)(2,1)S(1)}, bf16[32,640]{1,0:T(8,128)(2,1)S(1)}, u32[]{:S(2)}, u32[]{:S(2)}) collective-permute-start(bf16[32,640]{1,0:T(8,128)(2,1)S(1)} %shard_map.59.refs_1_), channel_id=1, source_target_pairs={{8,0},{16,8},{24,16},{32,24},{40,32},{48,40},{56,48},{9,1},{17,9},... | collective-permute-start | bytes 122888 | tf_op jit(solution)/shard_map/ppermute | solution.py:237
  28.2 4.1 %collective-permute-start.2 = (bf16[32,640]{1,0:T(8,128)(2,1)S(1)}, bf16[32,640]{1,0:T(8,128)(2,1)S(1)}, u32[]{:S(2)}, u32[]{:S(2)}) collective-permute-start(bf16[32,640]{1,0:T(8,128)(2,1)S(1)} %shard_map.59.refs_1_), channel_id=1, source_target_pairs={{0,8},{8,16},{16,24},{24,32},{32,40},{40,48},{48,56},{1,9},{9,17},... | collective-permute-start | bytes 122888 | tf_op jit(solution)/shard_map/ppermute | solution.py:237
  33.1 4.8 %collective-permute-start.4 = (f32[864,128]{1,0:T(8,128)S(1)}, f32[864,128]{1,0:T(8,128)S(1)}, u32[]{:S(2)}, u32[]{:S(2)}) collective-permute-start(f32[864,128]{1,0:T(8,128)S(1)} %get-tuple-element.35), channel_id=1, source_target_pairs={{0,8},{8,0},{1,9},{9,1},{2,10},{10,2},{3,11},{11,3},{4,12},{12,4},... | collective-permute-start | bytes 1327112 | tf_op jit(solution)/shard_map/ppermute | solution.py:298
  38.7 12.4 %copy-start = (bf16[27,32,256]{2,1,0:T(8,128)(2,1)S(1)}, bf16[27,32,256]{2,1,0:T(8,128)(2,1)}, u32[]{:S(2)}) copy-start(bf16[27,32,256]{2,1,0:T(8,128)(2,1)} %param.4) | copy-start | bytes 1327108
  38.7 23.2 %all-to-all-start.1 = ((f32[864,1,128]{2,1,0:T(1,128)}), f32[864,1,128]{2,1,0:T(1,128)S(1)}, u32[]{:S(2)}, u32[]{:S(2)}) async-start(f32[864,1,128]{2,1,0:T(1,128)} %bitcast.8), calls=%async_computation.1 | async-start | bytes 884736 | tf_op jit(solution)/shard_map/all_to_all | solution.py:242
  48.5 3.7 %collective-permute-start.5 = (bf16[256,448]{1,0:T(8,128)(2,1)S(1)}, bf16[256,448]{1,0:T(8,128)(2,1)S(1)}, u32[]{:S(2)}, u32[]{:S(2)}) collective-permute-start(bf16[256,448]{1,0:T(8,128)(2,1)S(1)} %get-tuple-element.39.mine), channel_id=1, source_target_pairs={{0,8},{8,0},{1,9},{9,1},{2,10},{10,2},{3,11},{11,3},{4,12},{12,4},... | collective-permute-start | bytes 688136 | tf_op jit(solution)/shard_map/ppermute | solution.py:302
  53.4 4.7 %collective-permute-start.6 = (f32[96,128]{1,0:T(8,128)S(1)}, f32[96,128]{1,0:T(8,128)S(1)}, u32[]{:S(2)}, u32[]{:S(2)}) collective-permute-start(f32[96,128]{1,0:T(8,128)S(1)} %get-tuple-element.43), channel_id=1, source_target_pairs={{0,1},{1,2},{2,3},{3,4},{4,5},{5,6},{6,7},{8,9},{9,10},{10,11},{11... | collective-permute-start | bytes 147464 | tf_op jit(solution)/shard_map/ppermute | solution.py:237
  56.8 5.1 %collective-permute-start.7 = (f32[96,128]{1,0:T(8,128)S(1)}, f32[96,128]{1,0:T(8,128)S(1)}, u32[]{:S(2)}, u32[]{:S(2)}) collective-permute-start(f32[96,128]{1,0:T(8,128)S(1)} %get-tuple-element.44), channel_id=1, source_target_pairs={{1,0},{2,1},{3,2},{4,3},{5,4},{6,5},{7,6},{9,8},{10,9},{11,10},{12... | collective-permute-start | bytes 147464 | tf_op jit(solution)/shard_map/ppermute | solution.py:237
  62.8 21.8 %all-to-all-start.2 = ((f32[864,1,128]{2,1,0:T(1,128)}), f32[864,1,128]{2,1,0:T(1,128)S(1)}, u32[]{:S(2)}, u32[]{:S(2)}) async-start(f32[864,1,128]{2,1,0:T(1,128)} %bitcast.11), calls=%async_computation.2 | async-start | bytes 884736 | tf_op jit(solution)/shard_map/all_to_all | solution.py:242
  72.1 8.5 %collective-permute-start.8 = (f32[64,512]{1,0:T(8,128)S(1)}, f32[64,512]{1,0:T(8,128)S(1)}, u32[]{:S(2)}, u32[]{:S(2)}) collective-permute-start(f32[64,512]{1,0:T(8,128)S(1)} %get-tuple-element.52), channel_id=1, source_target_pairs={{0,8},{8,16},{16,24},{24,32},{32,40},{40,48},{48,56},{1,9},{9,17},... | collective-permute-start | bytes 393224 | tf_op jit(solution)/shard_map/ppermute | solution.py:237
  77.5 7.1 %collective-permute-start.9 = (f32[64,512]{1,0:T(8,128)S(1)}, f32[64,512]{1,0:T(8,128)S(1)}, u32[]{:S(2)}, u32[]{:S(2)}) collective-permute-start(f32[64,512]{1,0:T(8,128)S(1)} %get-tuple-element.53), channel_id=1, source_target_pairs={{8,0},{16,8},{24,16},{32,24},{40,32},{48,40},{56,48},{9,1},{17,9},... | collective-permute-start | bytes 393224 | tf_op jit(solution)/shard_map/ppermute | solution.py:237
  84.6 6.9 %collective-permute-start.10 = (f32[864,128]{1,0:T(8,128)S(1)}, f32[864,128]{1,0:T(8,128)S(1)}, u32[]{:S(2)}, u32[]{:S(2)}) collective-permute-start(f32[864,128]{1,0:T(8,128)S(1)} %bitcast.26), channel_id=1, source_target_pairs={{0,8},{8,0},{1,9},{9,1},{2,10},{10,2},{3,11},{11,3},{4,12},{12,4},... | collective-permute-start | bytes 1327112 | tf_op jit(solution)/shard_map/ppermute | solution.py:333

commit v9 on v7

--- a/solution.py
+++ b/solution.py
@@ -15,7 +15,7 @@
 PARAMS = pltpu.CompilerParams(vmem_limit_bytes=16 * 2**20)
 
 
-def call(kernel, outs, flops, *args):
+def call(kernel, outs, flops, *args, scratch=()):
     moved = sum(a.size * a.dtype.itemsize for a in args)
     moved += sum(math.prod(s) * jnp.dtype(d).itemsize for s, d in outs)
     specs = [
@@ -26,6 +26,7 @@
         out_shape=[jax.ShapeDtypeStruct(s, d) for s, d in outs],
         in_specs=specs,
         out_specs=[pl.BlockSpec(memory_space=pltpu.VMEM) for _ in outs],
+        scratch_shapes=list(scratch),
         compiler_params=PARAMS,
         cost_estimate=pl.CostEstimate(flops=flops, bytes_accessed=moved, transcendentals=0),
     )(*args)
@@ -169,7 +170,8 @@
     ends[...], _ = store_spread(spread(z, -1, own, k), middle)
 
 
-def spread_volume(z, received, k_out, g_ends, middle, up, down):
+def spread_volume(z, core, k_mine, k_other, received, g_ends, middle, up, down, k_out):
+    weights_by_output(core, k_mine, k_other, k_out)
     cells = middle.shape[1]
     own = by_chan(received, cells, cells)
     ends, turned = store_spread(spread(z, 1, own, k_out), middle)
@@ -313,9 +315,16 @@
         spread_volume(z, *refs)
 
     g_middle, g_ends = call(from_cotangent, [middle, ends], work, received, k)
-    (k_out,) = call(weights_by_output, [((taps * c, total), BF16)], 0, core, k_mine, k_other)
     v_middle, up, down = call(
-        from_volume, [middle, ends, ends], work, received, k_out, g_ends
+        from_volume,
+        [middle, ends, ends],
+        work,
+        core,
+        k_mine,
+        k_other,
+        received,
+        g_ends,
+        scratch=[pltpu.VMEM((taps * c, total), BF16)],
     )
     before, after = neighbours(up, down, "sy")
     parts, before, after = lax.optimization_barrier((parts, before, after))

time: 93.1 us -> 93.3 us (level)
    pallas_call x11 -> x10, Pallas kernels: 6.15 us -> 6.36 us  [call(): pl.pallas_call(kernel, out_shape=[jax.ShapeDtypeStruct(s, d) for s, d in...]
  transfers between devices with their start and end apart: 14 -> 14, of which waited for: 8 -> 8; matrix products, arithmetic and copies ran while one was open for 0% -> 0% of each run, Pallas kernels for 3% -> 4%
where the time goes in v9:
time: 93.3 us; the launch traced here: 92.5 us
  starting transfers between devices  67.3 us (72%)
  waiting for transfers between devices  16 us (17%)
  Pallas kernels  8.4 us (9%)
    all_to_all x2, starting transfers between devices, exchange_rows(): return lax.all_to_all(apart, axis, 0, 0, tiled=True).reshape(value.shape)  19 us
    ppermute x4, starting transfers between devices, neighbours(): lax.ppermute(value_up, axis, up)  15 us
    all_to_all x1, starting transfers between devices, body(): lax.all_to_all(sends, 'chan', 0, 0, axis_index_groups=[turn(groups)], til...  13.2 us
    ppermute x4, waiting for transfers between devices, neighbours(): lax.ppermute(value_down, axis, down)  11.2 us
    ppermute x4, starting transfers between devices, neighbours(): lax.ppermute(value_down, axis, down)  8.7 us
    pallas_call x10, Pallas kernels, call(): pl.pallas_call(kernel, out_shape=[jax.ShapeDtypeStruct(s, d) for s, d in...  6.36 us
    ppermute x1, starting transfers between devices, body(): other = lax.ppermute(mine, 'core', swap)  5.48 us
    ppermute x1, starting transfers between devices, body(): lax.ppermute(send, 'core', swap)  3.36 us
  transfers between devices with their start and end apart: 14, of which 8 were waited for; matrix products, arithmetic and copies ran while one was open for 0% of the time, Pallas kernels for 4%

profile of v9, /device:TPU:1, one launch (start us, length us, event | category | flops | bytes accessed | tf_op | source)
XLA Modules:
  0.0 92.5 jit_solution(742589205750961764)
XLA Ops:
  0.6 2.0 %shard_map.58 = (bf16[32,64]{1,0:T(8,128)(2,1)}, bf16[32,64]{1,0:T(8,128)(2,1)}, bf16[8,32,1536]{2,1,0:T(8,128)(2,1)}) custom-call(s32[1]{0:T(128)} %bitcast.core.refs_0_, bf16[8,32,64]{2,1,0:T(8,128)(2,1)} %bitcast.28, bf16[8,32,64]{2,1,0:T(8,128)(2,1)} %bitcast.31, bf16[864,256]{1,0:T(8,128)(2,1)} %bitcast.24), custom_call_target="tpu_custom_call" | custom-call | bytes 1572864 | tf_op jit(solution)/shard_map/pallas_call | solution.py:268
  2.7 13.2 %all-to-all-start = ((bf16[8,32,1536]{2,1,0:T(8,128)(2,1)}), bf16[8,32,1536]{2,1,0:T(8,128)(2,1)S(1)}, u32[]{:S(2)}, u32[]{:S(2)}) async-start(bf16[8,32,1536]{2,1,0:T(8,128)(2,1)} %get-tuple-element.33), calls=%async_computation | async-start | bytes 1572864 | tf_op jit(solution)/shard_map/all_to_all | solution.py:286
  15.9 3.2 %collective-permute-start = (bf16[32,64]{1,0:T(8,128)(2,1)S(1)}, bf16[32,64]{1,0:T(8,128)(2,1)S(1)}, u32[]{:S(2)}, u32[]{:S(2)}) collective-permute-start(bf16[32,64]{1,0:T(8,128)(2,1)S(1)} %copy-done.3), channel_id=1, source_target_pairs={{0,1},{1,2},{2,3},{3,4},{4,5},{5,6},{6,7},{8,9},{9,10},{10,11},{11... | collective-permute-start | bytes 12296 | tf_op jit(solution)/shard_map/ppermute | solution.py:243
  19.1 1.3 %collective-permute-start.1 = (bf16[32,64]{1,0:T(8,128)(2,1)S(1)}, bf16[32,64]{1,0:T(8,128)(2,1)S(1)}, u32[]{:S(2)}, u32[]{:S(2)}) collective-permute-start(bf16[32,64]{1,0:T(8,128)(2,1)S(1)} %copy-done.2), channel_id=1, source_target_pairs={{1,0},{2,1},{3,2},{4,3},{5,4},{6,5},{7,6},{9,8},{10,9},{11,10},{12... | collective-permute-start | bytes 12296 | tf_op jit(solution)/shard_map/ppermute | solution.py:243
  20.4 3.4 %collective-permute-done.1.after = bf16[32,64]{1,0:T(8,128)(2,1)S(1)} collective-permute-done((bf16[32,64]{1,0:T(8,128)(2,1)S(1)}, bf16[32,64]{1,0:T(8,128)(2,1)S(1)}, u32[]{:S(2)}, u32[]{:S(2)}) %collective-permute-start.1) | collective-permute-done | bytes 4128 | tf_op jit(solution)/shard_map/ppermute | solution.py:243
  23.9 4.2 %collective-permute-start.3 = (bf16[32,640]{1,0:T(8,128)(2,1)S(1)}, bf16[32,640]{1,0:T(8,128)(2,1)S(1)}, u32[]{:S(2)}, u32[]{:S(2)}) collective-permute-start(bf16[32,640]{1,0:T(8,128)(2,1)S(1)} %shard_map.59.refs_1_), channel_id=1, source_target_pairs={{8,0},{16,8},{24,16},{32,24},{40,32},{48,40},{56,48},{9,1},{17,9},... | collective-permute-start | bytes 122888 | tf_op jit(solution)/shard_map/ppermute | solution.py:243
  28.1 3.0 %collective-permute-start.2 = (bf16[32,640]{1,0:T(8,128)(2,1)S(1)}, bf16[32,640]{1,0:T(8,128)(2,1)S(1)}, u32[]{:S(2)}, u32[]{:S(2)}) collective-permute-start(bf16[32,640]{1,0:T(8,128)(2,1)S(1)} %shard_map.59.refs_1_), channel_id=1, source_target_pairs={{0,8},{8,16},{16,24},{24,32},{32,40},{40,48},{48,56},{1,9},{9,17},... | collective-permute-start | bytes 122888 | tf_op jit(solution)/shard_map/ppermute | solution.py:243
  31.1 1.0 %collective-permute-done.2.refs_0_ = bf16[32,640]{1,0:T(8,128)(2,1)S(1)} collective-permute-done((bf16[32,640]{1,0:T(8,128)(2,1)S(1)}, bf16[32,640]{1,0:T(8,128)(2,1)S(1)}, u32[]{:S(2)}, u32[]{:S(2)}) %collective-permute-start.2) | collective-permute-done | bytes 40992 | tf_op jit(solution)/shard_map/ppermute | solution.py:243
  32.2 0.3 shard_map.60.columns
  32.5 0.4 shard_map.61
  33.0 3.4 %collective-permute-start.4 = (f32[864,128]{1,0:T(8,128)S(1)}, f32[864,128]{1,0:T(8,128)S(1)}, u32[]{:S(2)}, u32[]{:S(2)}) collective-permute-start(f32[864,128]{1,0:T(8,128)S(1)} %get-tuple-element.35), channel_id=1, source_target_pairs={{0,8},{8,0},{1,9},{9,1},{2,10},{10,2},{3,11},{11,3},{4,12},{12,4},... | collective-permute-start | bytes 1327112 | tf_op jit(solution)/shard_map/ppermute | solution.py:304
  36.3 1.4 %collective-permute-done.4.other = f32[864,128]{1,0:T(8,128)S(1)} collective-permute-done((f32[864,128]{1,0:T(8,128)S(1)}, f32[864,128]{1,0:T(8,128)S(1)}, u32[]{:S(2)}, u32[]{:S(2)}) %collective-permute-start.4) | collective-permute-done | bytes 442400 | tf_op jit(solution)/shard_map/ppermute | solution.py:304
  37.7 0.8 shard_map.62
  38.5 9.8 %all-to-all-start.1 = ((f32[864,1,128]{2,1,0:T(1,128)}), f32[864,1,128]{2,1,0:T(1,128)S(1)}, u32[]{:S(2)}, u32[]{:S(2)}) async-start(f32[864,1,128]{2,1,0:T(1,128)} %bitcast.8), calls=%async_computation.1 | async-start | bytes 884736 | tf_op jit(solution)/shard_map/all_to_all | solution.py:248
  48.3 2.6 %collective-permute-start.5 = (bf16[256,448]{1,0:T(8,128)(2,1)S(1)}, bf16[256,448]{1,0:T(8,128)(2,1)S(1)}, u32[]{:S(2)}, u32[]{:S(2)}) collective-permute-start(bf16[256,448]{1,0:T(8,128)(2,1)S(1)} %get-tuple-element.39.refs_1_), channel_id=1, source_target_pairs={{0,8},{8,0},{1,9},{9,1},{2,10},{10,2},{3,11},{11,3},{4,12},{12,4},... | collective-permute-start | bytes 688136 | tf_op jit(solution)/shard_map/ppermute | solution.py:308
  50.9 0.7 shard_map.63
  51.6 0.4 collective-permute-done.5.refs_2_
  52.1 1.4 %shard_map.64 = (f32[96,512]{1,0:T(8,128)S(1)}, f32[96,128]{1,0:T(8,128)S(1)}, f32[96,128]{1,0:T(8,128)S(1)}) custom-call(s32[1]{0:T(128)} %bitcast.core.refs_0_, bf16[256,448]{1,0:T(8,128)(2,1)S(1)} %get-tuple-element.39.refs_1_, bf16[256,448]{1,0:T(8,128)(2,1)S(1)} %collective-permute-done.5.refs_2_, ...), custom_call_target="tpu_custom_call" | custom-call | flops 226492416 | bytes 1589252 | tf_op jit(solution)/shard_map/pallas_call | solution.py:24
  53.5 3.4 %collective-permute-start.6 = (f32[96,128]{1,0:T(8,128)S(1)}, f32[96,128]{1,0:T(8,128)S(1)}, u32[]{:S(2)}, u32[]{:S(2)}) collective-permute-start(f32[96,128]{1,0:T(8,128)S(1)} %get-tuple-element.43), channel_id=1, source_target_pairs={{0,1},{1,2},{2,3},{3,4},{4,5},{5,6},{6,7},{8,9},{9,10},{10,11},{11... | collective-permute-start | bytes 147464 | tf_op jit(solution)/shard_map/ppermute | solution.py:243
  56.9 1.3 %collective-permute-start.7 = (f32[96,128]{1,0:T(8,128)S(1)}, f32[96,128]{1,0:T(8,128)S(1)}, u32[]{:S(2)}, u32[]{:S(2)}) collective-permute-start(f32[96,128]{1,0:T(8,128)S(1)} %get-tuple-element.44), channel_id=1, source_target_pairs={{1,0},{2,1},{3,2},{4,3},{5,4},{6,5},{7,6},{9,8},{10,9},{11,10},{12... | collective-permute-start | bytes 147464 | tf_op jit(solution)/shard_map/ppermute | solution.py:243
  58.2 3.8 %collective-permute-done.7.after = f32[96,128]{1,0:T(8,128)S(1)} collective-permute-done((f32[96,128]{1,0:T(8,128)S(1)}, f32[96,128]{1,0:T(8,128)S(1)}, u32[]{:S(2)}, u32[]{:S(2)}) %collective-permute-start.7) | collective-permute-done | bytes 49184 | tf_op jit(solution)/shard_map/ppermute | solution.py:243
  62.0 0.8 shard_map.65
  62.8 9.2 %all-to-all-start.2 = ((f32[864,1,128]{2,1,0:T(1,128)}), f32[864,1,128]{2,1,0:T(1,128)S(1)}, u32[]{:S(2)}, u32[]{:S(2)}) async-start(f32[864,1,128]{2,1,0:T(1,128)} %bitcast.11), calls=%async_computation.2 | async-start | bytes 884736 | tf_op jit(solution)/shard_map/all_to_all | solution.py:248
  72.0 0.1 shard_map.66
  72.1 5.4 %collective-permute-start.8 = (f32[64,512]{1,0:T(8,128)S(1)}, f32[64,512]{1,0:T(8,128)S(1)}, u32[]{:S(2)}, u32[]{:S(2)}) collective-permute-start(f32[64,512]{1,0:T(8,128)S(1)} %get-tuple-element.52), channel_id=1, source_target_pairs={{0,8},{8,16},{16,24},{24,32},{32,40},{40,48},{48,56},{1,9},{9,17},... | collective-permute-start | bytes 393224 | tf_op jit(solution)/shard_map/ppermute | solution.py:243
  77.5 1.9 %collective-permute-start.9 = (f32[64,512]{1,0:T(8,128)S(1)}, f32[64,512]{1,0:T(8,128)S(1)}, u32[]{:S(2)}, u32[]{:S(2)}) collective-permute-start(f32[64,512]{1,0:T(8,128)S(1)} %get-tuple-element.53), channel_id=1, source_target_pairs={{8,0},{16,8},{24,16},{32,24},{40,32},{48,40},{56,48},{9,1},{17,9},... | collective-permute-start | bytes 393224 | tf_op jit(solution)/shard_map/ppermute | solution.py:243
  79.5 1.2 %collective-permute-done.8.below = f32[64,512]{1,0:T(8,128)S(1)} collective-permute-done((f32[64,512]{1,0:T(8,128)S(1)}, f32[64,512]{1,0:T(8,128)S(1)}, u32[]{:S(2)}, u32[]{:S(2)}) %collective-permute-start.8) | collective-permute-done | bytes 131104 | tf_op jit(solution)/shard_map/ppermute | solution.py:243
  80.7 4.0 %collective-permute-done.9.above = f32[64,512]{1,0:T(8,128)S(1)} collective-permute-done((f32[64,512]{1,0:T(8,128)S(1)}, f32[64,512]{1,0:T(8,128)S(1)}, u32[]{:S(2)}, u32[]{:S(2)}) %collective-permute-start.9) | collective-permute-done | bytes 131104 | tf_op jit(solution)/shard_map/ppermute | solution.py:243
  84.7 5.5 %collective-permute-start.10 = (f32[864,128]{1,0:T(8,128)S(1)}, f32[864,128]{1,0:T(8,128)S(1)}, u32[]{:S(2)}, u32[]{:S(2)}) collective-permute-start(f32[864,128]{1,0:T(8,128)S(1)} %bitcast.26), channel_id=1, source_target_pairs={{0,8},{8,0},{1,9},{9,1},{2,10},{10,2},{3,11},{11,3},{4,12},{12,4},... | collective-permute-start | bytes 1327112 | tf_op jit(solution)/shard_map/ppermute | solution.py:346
  90.2 0.7 shard_map.67
  90.9 0.7 collective-permute-done.10.other
  91.6 1.0 %shard_map.68 = f32[864,256]{1,0:T(8,128)} custom-call(s32[1]{0:T(128)} %bitcast.core.refs_0_, f32[864,128]{1,0:T(8,128)S(1)} %bitcast.27, f32[864,128]{1,0:T(8,128)S(1)} %collective-permute-done.10.other), custom_call_target="tpu_custom_call" | custom-call | bytes 1769476 | tf_op jit(solution)/shard_map/pallas_call | solution.py:24
  (15 shorter events, 0.2 us)
Async XLA Ops:
  2.7 13.2 %copy-start.3 = (bf16[32,64]{1,0:T(8,128)(2,1)S(1)}, bf16[32,64]{1,0:T(8,128)(2,1)}, u32[]{:S(2)}) copy-start(bf16[32,64]{1,0:T(8,128)(2,1)} %get-tuple-element.31) | copy-start | bytes 12292
  2.7 16.4 %copy-start.2 = (bf16[32,64]{1,0:T(8,128)(2,1)S(1)}, bf16[32,64]{1,0:T(8,128)(2,1)}, u32[]{:S(2)}) copy-start(bf16[32,64]{1,0:T(8,128)(2,1)} %get-tuple-element.32) | copy-start | bytes 12292
  2.7 21.1 %copy-start.1 = (bf16[1,8,64,32]{2,3,1,0:T(8,128)(2,1)S(1)}, bf16[1,8,64,32]{2,3,1,0:T(8,128)(2,1)}, u32[]{:S(2)}) copy-start(bf16[1,8,64,32]{2,3,1,0:T(8,128)(2,1)} %param.3) | copy-start | bytes 98308
  2.7 29.8 %all-to-all-start = ((bf16[8,32,1536]{2,1,0:T(8,128)(2,1)}), bf16[8,32,1536]{2,1,0:T(8,128)(2,1)S(1)}, u32[]{:S(2)}, u32[]{:S(2)}) async-start(bf16[8,32,1536]{2,1,0:T(8,128)(2,1)} %get-tuple-element.33), calls=%async_computation | async-start | bytes 1572864 | tf_op jit(solution)/shard_map/all_to_all | solution.py:286
  15.9 4.5 %collective-permute-start = (bf16[32,64]{1,0:T(8,128)(2,1)S(1)}, bf16[32,64]{1,0:T(8,128)(2,1)S(1)}, u32[]{:S(2)}, u32[]{:S(2)}) collective-permute-start(bf16[32,64]{1,0:T(8,128)(2,1)S(1)} %copy-done.3), channel_id=1, source_target_pairs={{0,1},{1,2},{2,3},{3,4},{4,5},{5,6},{6,7},{8,9},{9,10},{10,11},{11... | collective-permute-start | bytes 12296 | tf_op jit(solution)/shard_map/ppermute | solution.py:243
  19.1 4.7 %collective-permute-start.1 = (bf16[32,64]{1,0:T(8,128)(2,1)S(1)}, bf16[32,64]{1,0:T(8,128)(2,1)S(1)}, u32[]{:S(2)}, u32[]{:S(2)}) collective-permute-start(bf16[32,64]{1,0:T(8,128)(2,1)S(1)} %copy-done.2), channel_id=1, source_target_pairs={{1,0},{2,1},{3,2},{4,3},{5,4},{6,5},{7,6},{9,8},{10,9},{11,10},{12... | collective-permute-start | bytes 12296 | tf_op jit(solution)/shard_map/ppermute | solution.py:243
  23.9 7.3 %collective-permute-start.3 = (bf16[32,640]{1,0:T(8,128)(2,1)S(1)}, bf16[32,640]{1,0:T(8,128)(2,1)S(1)}, u32[]{:S(2)}, u32[]{:S(2)}) collective-permute-start(bf16[32,640]{1,0:T(8,128)(2,1)S(1)} %shard_map.59.refs_1_), channel_id=1, source_target_pairs={{8,0},{16,8},{24,16},{32,24},{40,32},{48,40},{56,48},{9,1},{17,9},... | collective-permute-start | bytes 122888 | tf_op jit(solution)/shard_map/ppermute | solution.py:243
  28.1 4.1 %collective-permute-start.2 = (bf16[32,640]{1,0:T(8,128)(2,1)S(1)}, bf16[32,640]{1,0:T(8,128)(2,1)S(1)}, u32[]{:S(2)}, u32[]{:S(2)}) collective-permute-start(bf16[32,640]{1,0:T(8,128)(2,1)S(1)} %shard_map.59.refs_1_), channel_id=1, source_target_pairs={{0,8},{8,16},{16,24},{24,32},{32,40},{40,48},{48,56},{1,9},{9,17},... | collective-permute-start | bytes 122888 | tf_op jit(solution)/shard_map/ppermute | solution.py:243
  33.0 4.8 %collective-permute-start.4 = (f32[864,128]{1,0:T(8,128)S(1)}, f32[864,128]{1,0:T(8,128)S(1)}, u32[]{:S(2)}, u32[]{:S(2)}) collective-permute-start(f32[864,128]{1,0:T(8,128)S(1)} %get-tuple-element.35), channel_id=1, source_target_pairs={{0,8},{8,0},{1,9},{9,1},{2,10},{10,2},{3,11},{11,3},{4,12},{12,4},... | collective-permute-start | bytes 1327112 | tf_op jit(solution)/shard_map/ppermute | solution.py:304
  38.5 12.4 %copy-start = (bf16[27,32,256]{2,1,0:T(8,128)(2,1)S(1)}, bf16[27,32,256]{2,1,0:T(8,128)(2,1)}, u32[]{:S(2)}) copy-start(bf16[27,32,256]{2,1,0:T(8,128)(2,1)} %param.4) | copy-start | bytes 1327108
  38.5 23.5 %all-to-all-start.1 = ((f32[864,1,128]{2,1,0:T(1,128)}), f32[864,1,128]{2,1,0:T(1,128)S(1)}, u32[]{:S(2)}, u32[]{:S(2)}) async-start(f32[864,1,128]{2,1,0:T(1,128)} %bitcast.8), calls=%async_computation.1 | async-start | bytes 884736 | tf_op jit(solution)/shard_map/all_to_all | solution.py:248
  48.3 3.7 %collective-permute-start.5 = (bf16[256,448]{1,0:T(8,128)(2,1)S(1)}, bf16[256,448]{1,0:T(8,128)(2,1)S(1)}, u32[]{:S(2)}, u32[]{:S(2)}) collective-permute-start(bf16[256,448]{1,0:T(8,128)(2,1)S(1)} %get-tuple-element.39.refs_1_), channel_id=1, source_target_pairs={{0,8},{8,0},{1,9},{9,1},{2,10},{10,2},{3,11},{11,3},{4,12},{12,4},... | collective-permute-start | bytes 688136 | tf_op jit(solution)/shard_map/ppermute | solution.py:308
  53.5 4.7 %collective-permute-start.6 = (f32[96,128]{1,0:T(8,128)S(1)}, f32[96,128]{1,0:T(8,128)S(1)}, u32[]{:S(2)}, u32[]{:S(2)}) collective-permute-start(f32[96,128]{1,0:T(8,128)S(1)} %get-tuple-element.43), channel_id=1, source_target_pairs={{0,1},{1,2},{2,3},{3,4},{4,5},{5,6},{6,7},{8,9},{9,10},{10,11},{11... | collective-permute-start | bytes 147464 | tf_op jit(solution)/shard_map/ppermute | solution.py:243
  56.9 5.1 %collective-permute-start.7 = (f32[96,128]{1,0:T(8,128)S(1)}, f32[96,128]{1,0:T(8,128)S(1)}, u32[]{:S(2)}, u32[]{:S(2)}) collective-permute-start(f32[96,128]{1,0:T(8,128)S(1)} %get-tuple-element.44), channel_id=1, source_target_pairs={{1,0},{2,1},{3,2},{4,3},{5,4},{6,5},{7,6},{9,8},{10,9},{11,10},{12... | collective-permute-start | bytes 147464 | tf_op jit(solution)/shard_map/ppermute | solution.py:243
  62.8 21.8 %all-to-all-start.2 = ((f32[864,1,128]{2,1,0:T(1,128)}), f32[864,1,128]{2,1,0:T(1,128)S(1)}, u32[]{:S(2)}, u32[]{:S(2)}) async-start(f32[864,1,128]{2,1,0:T(1,128)} %bitcast.11), calls=%async_computation.2 | async-start | bytes 884736 | tf_op jit(solution)/shard_map/all_to_all | solution.py:248
  72.1 8.6 %collective-permute-start.8 = (f32[64,512]{1,0:T(8,128)S(1)}, f32[64,512]{1,0:T(8,128)S(1)}, u32[]{:S(2)}, u32[]{:S(2)}) collective-permute-start(f32[64,512]{1,0:T(8,128)S(1)} %get-tuple-element.52), channel_id=1, source_target_pairs={{0,8},{8,16},{16,24},{24,32},{32,40},{40,48},{48,56},{1,9},{9,17},... | collective-permute-start | bytes 393224 | tf_op jit(solution)/shard_map/ppermute | solution.py:243
  77.5 7.1 %collective-permute-start.9 = (f32[64,512]{1,0:T(8,128)S(1)}, f32[64,512]{1,0:T(8,128)S(1)}, u32[]{:S(2)}, u32[]{:S(2)}) collective-permute-start(f32[64,512]{1,0:T(8,128)S(1)} %get-tuple-element.53), channel_id=1, source_target_pairs={{8,0},{16,8},{24,16},{32,24},{40,32},{48,40},{56,48},{9,1},{17,9},... | collective-permute-start | bytes 393224 | tf_op jit(solution)/shard_map/ppermute | solution.py:243
  84.7 6.9 %collective-permute-start.10 = (f32[864,128]{1,0:T(8,128)S(1)}, f32[864,128]{1,0:T(8,128)S(1)}, u32[]{:S(2)}, u32[]{:S(2)}) collective-permute-start(f32[864,128]{1,0:T(8,128)S(1)} %bitcast.26), channel_id=1, source_target_pairs={{0,8},{8,0},{1,9},{9,1},{2,10},{10,2},{3,11},{11,3},{4,12},{12,4},... | collective-permute-start | bytes 1327112 | tf_op jit(solution)/shard_map/ppermute | solution.py:346

commit v10 on v9

--- a/solution.py
+++ b/solution.py
@@ -215,10 +215,6 @@
         out[r] = shifted[:, :z].astype(BF16)
 
 
-def add_halves(keep, other, out):
-    out[...] = keep[...] + other[...]
-
-
 def sum_pieces(scale, pieces, parts, out):
     rows = parts.shape[0] // pieces
     total = parts[:rows]
@@ -301,7 +297,7 @@
         received,
     )
     swap = [(0, 1), (1, 0)]
-    (halves,) = call(add_halves, [(piece, F32)], 0, keep, lax.ppermute(send, "core", swap))
+    halves = keep + lax.ppermute(send, "core", swap)
 
     halves, k_mine, received = lax.optimization_barrier((halves, k_mine, received))
     parts = exchange_rows(halves, ("x", "sy"))

time: 93.3 us -> 93.3 us (level)
    pallas_call x10 -> x9, Pallas kernels: 6.36 us -> 5.56 us  [call(): pl.pallas_call(kernel, out_shape=[jax.ShapeDtypeStruct(s, d) for s, d in...]
where the time goes in v10:
time: 93.3 us; the launch traced here: 92.6 us
  starting transfers between devices  67.3 us (72%)
  waiting for transfers between devices  16 us (17%)
  Pallas kernels  7.6 us (8%)
    all_to_all x2, starting transfers between devices, exchange_rows(): return lax.all_to_all(apart, axis, 0, 0, tiled=True).reshape(value.shape)  19 us
    ppermute x4, starting transfers between devices, neighbours(): lax.ppermute(value_up, axis, up)  15 us
    all_to_all x1, starting transfers between devices, body(): lax.all_to_all(sends, 'chan', 0, 0, axis_index_groups=[turn(groups)], til...  13.2 us
    ppermute x4, waiting for transfers between devices, neighbours(): lax.ppermute(value_down, axis, down)  11.2 us
    ppermute x4, starting transfers between devices, neighbours(): lax.ppermute(value_down, axis, down)  8.7 us
    pallas_call x9, Pallas kernels, call(): pl.pallas_call(kernel, out_shape=[jax.ShapeDtypeStruct(s, d) for s, d in...  5.56 us
    ppermute x1, starting transfers between devices, body(): other = lax.ppermute(mine, 'core', swap)  5.47 us
    ppermute x1, starting transfers between devices, body(): halves = keep + lax.ppermute(send, 'core', swap)  3.36 us
  transfers between devices with their start and end apart: 14, of which 8 were waited for; matrix products, arithmetic and copies ran while one was open for 0% of the time, Pallas kernels for 4%

profile of v10, /device:TPU:1, one launch (start us, length us, event | category | flops | bytes accessed | tf_op | source)
XLA Modules:
  0.0 92.6 jit_solution(7543754526738559549)
XLA Ops:
  0.6 2.0 %shard_map.58 = (bf16[32,64]{1,0:T(8,128)(2,1)}, bf16[32,64]{1,0:T(8,128)(2,1)}, bf16[8,32,1536]{2,1,0:T(8,128)(2,1)}) custom-call(s32[1]{0:T(128)} %bitcast.core.refs_0_, bf16[8,32,64]{2,1,0:T(8,128)(2,1)} %bitcast.28, bf16[8,32,64]{2,1,0:T(8,128)(2,1)} %bitcast.31, bf16[864,256]{1,0:T(8,128)(2,1)} %bitcast.24), custom_call_target="tpu_custom_call" | custom-call | bytes 1572864 | tf_op jit(solution)/shard_map/pallas_call | solution.py:264
  2.7 13.2 %all-to-all-start = ((bf16[8,32,1536]{2,1,0:T(8,128)(2,1)}), bf16[8,32,1536]{2,1,0:T(8,128)(2,1)S(1)}, u32[]{:S(2)}, u32[]{:S(2)}) async-start(bf16[8,32,1536]{2,1,0:T(8,128)(2,1)} %get-tuple-element.33), calls=%async_computation | async-start | bytes 1572864 | tf_op jit(solution)/shard_map/all_to_all | solution.py:282
  15.9 3.2 %collective-permute-start = (bf16[32,64]{1,0:T(8,128)(2,1)S(1)}, bf16[32,64]{1,0:T(8,128)(2,1)S(1)}, u32[]{:S(2)}, u32[]{:S(2)}) collective-permute-start(bf16[32,64]{1,0:T(8,128)(2,1)S(1)} %copy-done.3), channel_id=1, source_target_pairs={{0,1},{1,2},{2,3},{3,4},{4,5},{5,6},{6,7},{8,9},{9,10},{10,11},{11... | collective-permute-start | bytes 12296 | tf_op jit(solution)/shard_map/ppermute | solution.py:239
  19.1 1.3 %collective-permute-start.1 = (bf16[32,64]{1,0:T(8,128)(2,1)S(1)}, bf16[32,64]{1,0:T(8,128)(2,1)S(1)}, u32[]{:S(2)}, u32[]{:S(2)}) collective-permute-start(bf16[32,64]{1,0:T(8,128)(2,1)S(1)} %copy-done.2), channel_id=1, source_target_pairs={{1,0},{2,1},{3,2},{4,3},{5,4},{6,5},{7,6},{9,8},{10,9},{11,10},{12... | collective-permute-start | bytes 12296 | tf_op jit(solution)/shard_map/ppermute | solution.py:239
  20.4 3.4 %collective-permute-done.1.after = bf16[32,64]{1,0:T(8,128)(2,1)S(1)} collective-permute-done((bf16[32,64]{1,0:T(8,128)(2,1)S(1)}, bf16[32,64]{1,0:T(8,128)(2,1)S(1)}, u32[]{:S(2)}, u32[]{:S(2)}) %collective-permute-start.1) | collective-permute-done | bytes 4128 | tf_op jit(solution)/shard_map/ppermute | solution.py:239
  23.9 4.2 %collective-permute-start.3 = (bf16[32,640]{1,0:T(8,128)(2,1)S(1)}, bf16[32,640]{1,0:T(8,128)(2,1)S(1)}, u32[]{:S(2)}, u32[]{:S(2)}) collective-permute-start(bf16[32,640]{1,0:T(8,128)(2,1)S(1)} %shard_map.59.refs_1_), channel_id=1, source_target_pairs={{8,0},{16,8},{24,16},{32,24},{40,32},{48,40},{56,48},{9,1},{17,9},... | collective-permute-start | bytes 122888 | tf_op jit(solution)/shard_map/ppermute | solution.py:239
  28.1 3.0 %collective-permute-start.2 = (bf16[32,640]{1,0:T(8,128)(2,1)S(1)}, bf16[32,640]{1,0:T(8,128)(2,1)S(1)}, u32[]{:S(2)}, u32[]{:S(2)}) collective-permute-start(bf16[32,640]{1,0:T(8,128)(2,1)S(1)} %shard_map.59.refs_1_), channel_id=1, source_target_pairs={{0,8},{8,16},{16,24},{24,32},{32,40},{40,48},{48,56},{1,9},{9,17},... | collective-permute-start | bytes 122888 | tf_op jit(solution)/shard_map/ppermute | solution.py:239
  31.1 1.0 %collective-permute-done.2.refs_0_ = bf16[32,640]{1,0:T(8,128)(2,1)S(1)} collective-permute-done((bf16[32,640]{1,0:T(8,128)(2,1)S(1)}, bf16[32,640]{1,0:T(8,128)(2,1)S(1)}, u32[]{:S(2)}, u32[]{:S(2)}) %collective-permute-start.2) | collective-permute-done | bytes 40992 | tf_op jit(solution)/shard_map/ppermute | solution.py:239
  32.2 0.3 shard_map.60.columns
  32.5 0.4 shard_map.61
  33.0 3.4 %collective-permute-start.4 = (f32[864,128]{1,0:T(8,128)S(1)}, f32[864,128]{1,0:T(8,128)S(1)}, u32[]{:S(2)}, u32[]{:S(2)}) collective-permute-start(f32[864,128]{1,0:T(8,128)S(1)} %get-tuple-element.35), channel_id=1, source_target_pairs={{0,8},{8,0},{1,9},{9,1},{2,10},{10,2},{3,11},{11,3},{4,12},{12,4},... | collective-permute-start | bytes 1327112 | tf_op jit(solution)/shard_map/ppermute | solution.py:300
  36.3 1.4 %collective-permute-done.4 = f32[864,128]{1,0:T(8,128)S(1)} collective-permute-done((f32[864,128]{1,0:T(8,128)S(1)}, f32[864,128]{1,0:T(8,128)S(1)}, u32[]{:S(2)}, u32[]{:S(2)}) %collective-permute-start.4) | collective-permute-done | bytes 442400 | tf_op jit(solution)/shard_map/ppermute | solution.py:300
  37.7 0.8 add.3
  38.6 9.8 %all-to-all-start.1 = ((f32[864,1,128]{2,1,0:T(1,128)}), f32[864,1,128]{2,1,0:T(1,128)S(1)}, u32[]{:S(2)}, u32[]{:S(2)}) async-start(f32[864,1,128]{2,1,0:T(1,128)} %bitcast.8), calls=%async_computation.1 | async-start | bytes 884736 | tf_op jit(solution)/shard_map/all_to_all | solution.py:244
  48.4 2.6 %collective-permute-start.5 = (bf16[256,448]{1,0:T(8,128)(2,1)S(1)}, bf16[256,448]{1,0:T(8,128)(2,1)S(1)}, u32[]{:S(2)}, u32[]{:S(2)}) collective-permute-start(bf16[256,448]{1,0:T(8,128)(2,1)S(1)} %get-tuple-element.39.refs_1_), channel_id=1, source_target_pairs={{0,8},{8,0},{1,9},{9,1},{2,10},{10,2},{3,11},{11,3},{4,12},{12,4},... | collective-permute-start | bytes 688136 | tf_op jit(solution)/shard_map/ppermute | solution.py:304
  50.9 0.7 shard_map.62
  51.7 0.4 collective-permute-done.5.refs_2_
  52.1 1.4 %shard_map.63 = (f32[96,512]{1,0:T(8,128)S(1)}, f32[96,128]{1,0:T(8,128)S(1)}, f32[96,128]{1,0:T(8,128)S(1)}) custom-call(s32[1]{0:T(128)} %bitcast.core.refs_0_, bf16[256,448]{1,0:T(8,128)(2,1)S(1)} %get-tuple-element.39.refs_1_, bf16[256,448]{1,0:T(8,128)(2,1)S(1)} %collective-permute-done.5.refs_2_, ...), custom_call_target="tpu_custom_call" | custom-call | flops 226492416 | bytes 1589252 | tf_op jit(solution)/shard_map/pallas_call | solution.py:24
  53.5 3.4 %collective-permute-start.6 = (f32[96,128]{1,0:T(8,128)S(1)}, f32[96,128]{1,0:T(8,128)S(1)}, u32[]{:S(2)}, u32[]{:S(2)}) collective-permute-start(f32[96,128]{1,0:T(8,128)S(1)} %get-tuple-element.43), channel_id=1, source_target_pairs={{0,1},{1,2},{2,3},{3,4},{4,5},{5,6},{6,7},{8,9},{9,10},{10,11},{11... | collective-permute-start | bytes 147464 | tf_op jit(solution)/shard_map/ppermute | solution.py:239
  56.9 1.3 %collective-permute-start.7 = (f32[96,128]{1,0:T(8,128)S(1)}, f32[96,128]{1,0:T(8,128)S(1)}, u32[]{:S(2)}, u32[]{:S(2)}) collective-permute-start(f32[96,128]{1,0:T(8,128)S(1)} %get-tuple-element.44), channel_id=1, source_target_pairs={{1,0},{2,1},{3,2},{4,3},{5,4},{6,5},{7,6},{9,8},{10,9},{11,10},{12... | collective-permute-start | bytes 147464 | tf_op jit(solution)/shard_map/ppermute | solution.py:239
  58.2 3.8 %collective-permute-done.7.after = f32[96,128]{1,0:T(8,128)S(1)} collective-permute-done((f32[96,128]{1,0:T(8,128)S(1)}, f32[96,128]{1,0:T(8,128)S(1)}, u32[]{:S(2)}, u32[]{:S(2)}) %collective-permute-start.7) | collective-permute-done | bytes 49184 | tf_op jit(solution)/shard_map/ppermute | solution.py:239
  62.0 0.8 shard_map.64
  62.9 9.2 %all-to-all-start.2 = ((f32[864,1,128]{2,1,0:T(1,128)}), f32[864,1,128]{2,1,0:T(1,128)S(1)}, u32[]{:S(2)}, u32[]{:S(2)}) async-start(f32[864,1,128]{2,1,0:T(1,128)} %bitcast.11), calls=%async_computation.2 | async-start | bytes 884736 | tf_op jit(solution)/shard_map/all_to_all | solution.py:244
  72.1 0.1 shard_map.65
  72.2 5.4 %collective-permute-start.8 = (f32[64,512]{1,0:T(8,128)S(1)}, f32[64,512]{1,0:T(8,128)S(1)}, u32[]{:S(2)}, u32[]{:S(2)}) collective-permute-start(f32[64,512]{1,0:T(8,128)S(1)} %get-tuple-element.52), channel_id=1, source_target_pairs={{0,8},{8,16},{16,24},{24,32},{32,40},{40,48},{48,56},{1,9},{9,17},... | collective-permute-start | bytes 393224 | tf_op jit(solution)/shard_map/ppermute | solution.py:239
  77.6 1.9 %collective-permute-start.9 = (f32[64,512]{1,0:T(8,128)S(1)}, f32[64,512]{1,0:T(8,128)S(1)}, u32[]{:S(2)}, u32[]{:S(2)}) collective-permute-start(f32[64,512]{1,0:T(8,128)S(1)} %get-tuple-element.53), channel_id=1, source_target_pairs={{8,0},{16,8},{24,16},{32,24},{40,32},{48,40},{56,48},{9,1},{17,9},... | collective-permute-start | bytes 393224 | tf_op jit(solution)/shard_map/ppermute | solution.py:239
  79.5 1.2 %collective-permute-done.8.below = f32[64,512]{1,0:T(8,128)S(1)} collective-permute-done((f32[64,512]{1,0:T(8,128)S(1)}, f32[64,512]{1,0:T(8,128)S(1)}, u32[]{:S(2)}, u32[]{:S(2)}) %collective-permute-start.8) | collective-permute-done | bytes 131104 | tf_op jit(solution)/shard_map/ppermute | solution.py:239
  80.7 4.0 %collective-permute-done.9.above = f32[64,512]{1,0:T(8,128)S(1)} collective-permute-done((f32[64,512]{1,0:T(8,128)S(1)}, f32[64,512]{1,0:T(8,128)S(1)}, u32[]{:S(2)}, u32[]{:S(2)}) %collective-permute-start.9) | collective-permute-done | bytes 131104 | tf_op jit(solution)/shard_map/ppermute | solution.py:239
  84.7 5.5 %collective-permute-start.10 = (f32[864,128]{1,0:T(8,128)S(1)}, f32[864,128]{1,0:T(8,128)S(1)}, u32[]{:S(2)}, u32[]{:S(2)}) collective-permute-start(f32[864,128]{1,0:T(8,128)S(1)} %bitcast.26), channel_id=1, source_target_pairs={{0,8},{8,0},{1,9},{9,1},{2,10},{10,2},{3,11},{11,3},{4,12},{12,4},... | collective-permute-start | bytes 1327112 | tf_op jit(solution)/shard_map/ppermute | solution.py:342
  90.2 0.7 shard_map.66
  90.9 0.7 collective-permute-done.10.other
  91.6 1.0 %shard_map.67 = f32[864,256]{1,0:T(8,128)} custom-call(s32[1]{0:T(128)} %bitcast.core.refs_0_, f32[864,128]{1,0:T(8,128)S(1)} %bitcast.27, f32[864,128]{1,0:T(8,128)S(1)} %collective-permute-done.10.other), custom_call_target="tpu_custom_call" | custom-call | bytes 1769476 | tf_op jit(solution)/shard_map/pallas_call | solution.py:24
  (15 shorter events, 0.2 us)
Async XLA Ops:
  2.7 13.2 %copy-start.3 = (bf16[32,64]{1,0:T(8,128)(2,1)S(1)}, bf16[32,64]{1,0:T(8,128)(2,1)}, u32[]{:S(2)}) copy-start(bf16[32,64]{1,0:T(8,128)(2,1)} %get-tuple-element.31) | copy-start | bytes 12292
  2.7 16.4 %copy-start.2 = (bf16[32,64]{1,0:T(8,128)(2,1)S(1)}, bf16[32,64]{1,0:T(8,128)(2,1)}, u32[]{:S(2)}) copy-start(bf16[32,64]{1,0:T(8,128)(2,1)} %get-tuple-element.32) | copy-start | bytes 12292
  2.7 21.1 %copy-start.1 = (bf16[1,8,64,32]{2,3,1,0:T(8,128)(2,1)S(1)}, bf16[1,8,64,32]{2,3,1,0:T(8,128)(2,1)}, u32[]{:S(2)}) copy-start(bf16[1,8,64,32]{2,3,1,0:T(8,128)(2,1)} %param.3) | copy-start | bytes 98308
  2.7 29.8 %all-to-all-start = ((bf16[8,32,1536]{2,1,0:T(8,128)(2,1)}), bf16[8,32,1536]{2,1,0:T(8,128)(2,1)S(1)}, u32[]{:S(2)}, u32[]{:S(2)}) async-start(bf16[8,32,1536]{2,1,0:T(8,128)(2,1)} %get-tuple-element.33), calls=%async_computation | async-start | bytes 1572864 | tf_op jit(solution)/shard_map/all_to_all | solution.py:282
  15.9 4.5 %collective-permute-start = (bf16[32,64]{1,0:T(8,128)(2,1)S(1)}, bf16[32,64]{1,0:T(8,128)(2,1)S(1)}, u32[]{:S(2)}, u32[]{:S(2)}) collective-permute-start(bf16[32,64]{1,0:T(8,128)(2,1)S(1)} %copy-done.3), channel_id=1, source_target_pairs={{0,1},{1,2},{2,3},{3,4},{4,5},{5,6},{6,7},{8,9},{9,10},{10,11},{11... | collective-permute-start | bytes 12296 | tf_op jit(solution)/shard_map/ppermute | solution.py:239
  19.1 4.7 %collective-permute-start.1 = (bf16[32,64]{1,0:T(8,128)(2,1)S(1)}, bf16[32,64]{1,0:T(8,128)(2,1)S(1)}, u32[]{:S(2)}, u32[]{:S(2)}) collective-permute-start(bf16[32,64]{1,0:T(8,128)(2,1)S(1)} %copy-done.2), channel_id=1, source_target_pairs={{1,0},{2,1},{3,2},{4,3},{5,4},{6,5},{7,6},{9,8},{10,9},{11,10},{12... | collective-permute-start | bytes 12296 | tf_op jit(solution)/shard_map/ppermute | solution.py:239
  23.9 7.3 %collective-permute-start.3 = (bf16[32,640]{1,0:T(8,128)(2,1)S(1)}, bf16[32,640]{1,0:T(8,128)(2,1)S(1)}, u32[]{:S(2)}, u32[]{:S(2)}) collective-permute-start(bf16[32,640]{1,0:T(8,128)(2,1)S(1)} %shard_map.59.refs_1_), channel_id=1, source_target_pairs={{8,0},{16,8},{24,16},{32,24},{40,32},{48,40},{56,48},{9,1},{17,9},... | collective-permute-start | bytes 122888 | tf_op jit(solution)/shard_map/ppermute | solution.py:239
  28.1 4.1 %collective-permute-start.2 = (bf16[32,640]{1,0:T(8,128)(2,1)S(1)}, bf16[32,640]{1,0:T(8,128)(2,1)S(1)}, u32[]{:S(2)}, u32[]{:S(2)}) collective-permute-start(bf16[32,640]{1,0:T(8,128)(2,1)S(1)} %shard_map.59.refs_1_), channel_id=1, source_target_pairs={{0,8},{8,16},{16,24},{24,32},{32,40},{40,48},{48,56},{1,9},{9,17},... | collective-permute-start | bytes 122888 | tf_op jit(solution)/shard_map/ppermute | solution.py:239
  33.0 4.8 %collective-permute-start.4 = (f32[864,128]{1,0:T(8,128)S(1)}, f32[864,128]{1,0:T(8,128)S(1)}, u32[]{:S(2)}, u32[]{:S(2)}) collective-permute-start(f32[864,128]{1,0:T(8,128)S(1)} %get-tuple-element.35), channel_id=1, source_target_pairs={{0,8},{8,0},{1,9},{9,1},{2,10},{10,2},{3,11},{11,3},{4,12},{12,4},... | collective-permute-start | bytes 1327112 | tf_op jit(solution)/shard_map/ppermute | solution.py:300
  38.6 12.4 %copy-start = (bf16[27,32,256]{2,1,0:T(8,128)(2,1)S(1)}, bf16[27,32,256]{2,1,0:T(8,128)(2,1)}, u32[]{:S(2)}) copy-start(bf16[27,32,256]{2,1,0:T(8,128)(2,1)} %param.4) | copy-start | bytes 1327108
  38.6 23.5 %all-to-all-start.1 = ((f32[864,1,128]{2,1,0:T(1,128)}), f32[864,1,128]{2,1,0:T(1,128)S(1)}, u32[]{:S(2)}, u32[]{:S(2)}) async-start(f32[864,1,128]{2,1,0:T(1,128)} %bitcast.8), calls=%async_computation.1 | async-start | bytes 884736 | tf_op jit(solution)/shard_map/all_to_all | solution.py:244
  48.4 3.7 %collective-permute-start.5 = (bf16[256,448]{1,0:T(8,128)(2,1)S(1)}, bf16[256,448]{1,0:T(8,128)(2,1)S(1)}, u32[]{:S(2)}, u32[]{:S(2)}) collective-permute-start(bf16[256,448]{1,0:T(8,128)(2,1)S(1)} %get-tuple-element.39.refs_1_), channel_id=1, source_target_pairs={{0,8},{8,0},{1,9},{9,1},{2,10},{10,2},{3,11},{11,3},{4,12},{12,4},... | collective-permute-start | bytes 688136 | tf_op jit(solution)/shard_map/ppermute | solution.py:304
  53.5 4.7 %collective-permute-start.6 = (f32[96,128]{1,0:T(8,128)S(1)}, f32[96,128]{1,0:T(8,128)S(1)}, u32[]{:S(2)}, u32[]{:S(2)}) collective-permute-start(f32[96,128]{1,0:T(8,128)S(1)} %get-tuple-element.43), channel_id=1, source_target_pairs={{0,1},{1,2},{2,3},{3,4},{4,5},{5,6},{6,7},{8,9},{9,10},{10,11},{11... | collective-permute-start | bytes 147464 | tf_op jit(solution)/shard_map/ppermute | solution.py:239
  56.9 5.1 %collective-permute-start.7 = (f32[96,128]{1,0:T(8,128)S(1)}, f32[96,128]{1,0:T(8,128)S(1)}, u32[]{:S(2)}, u32[]{:S(2)}) collective-permute-start(f32[96,128]{1,0:T(8,128)S(1)} %get-tuple-element.44), channel_id=1, source_target_pairs={{1,0},{2,1},{3,2},{4,3},{5,4},{6,5},{7,6},{9,8},{10,9},{11,10},{12... | collective-permute-start | bytes 147464 | tf_op jit(solution)/shard_map/ppermute | solution.py:239
  62.9 21.9 %all-to-all-start.2 = ((f32[864,1,128]{2,1,0:T(1,128)}), f32[864,1,128]{2,1,0:T(1,128)S(1)}, u32[]{:S(2)}, u32[]{:S(2)}) async-start(f32[864,1,128]{2,1,0:T(1,128)} %bitcast.11), calls=%async_computation.2 | async-start | bytes 884736 | tf_op jit(solution)/shard_map/all_to_all | solution.py:244
  72.2 8.6 %collective-permute-start.8 = (f32[64,512]{1,0:T(8,128)S(1)}, f32[64,512]{1,0:T(8,128)S(1)}, u32[]{:S(2)}, u32[]{:S(2)}) collective-permute-start(f32[64,512]{1,0:T(8,128)S(1)} %get-tuple-element.52), channel_id=1, source_target_pairs={{0,8},{8,16},{16,24},{24,32},{32,40},{40,48},{48,56},{1,9},{9,17},... | collective-permute-start | bytes 393224 | tf_op jit(solution)/shard_map/ppermute | solution.py:239
  77.6 7.2 %collective-permute-start.9 = (f32[64,512]{1,0:T(8,128)S(1)}, f32[64,512]{1,0:T(8,128)S(1)}, u32[]{:S(2)}, u32[]{:S(2)}) collective-permute-start(f32[64,512]{1,0:T(8,128)S(1)} %get-tuple-element.53), channel_id=1, source_target_pairs={{8,0},{16,8},{24,16},{32,24},{40,32},{48,40},{56,48},{9,1},{17,9},... | collective-permute-start | bytes 393224 | tf_op jit(solution)/shard_map/ppermute | solution.py:239
  84.7 6.9 %collective-permute-start.10 = (f32[864,128]{1,0:T(8,128)S(1)}, f32[864,128]{1,0:T(8,128)S(1)}, u32[]{:S(2)}, u32[]{:S(2)}) collective-permute-start(f32[864,128]{1,0:T(8,128)S(1)} %bitcast.26), channel_id=1, source_target_pairs={{0,8},{8,0},{1,9},{9,1},{2,10},{10,2},{3,11},{11,3},{4,12},{12,4},... | collective-permute-start | bytes 1327112 | tf_op jit(solution)/shard_map/ppermute | solution.py:342
